TPU v7x, 32 devices: a whole 2x2x4 slice. The times are simulated.
32 devices in a mesh: dp: 16 (over z, y, x), tensor: 2 (over core).
Axes of the slice: x: 2, y: 2, z: 4, core: 2. Of those that a mesh axis runs over, the one named last changes fastest.
Arguments:
- pixels: bfloat16 [32, 3, 240, 240], P('dp'), may hold values from -6 to 6
- patch_size: int32 [32], P('dp'), may hold values from 8 to 48, as said below
- counts: int32 [32], P('dp'), may hold values from 25 to 900, as said below
- offsets: int32 [32], P('dp'), may hold values from 0 to 900, as said below
- resize_table: bfloat16 [49, 48, 32], replicated, may hold values from -0.875 to 0.875
- pos_table: bfloat16 [31, 900, 49], replicated, may hold values from 0 to 0.29882812
- w_base: bfloat16 [768, 3072], replicated, may hold values from -0.109375 to 0.109375
- patch_bias: bfloat16 [768], replicated, may hold values from -1.75 to 1.75
- pos_base: bfloat16 [768, 49], replicated, may hold values from -3 to 3
- gain_one: bfloat16 [768], replicated, may hold values from 0.5 to 1.5
- shift_one: bfloat16 [768], replicated, may hold values from -1.75 to 1.75
- w_query: bfloat16 [768, 768], P(None, 'tensor'), may hold values from -0.21875 to 0.21875
- bias_query: bfloat16 [768], P('tensor'), may hold values from -1.75 to 1.75
- w_key: bfloat16 [768, 768], P(None, 'tensor'), may hold values from -0.21875 to 0.21875
- w_value: bfloat16 [768, 768], P(None, 'tensor'), may hold values from -0.21875 to 0.21875
- bias_value: bfloat16 [768], P('tensor'), may hold values from -1.75 to 1.75
- w_out: bfloat16 [768, 768], P('tensor'), may hold values from -0.875 to 0.875
- bias_out: bfloat16 [768], replicated, may hold values from -1.25 to 1.25
- gain_two: bfloat16 [768], replicated, may hold values from 0.5 to 1.5
- shift_two: bfloat16 [768], replicated, may hold values from -1.75 to 1.75
- w_up: bfloat16 [768, 3072], P(None, 'tensor'), may hold values from -0.21875 to 0.21875
- bias_up: bfloat16 [3072], P('tensor'), may hold values from -1.75 to 1.75
- w_down: bfloat16 [3072, 768], P('tensor'), may hold values from -0.109375 to 0.109375
- bias_down: bfloat16 [768], replicated, may hold values from -1.25 to 1.25
- cotangent: bfloat16 [16384, 768], P('dp'), may hold values from -6 to 6
Outputs:
- out: bfloat16 [16384, 768], P('dp')
- pixel_grad: float32 [32, 3, 240, 240], P('dp')
- grad_w_base: float32 [768, 3072], replicated
- grad_patch_bias: float32 [768], replicated
- grad_pos_base: float32 [768, 49], replicated
- grad_gain_one: float32 [768], replicated
- grad_shift_one: float32 [768], replicated
- grad_w_query: float32 [768, 768], P(None, 'tensor')
- grad_bias_query: float32 [768], P('tensor')
- grad_w_key: float32 [768, 768], P(None, 'tensor')
- grad_w_value: float32 [768, 768], P(None, 'tensor')
- grad_bias_value: float32 [768], P('tensor')
- grad_w_out: float32 [768, 768], P('tensor')
- grad_bias_out: float32 [768], replicated
- grad_gain_two: float32 [768], replicated
- grad_shift_two: float32 [768], replicated
- grad_w_up: float32 [768, 3072], P(None, 'tensor')
- grad_bias_up: float32 [3072], P('tensor')
- grad_w_down: float32 [3072, 768], P('tensor')
- grad_bias_down: float32 [768], replicated
Inputs may be any that keep to these rules, and one draw needn't show every extreme that they name: `patch_size`: every patch size divides 240. Images 4 i to 4 i + 3 lie on two devices; on one of them the first image has patch size 8 and the second 24; every other image has a patch size from 24 to 48. counts is (240 / patch size) squared; the two images of a device hold at most 900 + 10^2 tokens together, and every pair of devices reaches that. `offsets`: A device's first image starts at row 0, its second right after the first.
All inputs are finite; a program needn't handle non-finite values.
Results may differ from a plain program's by a relative error of at most 0.015.
Values sent between devices are 32-bit elements; how exact they have to be, the bound alone decides.
A program may use at most 320 MiB of HBM per device.

v0:
```python
import math

import jax
import jax.numpy as jnp
from jax import lax
from jax.sharding import PartitionSpec as P

HD = 64
BASE = 32
RES = 240
GMAX = 30


def standardize(values):
    centered = values - jnp.mean(values, axis=-1, keepdims=True)
    spread = jnp.mean(centered * centered, axis=-1, keepdims=True)
    return centered * lax.rsqrt(spread + 1e-06)


def token_layout(patch_size, counts, offsets, rows_total):
    row_ids = jnp.arange(rows_total, dtype=jnp.int32)
    inside = (row_ids[:, None] >= offsets[None, :]) & (
        row_ids[:, None] < (offsets + counts)[None, :]
    )
    inside_int = inside.astype(jnp.int32)
    valid_int = jnp.sum(inside_int, axis=1)
    image_slots = jnp.arange(patch_size.shape[0], dtype=jnp.int32)
    image_index = jnp.sum(inside_int * image_slots[None, :], axis=1)
    row_start = jnp.sum(inside_int * offsets[None, :], axis=1)
    grid_sides = jnp.sum(inside_int * (RES // patch_size)[None, :], axis=1) + (1 - valid_int)
    within = (row_ids - row_start) * valid_int
    grid_row = within // grid_sides
    grid_col = within % grid_sides
    table_row = image_index * (GMAX * GMAX) + grid_row * GMAX + grid_col
    pos_row = grid_sides * (GMAX * GMAX) + within
    segment = image_index + (1 - valid_int) * patch_size.shape[0]
    return (table_row, pos_row, segment, valid_int)


def resize_matrix(kernel_table, patch_side):
    row_ids = jnp.arange(RES, dtype=jnp.int32)
    col_ids = jnp.arange(GMAX * BASE, dtype=jnp.int32)
    kernel = jnp.take(kernel_table, patch_side, axis=0)
    picked = jnp.take(kernel, row_ids % patch_side, axis=0)
    tiled_rows = jnp.tile(picked, (1, GMAX))
    same_block = (row_ids // patch_side)[:, None] == (col_ids // BASE)[None, :]
    return jnp.where(same_block, tiled_rows, jnp.zeros_like(tiled_rows))


def flatten_grads(parts):
    flat = jnp.concatenate([member.reshape(-1) for member in parts])
    return flat


def restore_grads(flat, templates):
    restored = []
    position = 0
    for template in templates:
        length = template.size
        restored.append(flat[position : position + length].reshape(template.shape))
        position = position + length
    return tuple(restored)


def masked_scores(block_queries, block_segment, key_rows, segment):
    score_scale = 1.0 / math.sqrt(block_queries.shape[-1])
    scores = (
        jnp.einsum("qhd,khd->hqk", block_queries, key_rows, preferred_element_type=jnp.float32)
        * score_scale
    )
    same_image = block_segment[:, None] == segment[None, :]
    return jnp.where(same_image[None, :, :], scores, -1000000000.0)


def attention_forward(queries, key_rows, value_rows, segment, block_rows):
    row_count, head_count, head_size = queries.shape
    block_count = row_count // block_rows

    def one_block(pieces):
        block_queries, block_segment = pieces
        scores = masked_scores(block_queries, block_segment, key_rows, segment)
        row_max = jnp.max(scores, axis=-1, keepdims=True)
        weights = jnp.exp(scores - row_max)
        row_total = jnp.sum(weights, axis=-1, keepdims=True)
        probs_low = (weights / row_total).astype(jnp.bfloat16)
        output = jnp.einsum(
            "hqk,khd->qhd", probs_low, value_rows, preferred_element_type=jnp.float32
        )
        return (output, (row_max + jnp.log(row_total))[:, :, 0])

    outputs, log_totals = lax.map(
        one_block,
        (
            queries.reshape(block_count, block_rows, head_count, head_size),
            segment.reshape(block_count, block_rows),
        ),
    )
    return (outputs.reshape(row_count, head_count * head_size), log_totals)


def attention_backward(queries, key_rows, value_rows, segment, log_totals, grad_mixed, block_rows):
    row_count, head_count, head_size = queries.shape
    block_count = row_count // block_rows
    score_scale = 1.0 / math.sqrt(head_size)

    def one_block(carried, pieces):
        grad_keys, grad_values = carried
        block_queries, block_segment, block_grad, block_log = pieces
        scores = masked_scores(block_queries, block_segment, key_rows, segment)
        attn_probs = jnp.exp(scores - block_log[:, :, None])
        grad_probs = jnp.einsum(
            "qhd,khd->hqk", block_grad, value_rows, preferred_element_type=jnp.float32
        )
        inner_sum = jnp.sum(attn_probs * grad_probs, axis=-1, keepdims=True)
        grad_scores = (attn_probs * (grad_probs - inner_sum)).astype(jnp.bfloat16)
        grad_queries = (
            jnp.einsum("hqk,khd->qhd", grad_scores, key_rows, preferred_element_type=jnp.float32)
            * score_scale
        )
        grad_keys = (
            grad_keys
            + jnp.einsum(
                "hqk,qhd->khd", grad_scores, block_queries, preferred_element_type=jnp.float32
            )
            * score_scale
        )
        grad_values = grad_values + jnp.einsum(
            "hqk,qhd->khd",
            attn_probs.astype(jnp.bfloat16),
            block_grad,
            preferred_element_type=jnp.float32,
        )
        return ((grad_keys, grad_values), grad_queries)

    zero_rows = jnp.zeros((row_count, head_count, head_size), jnp.float32)
    shaped = (block_count, block_rows, head_count, head_size)
    (grad_keys, grad_values), grad_queries = lax.scan(
        one_block,
        (zero_rows, zero_rows),
        (
            queries.reshape(shaped),
            segment.reshape(block_count, block_rows),
            grad_mixed.reshape(shaped),
            log_totals,
        ),
    )
    return (
        grad_queries.reshape(row_count, head_count * head_size),
        grad_keys.reshape(row_count, head_count * head_size),
        grad_values.reshape(row_count, head_count * head_size),
    )


def local(
    pixels,
    patch_size,
    counts,
    offsets,
    resize_table,
    pos_table,
    w_base,
    patch_bias,
    pos_base,
    gain_one,
    shift_one,
    w_query,
    bias_query,
    w_key,
    w_value,
    bias_value,
    w_out,
    bias_out,
    gain_two,
    shift_two,
    w_up,
    bias_up,
    w_down,
    bias_down,
    cotangent,
):
    rows_total = cotangent.shape[0]
    images = pixels.shape[0]
    block_rows = min(512, rows_total)
    heads_local = w_query.shape[1] // HD
    table_row, pos_row, segment, valid_int = token_layout(patch_size, counts, offsets, rows_total)
    valid_rows = valid_int.astype(jnp.float32)[:, None]
    valid_low = valid_rows.astype(jnp.bfloat16)
    mixers = jax.vmap(resize_matrix, in_axes=(None, 0))(resize_table, patch_size)
    mixer_grid = mixers.reshape(images, RES, GMAX, BASE)
    halves = jnp.einsum(
        "icrs,isg->icrg", pixels, mixers, preferred_element_type=jnp.float32
    ).astype(jnp.bfloat16)
    grid_table = jnp.einsum(
        "irxa,icryb->ixycab",
        mixer_grid,
        halves.reshape(images, 3, RES, GMAX, BASE),
        preferred_element_type=jnp.float32,
    ).astype(jnp.bfloat16)
    grid_table = grid_table.reshape(images * GMAX * GMAX, 3 * BASE * BASE)
    base_tokens = jnp.take(grid_table, table_row, axis=0) * valid_low
    pos_rows = jnp.take(pos_table.reshape(-1, pos_table.shape[2]), pos_row, axis=0) * valid_low
    embedded = (
        jnp.einsum("tf,df->td", base_tokens, w_base, preferred_element_type=jnp.float32)
        + patch_bias.astype(jnp.float32)
        + jnp.einsum("tp,dp->td", pos_rows, pos_base, preferred_element_type=jnp.float32)
    )
    standard_one, standard_back_one = jax.vjp(standardize, embedded)
    normed_one = (
        standard_one * gain_one.astype(jnp.float32) + shift_one.astype(jnp.float32)
    ).astype(jnp.bfloat16)
    queries = (
        jnp.dot(normed_one, w_query, preferred_element_type=jnp.float32)
        + bias_query.astype(jnp.float32)
    ).astype(jnp.bfloat16)
    key_rows = jnp.dot(normed_one, w_key, preferred_element_type=jnp.float32).astype(jnp.bfloat16)
    value_rows = (
        jnp.dot(normed_one, w_value, preferred_element_type=jnp.float32)
        + bias_value.astype(jnp.float32)
    ).astype(jnp.bfloat16)
    shaped = (rows_total, heads_local, HD)
    mixed_wide, log_totals = attention_forward(
        queries.reshape(shaped),
        key_rows.reshape(shaped),
        value_rows.reshape(shaped),
        segment,
        block_rows,
    )
    mixed = mixed_wide.astype(jnp.bfloat16)
    attended = lax.psum(
        jnp.dot(mixed, w_out, preferred_element_type=jnp.float32), "tensor"
    ) + bias_out.astype(jnp.float32)
    middle = embedded + attended
    standard_two, standard_back_two = jax.vjp(standardize, middle)
    normed_two = (
        standard_two * gain_two.astype(jnp.float32) + shift_two.astype(jnp.float32)
    ).astype(jnp.bfloat16)
    hidden = jnp.dot(normed_two, w_up, preferred_element_type=jnp.float32) + bias_up.astype(
        jnp.float32
    )
    activated_wide, gelu_back = jax.vjp(jax.nn.gelu, hidden)
    activated = activated_wide.astype(jnp.bfloat16)
    branch = lax.psum(
        jnp.dot(activated, w_down, preferred_element_type=jnp.float32), "tensor"
    ) + bias_down.astype(jnp.float32)
    output = ((middle + branch) * valid_rows).astype(jnp.bfloat16)
    grad_out = cotangent.astype(jnp.float32) * valid_rows
    grad_branch = grad_out.astype(jnp.bfloat16)
    grad_w_down = jnp.einsum(
        "tf,td->fd", activated, grad_branch, preferred_element_type=jnp.float32
    )
    grad_activated = jnp.einsum(
        "td,fd->tf", grad_branch, w_down, preferred_element_type=jnp.float32
    )
    grad_hidden = gelu_back(grad_activated)[0].astype(jnp.bfloat16)
    grad_w_up = jnp.einsum("td,tf->df", normed_two, grad_hidden, preferred_element_type=jnp.float32)
    grad_bias_up = jnp.sum(grad_hidden, axis=0, dtype=jnp.float32)
    grad_normed_two = lax.psum(
        jnp.einsum("tf,df->td", grad_hidden, w_up, preferred_element_type=jnp.float32), "tensor"
    )
    grad_middle = grad_out + standard_back_two(grad_normed_two * gain_two.astype(jnp.float32))[0]
    grad_attended = grad_middle.astype(jnp.bfloat16)
    grad_w_out = jnp.einsum("te,td->ed", mixed, grad_attended, preferred_element_type=jnp.float32)
    grad_mixed = jnp.einsum(
        "td,ed->te", grad_attended, w_out, preferred_element_type=jnp.float32
    ).astype(jnp.bfloat16)
    grad_q_wide, grad_k_wide, grad_v_wide = attention_backward(
        queries.reshape(shaped),
        key_rows.reshape(shaped),
        value_rows.reshape(shaped),
        segment,
        log_totals,
        grad_mixed.reshape(shaped),
        block_rows,
    )
    grad_queries = grad_q_wide.astype(jnp.bfloat16)
    grad_keys = grad_k_wide.astype(jnp.bfloat16)
    grad_values = grad_v_wide.astype(jnp.bfloat16)
    grad_w_query = jnp.einsum(
        "td,te->de", normed_one, grad_queries, preferred_element_type=jnp.float32
    )
    grad_w_key = jnp.einsum("td,te->de", normed_one, grad_keys, preferred_element_type=jnp.float32)
    grad_w_value = jnp.einsum(
        "td,te->de", normed_one, grad_values, preferred_element_type=jnp.float32
    )
    grad_bias_query = jnp.sum(grad_queries, axis=0, dtype=jnp.float32)
    grad_bias_value = jnp.sum(grad_values, axis=0, dtype=jnp.float32)
    back_terms = (
        jnp.einsum("te,de->td", grad_queries, w_query, preferred_element_type=jnp.float32)
        + jnp.einsum("te,de->td", grad_keys, w_key, preferred_element_type=jnp.float32)
        + jnp.einsum("te,de->td", grad_values, w_value, preferred_element_type=jnp.float32)
    )
    grad_normed_one = lax.psum(back_terms, "tensor")
    grad_embedded = (
        grad_middle + standard_back_one(grad_normed_one * gain_one.astype(jnp.float32))[0]
    )
    grad_embedded_low = grad_embedded.astype(jnp.bfloat16)
    grad_tokens = (
        jnp.einsum("td,df->tf", grad_embedded_low, w_base, preferred_element_type=jnp.float32)
        * valid_rows
    )
    grad_table = (
        jnp.zeros((images * GMAX * GMAX, 3 * BASE * BASE), jnp.float32)
        .at[table_row]
        .add(grad_tokens)
        .astype(jnp.bfloat16)
    )
    grad_half = jnp.einsum(
        "irxa,ixycab->icryb",
        mixer_grid,
        grad_table.reshape(images, GMAX, GMAX, 3, BASE, BASE),
        preferred_element_type=jnp.float32,
    ).astype(jnp.bfloat16)
    pixel_grad = jnp.einsum(
        "icrg,isg->icrs",
        grad_half.reshape(images, 3, RES, GMAX * BASE),
        mixers,
        preferred_element_type=jnp.float32,
    )
    replicas = lax.axis_size("dp")
    grad_w_base = jnp.einsum(
        "td,tf->df", grad_embedded_low, base_tokens, preferred_element_type=jnp.float32
    )
    grad_patch_bias = jnp.sum(grad_embedded_low, axis=0, dtype=jnp.float32)
    grad_pos_base = jnp.einsum(
        "td,tp->dp", grad_embedded_low, pos_rows, preferred_element_type=jnp.float32
    )
    grad_gain_one = jnp.sum(grad_normed_one * standard_one, axis=0)
    grad_shift_one = jnp.sum(grad_normed_one, axis=0)
    grad_bias_out = jnp.sum(grad_attended, axis=0, dtype=jnp.float32)
    grad_gain_two = jnp.sum(grad_normed_two * standard_two, axis=0)
    grad_shift_two = jnp.sum(grad_normed_two, axis=0)
    grad_bias_down = jnp.sum(grad_branch, axis=0, dtype=jnp.float32)
    all_parts = (
        grad_w_base,
        grad_patch_bias,
        grad_pos_base,
        grad_gain_one,
        grad_shift_one,
        grad_w_query,
        grad_bias_query,
        grad_w_key,
        grad_w_value,
        grad_bias_value,
        grad_w_out,
        grad_bias_out,
        grad_gain_two,
        grad_shift_two,
        grad_w_up,
        grad_bias_up,
        grad_w_down,
        grad_bias_down,
    )
    summed = lax.psum_scatter(flatten_grads(all_parts), "dp", scatter_dimension=0, tiled=True)
    gathered = lax.all_gather(summed / replicas, "dp", axis=0, tiled=True)
    results = restore_grads(gathered, all_parts)
    return (
        output,
        pixel_grad,
        results[0],
        results[1],
        results[2],
        results[3],
        results[4],
        results[5],
        results[6],
        results[7],
        results[8],
        results[9],
        results[10],
        results[11],
        results[12],
        results[13],
        results[14],
        results[15],
        results[16],
        results[17],
    )


def solution(mesh):
    in_specs = (
        P("dp", None, None, None),
        P("dp"),
        P("dp"),
        P("dp"),
        P(),
        P(),
        P(),
        P(),
        P(),
        P(),
        P(),
        P(None, "tensor"),
        P("tensor"),
        P(None, "tensor"),
        P(None, "tensor"),
        P("tensor"),
        P("tensor", None),
        P(),
        P(),
        P(),
        P(None, "tensor"),
        P("tensor"),
        P("tensor", None),
        P(),
        P("dp", None),
    )
    out_specs = (
        P("dp", None),
        P("dp", None, None, None),
        P(),
        P(),
        P(),
        P(),
        P(),
        P(None, "tensor"),
        P("tensor"),
        P(None, "tensor"),
        P(None, "tensor"),
        P("tensor"),
        P("tensor", None),
        P(),
        P(),
        P(),
        P(None, "tensor"),
        P("tensor"),
        P("tensor", None),
        P(),
    )
    return jax.shard_map(local, mesh=mesh, in_specs=in_specs, out_specs=out_specs, check_vma=False)
```

profile of v0, /device:TPU:0, one launch (start us, length us, event | category | flops | bytes accessed | tf_op | source)
XLA Modules:
  0.0 1959.4 jit_solution(10637002605517371096)
XLA Ops:
  22.5 17.9 convert_bitcast_fusion
  40.4 54.4 %copy.115 = bf16[2,30,30,3,32,32]{5,4,3,2,1,0:T(8,128)(2,1)} copy(bf16[2,30,30,3,32,32]{4,5,1,2,3,0:T(8,128)(2,1)} %convert_bitcast_fusion) | data formatting | bytes 22118400 | tf_op jit(solution)/shard_map/convert_element_type | solution.py:198
  94.8 55.3 %reshape.711 = bf16[1800,3072]{1,0:T(8,128)(2,1)} reshape(bf16[2,30,30,3,32,32]{5,4,3,2,1,0:T(8,128)(2,1)} %copy.115) | data formatting | bytes 22118400 | tf_op jit(solution)/shard_map/reshape | solution.py:199
  166.0 17.9 gather_fusion.1
  217.5 25.2 %while.27 = (s32[]{:T(128)}, bf16[2,512,6,64]{1,3,2,0:T(8,128)(2,1)}, f32[2,6,512]{2,1,0:T(8,128)S(1)}, s32[2,512]{1,0:T(2,128)S(1)}, s32[1024]{0:T(1024)S(1)}, ...) while((s32[]{:T(128)}, ...), condition=%wide.region_9.10_spmd, body=%wide.region_6.9_spmd.sunk | while | flops 843576320 | bytes 45866112 | solution.py:91
  251.9 22.6 %all-reduce.9.cloned.1.call-done = f32[1024,768]{0,1:T(8,128)} async-done(((f32[1024,768]{0,1:T(8,128)}), f32[1024,768]{0,1:T(8,128)}) %all-reduce.9.cloned.1.call-update) | async-done | bytes 3145744 | tf_op jit(solution)/shard_map/psum | solution.py:229
  305.2 16.2 all-reduce.11.cloned.1.call-done
  341.1 86.0 %while.28 = (s32[]{:T(128)}, f32[1024,6,64]{0,2,1:T(8,128)S(1)}, f32[1024,6,64]{0,2,1:T(8,128)}, bf16[2,512,6,64]{1,3,2,0:T(8,128)(2,1)}, bf16[2,512,6,64]{1,3,2...) while((s32[]{:T(128)}, f32[1024,6,64]{0,2,1:T(8,128)S(1)}, ...), condition=%wide.region_19.20_spmd.clone, body=%wide.region_17.19_spmd.clone.sunk | while | flops 2063135744 | bytes 217685808 | solution.py:137
  352.4 9.7 multiply_convert_fusion.6
  389.1 9.7 multiply_convert_fusion.6
  452.3 9.7 fusion.51
  534.9 10.9 dynamic-update-slice.8
  545.9 10.9 dynamic-update-slice.9
  558.0 10.9 dynamic-update-slice.11
  578.1 40.8 %dynamic-update-slice.17 = f32[5943552]{0:T(1024)} dynamic-update-slice(f32[5943552]{0:T(1024)} %constant_dynamic-update-slice_fusion.1, f32[1179648]{0:T(1024)} %reshape.724, s32[]{} %constant.239) | dynamic-update-slice | bytes 9437188
  622.8 625.7 %all-reduce.15.cloned.1.call-done = f32[5943552]{0:T(1024)} async-done(((f32[5943552]{0:T(1024)}), f32[5943552]{0:T(1024)}) %all-reduce.15.cloned.1.call-update) | async-done | bytes 23774224
  1258.4 12.9 dynamic-update-slice
  1272.7 10.3 fusion.105
  1283.0 29.4 %scatter_custom_fusion = f32[1800,3072]{1,0:T(8,128)} fusion(s32[1024]{0:T(1024)} %bitcast.225, f32[1024,3072]{1,0:T(8,128)} %fusion.105, f32[]{:T(128)} %constant.184.clone.1, f32[1024]{0:T(1024)S(1)} %copy-done.61), kind=kCustom, calls=%fused_computation.53 | custom fusion | flops 6291456 | bytes 34705920 | tf_op jit(solution)/shard_map/scatter-add | solution.py:304
  1312.4 13.5 convert_element_type.206
  1326.0 46.0 %reshape.715 = bf16[2,30,30,3,32,32]{5,4,3,2,1,0:T(8,128)(2,1)} reshape(bf16[1800,3072]{1,0:T(8,128)(2,1)} %convert_element_type.206) | data formatting | bytes 22118400 | tf_op jit(solution)/shard_map/reshape | solution.py:310
  1372.0 20.4 %fusion.47 = bf16[2,3,240,30,32]{2,4,1,3,0:T(8,128)(2,1)} fusion(bf16[2,30,30,3,32,32]{5,4,3,2,1,0:T(8,128)(2,1)} %reshape.715, s32[30,32]{1,0:T(8,128)S(1)} %copy-done.47, s32[2,240]{1,0:T(2,128)S(1)} %copy-done.55, bf16[2,240,32]{1,2,0:T(8,128)(2,1)S(1)} %copy-done.45), kind=kOutput, calls=%fused_computation.92 | convolution fusion | flops 2656512000 | bytes 13860480 | tf_op jit(solution)/shard_map/irxa,ixycab->icryb/dot_general | solution.py:307
  1403.2 494.2 %all-reduce.13.cloned.1.call-done = f32[5943552]{0:T(1024)} async-done(((f32[5943552]{0:T(1024)}), f32[5943552]{0:T(1024)}) %all-reduce.13.cloned.1.call-update) | async-done | bytes 23774224
  1905.8 10.9 reshape.725
  (409 shorter events, 380.6 us)
Async XLA Ops:
  7.2 276.5 %copy-start = (bf16[1536,768]{1,0:T(8,128)(2,1)S(1)}, bf16[1536,768]{1,0:T(8,128)(2,1)}, u32[]{:S(2)}) copy-start(bf16[1536,768]{1,0:T(8,128)(2,1)} %param.51) | copy-start | bytes 7077892
  7.2 267.3 %all-reduce.9.cloned.1.call-start = ((), (), s32[]{:S(2)}) async-start(), calls=%async_computation | async-start | bytes 6291456 | tf_op jit(solution)/shard_map/psum | solution.py:229
  94.8 55.3 %copy-start.100 = (s32[2]{0:T(128)S(1)}, s32[2]{0:T(128)}, u32[]{:S(2)}) copy-start(s32[2]{0:T(128)} %param.32) | copy-start | bytes 28
  94.8 55.3 %copy-start.102 = (s32[2]{0:T(128)S(1)}, s32[2]{0:T(128)}, u32[]{:S(2)}) copy-start(s32[2]{0:T(128)} %param.31) | copy-start | bytes 28
  150.8 49.4 %copy-start.78 = (bf16[1024]{0:T(1024)(128)(2,1)}, bf16[1024]{0:T(1024)(128)(2,1)S(1)}, u32[]{:S(2)}) copy-start(bf16[1024]{0:T(1024)(128)(2,1)S(1)} %get-tuple-element.406) | copy-start | bytes 6148
  151.0 39.9 %copy-start.98 = (pred[1024]{0:T(1024)(128)(4,1)}, pred[1024]{0:T(1024)(128)(4,1)S(1)}, u32[]{:S(2)}) copy-start(pred[1024]{0:T(1024)(128)(4,1)S(1)} %get-tuple-element.401) | copy-start | bytes 3076
  151.0 49.3 %copy-start.83 = (pred[1024]{0:T(1024)(128)(4,1)}, pred[1024]{0:T(1024)(128)(4,1)S(1)}, u32[]{:S(2)}) copy-start(pred[1024]{0:T(1024)(128)(4,1)S(1)} %get-tuple-element.400) | copy-start | bytes 3076
  248.5 73.0 %all-reduce.11.cloned.1.call-start = ((), (), s32[]{:S(2)}) async-start(), calls=%async_computation.1 | async-start | bytes 6291456 | tf_op jit(solution)/shard_map/psum | solution.py:257
  249.1 77.0 %copy-start.62 = (f32[768]{0:T(1024)}, f32[768]{0:T(1024)S(1)}, u32[]{:S(2)}) copy-start(f32[768]{0:T(1024)S(1)} %convert_element_type.187) | copy-start | bytes 9220
  249.1 29.1 %copy-start.86 = (f32[768]{0:T(1024)}, f32[768]{0:T(1024)S(1)}, u32[]{:S(2)}) copy-start(f32[768]{0:T(1024)S(1)} %convert_element_type.188) | copy-start | bytes 9220
  251.9 45.2 %copy-start.80 = (f32[1536]{0:T(1024)}, f32[1536]{0:T(1024)S(1)}, u32[]{:S(2)}) copy-start(f32[1536]{0:T(1024)S(1)} %convert_element_type.190) | copy-start | bytes 18436
  277.8 48.3 %copy-start.56 = (f32[1024]{0:T(1024)}, f32[1024]{0:T(1024)S(1)}, u32[]{:S(2)}) copy-start(f32[1024]{0:T(1024)S(1)} %broadcast_multiply_fusion) | copy-start | bytes 12292
  280.6 45.5 %copy-start.64 = (f32[1024]{0:T(1024)}, f32[1024]{0:T(1024)S(1)}, u32[]{:S(2)}) copy-start(f32[1024]{0:T(1024)S(1)} %fusion.80) | copy-start | bytes 12292
  296.9 195.2 %all-reduce.17.cloned.1.call-start = ((), (), s32[]{:S(2)}) async-start(), calls=%async_computation.4 | async-start | bytes 12582912 | tf_op jit(solution)/shard_map/psum | solution.py:242
  436.6 811.8 %all-reduce.15.cloned.1.call-start = ((), (), s32[]{:S(2)}) async-start(), calls=%async_computation.3 | async-start | bytes 47554560
  533.5 24.5 %copy-start.30 = (f32[294912]{0:T(1024)S(1)}, f32[294912]{0:T(1024)}, u32[]{:S(2)}) copy-start(f32[294912]{0:T(1024)} %reshape.722) | copy-start | bytes 3538948
  534.9 34.0 %copy-start.73 = (f32[768]{0:T(1024)S(1)}, f32[768]{0:T(1024)}, u32[]{:S(2)}) copy-start(f32[768]{0:T(1024)} %get-tuple-element.370) | copy-start | bytes 9220
  534.9 35.3 %copy-start.72 = (f32[768]{0:T(1024)S(1)}, f32[768]{0:T(1024)}, u32[]{:S(2)}) copy-start(f32[768]{0:T(1024)} %get-tuple-element.321) | copy-start | bytes 9220
  534.9 36.6 %copy-start.70 = (f32[768]{0:T(1024)S(1)}, f32[768]{0:T(1024)}, u32[]{:S(2)}) copy-start(f32[768]{0:T(1024)} %get-tuple-element.323) | copy-start | bytes 9220
  578.1 40.8 %copy-start.71 = (f32[768]{0:T(1024)S(1)}, f32[768]{0:T(1024)}, u32[]{:S(2)}) copy-start(f32[768]{0:T(1024)} %get-tuple-element.399) | copy-start | bytes 9220
  620.3 1277.2 %all-reduce.13.cloned.1.call-start = ((), (), s32[]{:S(2)}) async-start(), calls=%async_computation.2 | async-start | bytes 47554560
  1326.0 46.0 %copy-start.45 = (bf16[2,240,32]{1,2,0:T(8,128)(2,1)S(1)}, bf16[2,240,32]{1,2,0:T(8,128)(2,1)}, u32[]{:S(2)}) copy-start(bf16[2,240,32]{1,2,0:T(8,128)(2,1)} %copy-done.44) | copy-start | bytes 92164
  1326.0 46.0 %copy-start.47 = (s32[30,32]{1,0:T(8,128)S(1)}, s32[30,32]{1,0:T(8,128)}, u32[]{:S(2)}) copy-start(s32[30,32]{1,0:T(8,128)} %copy-done.46) | copy-start | bytes 11524
  1326.0 46.0 %copy-start.55 = (s32[2,240]{1,0:T(2,128)S(1)}, s32[2,240]{1,0:T(2,128)}, u32[]{:S(2)}) copy-start(s32[2,240]{1,0:T(2,128)} %copy-done.54) | copy-start | bytes 5764
  (94 other events, 470.5 us)
Sparse Core Ops, SparseCore 0:
  248.6 25.9 all-reduce.8
  297.0 24.3 all-reduce.10
  436.8 33.2 all-reduce.16
  620.4 628.0 all-reduce.14
  1271.5 625.9 all-reduce.12
where the time goes:
time: 1980 us; the launch traced here: 1960 us
  waiting for transfers between devices  1160 us (59%)
  local copies, waits for them, and re-layouts  451 us (23%)
  matrix products  216 us (11%)
  other arithmetic  105 us (5%)
    unnamed x7, waiting for transfers between devices  1120 us
    unnamed x230, local copies, waits for them, and re-layouts  149 us
    reshape x1, local copies, waits for them, and re-layouts, local(): grid_table = grid_table.reshape(images * GMAX * GMAX, 3 * BASE * BASE)  55.3 us
    convert_element_type x1, local copies, waits for them, and re-layouts, local(): grid_table = jnp.einsum('irxa,icryb->ixycab', mixer_grid, halves.reshape(...  54.4 us
    reshape x1, local copies, waits for them, and re-layouts, local(): grad_table.reshape(images, GMAX, GMAX, 3, BASE, BASE)  46 us
  transfers between devices with their start and end apart: 5, of which 4 were waited for; matrix products, arithmetic and copies ran while one was open for 10% of the time, Pallas kernels for 0%

commit v1 on v0

--- a/solution.py
+++ b/solution.py
@@ -1,8 +1,11 @@
+import functools
 import math
 
 import jax
 import jax.numpy as jnp
 from jax import lax
+from jax.experimental import pallas as pl
+from jax.experimental.pallas import tpu as pltpu
 from jax.sharding import PartitionSpec as P
 
 HD = 64
@@ -47,19 +50,398 @@
     return jnp.where(same_block, tiled_rows, jnp.zeros_like(tiled_rows))
 
 
-def flatten_grads(parts):
-    flat = jnp.concatenate([member.reshape(-1) for member in parts])
-    return flat
-
-
-def restore_grads(flat, templates):
-    restored = []
-    position = 0
-    for template in templates:
-        length = template.size
-        restored.append(flat[position : position + length].reshape(template.shape))
-        position = position + length
-    return tuple(restored)
+LINE = 4
+MESH_ID = pl.DeviceIdType.MESH
+
+
+def sync_kernel(pieces, scale, in_count, out_count, *refs):
+    grads = refs[:in_count]
+    outs = refs[in_count : in_count + out_count]
+    acc, land, land_right, land_left, land_last, sems = refs[in_count + out_count :]
+    device = lax.axis_index("dp")
+    core = lax.axis_index("tensor")
+    place_x = lax.rem(device, 2)
+    place_y = lax.rem(device // 2, 2)
+    place_z = lax.rem(device // 4, LINE)
+    beside = {"x": device + 1 - 2 * place_x, "y": device + 2 - 4 * place_y}
+    bits = {"x": place_x, "y": place_y}
+    up = device + 4
+    down = device - 4
+
+    barrier = pltpu.get_barrier_semaphore()
+    for partner in (beside["x"], beside["y"]):
+        pl.semaphore_signal(barrier, inc=1, device_id=(partner, core), device_id_type=MESH_ID)
+    pl.semaphore_signal(barrier, inc=1, device_id=(device, 1 - core), device_id_type=MESH_ID)
+
+    @pl.when(place_z < LINE - 1)
+    def _():
+        pl.semaphore_signal(barrier, inc=1, device_id=(up, core), device_id_type=MESH_ID)
+
+    @pl.when(place_z > 0)
+    def _():
+        pl.semaphore_signal(barrier, inc=1, device_id=(down, core), device_id_type=MESH_ID)
+
+    inner = (place_z + LINE - 1) // LINE + (2 * (LINE - 1) - place_z) // LINE
+    pl.semaphore_wait(barrier, 3 + inner)
+
+    def rows_at(ref, start, size, column, width):
+        return ref.at[pl.ds(pl.multiple_of(start, 8), size), pl.ds(column, width)]
+
+    def remote(src, dst, send, recv, where):
+        return pltpu.make_async_remote_copy(
+            src_ref=src,
+            dst_ref=dst,
+            send_sem=send,
+            recv_sem=recv,
+            device_id=where,
+            device_id_type=MESH_ID,
+        )
+
+    def add_rows(total, start, extra, size, width, factor=None):
+        step = 24 if size % 24 == 0 else 8
+
+        @pl.loop(0, size // step)
+        def _(i):
+            here = pl.ds(pl.multiple_of(start + i * step, 8), step)
+            there = pl.ds(pl.multiple_of(i * step, 8), step)
+            value = total[here, :width] + extra[there, :width]
+            total[here, :width] = value if factor is None else value * factor
+
+    def build(number, piece):
+        source, in_row, in_col, target, out_row, out_col, rows, width, first = piece
+        second = "y" if first == "x" else "x"
+        half, chunk, share = rows // 2, rows // 8, rows // 16
+        grad, out = grads[source], outs[target]
+        own, other = bits[first], bits[second]
+        mine = acc.at[number]
+        sem = lambda k: sems.at[number, k]
+        base_row = out_row + core * rows if piece_swaps(piece) else out_row
+        half_row = base_row + own * half
+
+        def first_copy():
+            return remote(
+                rows_at(grad, in_row + (1 - own) * half, half, in_col, width),
+                land.at[number, :half, :width],
+                sem(0),
+                sem(1),
+                (beside[first], core),
+            )
+
+        def load():
+            return pltpu.make_async_copy(
+                rows_at(grad, in_row + own * half, half, in_col, width),
+                mine.at[:half, :width],
+                sem(2),
+            )
+
+        def right(k):
+            return remote(
+                rows_at(mine, (LINE - k + place_z) * chunk, chunk, 0, width),
+                land_right.at[number, k - 1, :chunk, :width],
+                sem(2 + k),
+                sem(5 + k),
+                (up, core),
+            )
+
+        def left(k):
+            return remote(
+                rows_at(mine, (k - 1 - (LINE - 1 - place_z)) * chunk, chunk, 0, width),
+                land_left.at[number, k - 1, :chunk, :width],
+                sem(8 + k),
+                sem(11 + k),
+                (down, core),
+            )
+
+        def got_right(k):
+            return remote(
+                land_right.at[number, k - 1, :chunk, :width],
+                land_right.at[number, k - 1, :chunk, :width],
+                sem(2 + k),
+                sem(5 + k),
+                (down, core),
+            )
+
+        def got_left(k):
+            return remote(
+                land_left.at[number, k - 1, :chunk, :width],
+                land_left.at[number, k - 1, :chunk, :width],
+                sem(8 + k),
+                sem(11 + k),
+                (up, core),
+            )
+
+        mirror = LINE - 1 - place_z
+
+        def send_line(k):
+            @pl.when((place_z <= k - 1) & (place_z < LINE - 1))
+            def _():
+                right(k).start()
+
+            @pl.when((mirror <= k - 1) & (mirror < LINE - 1))
+            def _():
+                left(k).start()
+
+        def wait_line(k):
+            @pl.when((place_z >= 1) & (place_z <= k))
+            def _():
+                got_right(k).wait_recv()
+                add_rows(
+                    mine, (LINE - 1 - k + place_z) * chunk, land_right.at[number, k - 1], chunk, width
+                )
+
+            @pl.when((mirror >= 1) & (mirror <= k))
+            def _():
+                got_left(k).wait_recv()
+                add_rows(mine, (k - mirror) * chunk, land_left.at[number, k - 1], chunk, width)
+
+        def last_copy():
+            return remote(
+                rows_at(mine, place_z * chunk + (1 - other) * share, share, 0, width),
+                land_last.at[number, :share, :width],
+                sem(15),
+                sem(16),
+                (beside[second], core),
+            )
+
+        share_row = half_row + place_z * chunk + other * share
+
+        def share_out():
+            return remote(
+                rows_at(mine, place_z * chunk + other * share, share, 0, width),
+                rows_at(out, share_row, share, out_col, width),
+                sem(17),
+                sem(18),
+                (beside[second], core),
+            )
+
+        def share_in():
+            return remote(
+                rows_at(mine, place_z * chunk + other * share, share, 0, width),
+                rows_at(out, half_row + place_z * chunk + (1 - other) * share, share, out_col, width),
+                sem(17),
+                sem(18),
+                (beside[second], core),
+            )
+
+        def share_store():
+            return pltpu.make_async_copy(
+                rows_at(mine, place_z * chunk + other * share, share, 0, width),
+                rows_at(out, share_row, share, out_col, width),
+                sem(19),
+            )
+
+        def chunk_out(position):
+            return rows_at(out, half_row + position * chunk, chunk, out_col, width)
+
+        def spread_right(k, position, where):
+            return remote(
+                chunk_out(position), chunk_out(position), sem(19 + k), sem(22 + k), (where, core)
+            )
+
+        def spread_left(k, position, where):
+            return remote(
+                chunk_out(position), chunk_out(position), sem(25 + k), sem(28 + k), (where, core)
+            )
+
+        def send_spread(k):
+            @pl.when((place_z >= k - 1) & (place_z < LINE - 1))
+            def _():
+                spread_right(k, place_z - (k - 1), up).start()
+
+            @pl.when((mirror >= k - 1) & (mirror < LINE - 1))
+            def _():
+                spread_left(k, place_z + (k - 1), down).start()
+
+        def wait_spread(k):
+            @pl.when(place_z >= k)
+            def _():
+                spread_right(k, place_z - k, down).wait_recv()
+
+            @pl.when(mirror >= k)
+            def _():
+                spread_left(k, place_z + k, up).wait_recv()
+
+        def half_out():
+            here = rows_at(out, half_row, half, out_col, width)
+            return remote(here, here, sem(32), sem(33), (beside[first], core))
+
+        def half_in():
+            there = rows_at(out, base_row + (1 - own) * half, half, out_col, width)
+            return remote(there, there, sem(32), sem(33), (beside[first], core))
+
+        def swap_out():
+            here = rows_at(out, base_row, rows, out_col, width)
+            return remote(here, here, sem(34), sem(35), (device, 1 - core))
+
+        def swap_in():
+            there = rows_at(out, out_row + (1 - core) * rows, rows, out_col, width)
+            return remote(there, there, sem(34), sem(35), (device, 1 - core))
+
+        def stage_0():
+            first_copy().start()
+            load().start()
+
+        def stage_1():
+            load().wait()
+            first_copy().wait_recv()
+            add_rows(mine, 0, land.at[number], half, width)
+            send_line(1)
+
+        def stage_2():
+            wait_line(1)
+            send_line(2)
+
+        def stage_3():
+            wait_line(2)
+            send_line(3)
+
+        def stage_4():
+            wait_line(3)
+            last_copy().start()
+
+        def stage_5():
+            last_copy().wait()
+            add_rows(
+                mine, place_z * chunk + other * share, land_last.at[number], share, width, scale
+            )
+            share_out().start()
+            share_store().start()
+
+        def stage_6():
+            share_store().wait()
+            share_in().wait_recv()
+            send_spread(1)
+
+        def stage_7():
+            wait_spread(1)
+            send_spread(2)
+
+        def stage_8():
+            wait_spread(2)
+            send_spread(3)
+
+        def stage_9():
+            wait_spread(3)
+            half_out().start()
+
+        def stage_10():
+            half_in().wait_recv()
+            if piece_swaps(piece):
+                swap_out().start()
+
+        def stage_11():
+            if piece_swaps(piece):
+                swap_in().wait_recv()
+                swap_out().wait_send()
+            first_copy().wait_send()
+            share_out().wait_send()
+            half_out().wait_send()
+            for k in range(1, LINE):
+
+                @pl.when((place_z <= k - 1) & (place_z < LINE - 1))
+                def _():
+                    right(k).wait_send()
+
+                @pl.when((mirror <= k - 1) & (mirror < LINE - 1))
+                def _():
+                    left(k).wait_send()
+
+                @pl.when((place_z >= k - 1) & (place_z < LINE - 1))
+                def _():
+                    spread_right(k, place_z - (k - 1), up).wait_send()
+
+                @pl.when((mirror >= k - 1) & (mirror < LINE - 1))
+                def _():
+                    spread_left(k, place_z + (k - 1), down).wait_send()
+
+        return [
+            stage_0,
+            stage_1,
+            stage_2,
+            stage_3,
+            stage_4,
+            stage_5,
+            stage_6,
+            stage_7,
+            stage_8,
+            stage_9,
+            stage_10,
+            stage_11,
+        ]
+
+    lines = [build(number, piece) for number, piece in enumerate(pieces)]
+    pairs = [lines[i : i + 2] for i in range(0, len(lines), 2)]
+    depth = len(lines[0])
+    ahead = 1
+    for j in range(ahead):
+        for line in pairs[j]:
+            line[0]()
+    for tick in range(len(pairs) + depth - 1):
+        if tick + ahead < len(pairs):
+            for line in pairs[tick + ahead]:
+                line[0]()
+        for j in range(max(0, tick - depth + 1), min(tick, len(pairs))):
+            for line in pairs[j]:
+                line[tick - j]()
+
+
+def piece_swaps(piece):
+    return piece[3] == SWAPPED
+
+
+SWAPPED = 0
+PIECE_ROWS = 384
+PIECE_COLS = 768
+
+
+def sync_plan(in_shapes, out_shapes, out_of):
+    pieces = []
+    for source, shape in enumerate(in_shapes):
+        targets = out_of[source]
+        col_of_source = 0
+        for target in targets:
+            cols = out_shapes[target][1]
+            rows = shape[0]
+            tall = min(PIECE_ROWS, rows)
+            wide = min(PIECE_COLS, cols)
+            for row in range(0, rows, tall):
+                for col in range(0, cols, wide):
+                    pieces.append([source, row, col_of_source + col, target, row, col, tall, wide])
+            col_of_source += cols
+    return [tuple(piece) + ("xy"[i % 2],) for i, piece in enumerate(pieces)]
+
+
+def sync_grads(grads, out_shapes, out_of, replicas):
+    pieces = sync_plan([g.shape for g in grads], out_shapes, out_of)
+    count = len(pieces)
+    high = max(p[6] for p in pieces)
+    wide = max(p[7] for p in pieces)
+    kernel = functools.partial(
+        sync_kernel, pieces, 1.0 / replicas, len(grads), len(out_shapes)
+    )
+    vmem = lambda *dims: pltpu.VMEM(dims, jnp.float32)
+    return pl.pallas_call(
+        kernel,
+        out_shape=[jax.ShapeDtypeStruct(s, jnp.float32) for s in out_shapes],
+        in_specs=[pl.BlockSpec(memory_space=pl.ANY)] * len(grads),
+        out_specs=[pl.BlockSpec(memory_space=pl.ANY)] * len(out_shapes),
+        scratch_shapes=[
+            vmem(count, high // 2, wide),
+            vmem(count, high // 2, wide),
+            vmem(count, LINE - 1, high // 8, wide),
+            vmem(count, LINE - 1, high // 8, wide),
+            vmem(count, high // 16, wide),
+            pltpu.SemaphoreType.DMA((count, 36)),
+        ],
+        compiler_params=pltpu.CompilerParams(
+            collective_id=0, has_side_effects=True, vmem_limit_bytes=56 << 20
+        ),
+        name="sync_grads",
+    )(*grads)
+
+
+def tensor_sum(partial):
+    return partial + lax.ppermute(partial, "tensor", [(0, 1), (1, 0)])
 
 
 def masked_scores(block_queries, block_segment, key_rows, segment):
@@ -226,8 +608,8 @@
         block_rows,
     )
     mixed = mixed_wide.astype(jnp.bfloat16)
-    attended = lax.psum(
-        jnp.dot(mixed, w_out, preferred_element_type=jnp.float32), "tensor"
+    attended = tensor_sum(
+        jnp.dot(mixed, w_out, preferred_element_type=jnp.float32)
     ) + bias_out.astype(jnp.float32)
     middle = embedded + attended
     standard_two, standard_back_two = jax.vjp(standardize, middle)
@@ -239,8 +621,8 @@
     )
     activated_wide, gelu_back = jax.vjp(jax.nn.gelu, hidden)
     activated = activated_wide.astype(jnp.bfloat16)
-    branch = lax.psum(
-        jnp.dot(activated, w_down, preferred_element_type=jnp.float32), "tensor"
+    branch = tensor_sum(
+        jnp.dot(activated, w_down, preferred_element_type=jnp.float32)
     ) + bias_down.astype(jnp.float32)
     output = ((middle + branch) * valid_rows).astype(jnp.bfloat16)
     grad_out = cotangent.astype(jnp.float32) * valid_rows
@@ -254,8 +636,8 @@
     grad_hidden = gelu_back(grad_activated)[0].astype(jnp.bfloat16)
     grad_w_up = jnp.einsum("td,tf->df", normed_two, grad_hidden, preferred_element_type=jnp.float32)
     grad_bias_up = jnp.sum(grad_hidden, axis=0, dtype=jnp.float32)
-    grad_normed_two = lax.psum(
-        jnp.einsum("tf,df->td", grad_hidden, w_up, preferred_element_type=jnp.float32), "tensor"
+    grad_normed_two = tensor_sum(
+        jnp.einsum("tf,df->td", grad_hidden, w_up, preferred_element_type=jnp.float32)
     )
     grad_middle = grad_out + standard_back_two(grad_normed_two * gain_two.astype(jnp.float32))[0]
     grad_attended = grad_middle.astype(jnp.bfloat16)
@@ -275,13 +657,8 @@
     grad_queries = grad_q_wide.astype(jnp.bfloat16)
     grad_keys = grad_k_wide.astype(jnp.bfloat16)
     grad_values = grad_v_wide.astype(jnp.bfloat16)
-    grad_w_query = jnp.einsum(
-        "td,te->de", normed_one, grad_queries, preferred_element_type=jnp.float32
-    )
-    grad_w_key = jnp.einsum("td,te->de", normed_one, grad_keys, preferred_element_type=jnp.float32)
-    grad_w_value = jnp.einsum(
-        "td,te->de", normed_one, grad_values, preferred_element_type=jnp.float32
-    )
+    grad_qkv = jnp.concatenate([grad_queries, grad_keys, grad_values], axis=1)
+    grad_w_qkv = jnp.einsum("td,te->de", normed_one, grad_qkv, preferred_element_type=jnp.float32)
     grad_bias_query = jnp.sum(grad_queries, axis=0, dtype=jnp.float32)
     grad_bias_value = jnp.sum(grad_values, axis=0, dtype=jnp.float32)
     back_terms = (
@@ -289,7 +666,7 @@
         + jnp.einsum("te,de->td", grad_keys, w_key, preferred_element_type=jnp.float32)
         + jnp.einsum("te,de->td", grad_values, w_value, preferred_element_type=jnp.float32)
     )
-    grad_normed_one = lax.psum(back_terms, "tensor")
+    grad_normed_one = tensor_sum(back_terms)
     grad_embedded = (
         grad_middle + standard_back_one(grad_normed_one * gain_one.astype(jnp.float32))[0]
     )
@@ -317,12 +694,17 @@
         preferred_element_type=jnp.float32,
     )
     replicas = lax.axis_size("dp")
+    core = lax.axis_index("tensor")
+    half_width = grad_embedded_low.shape[1] // 2
+    grad_embedded_half = lax.dynamic_slice_in_dim(
+        grad_embedded_low, core * half_width, half_width, axis=1
+    )
     grad_w_base = jnp.einsum(
-        "td,tf->df", grad_embedded_low, base_tokens, preferred_element_type=jnp.float32
+        "td,tf->df", grad_embedded_half, base_tokens, preferred_element_type=jnp.float32
     )
     grad_patch_bias = jnp.sum(grad_embedded_low, axis=0, dtype=jnp.float32)
     grad_pos_base = jnp.einsum(
-        "td,tp->dp", grad_embedded_low, pos_rows, preferred_element_type=jnp.float32
+        "td,tp->pd", grad_embedded_low, pos_rows, preferred_element_type=jnp.float32
     )
     grad_gain_one = jnp.sum(grad_normed_one * standard_one, axis=0)
     grad_shift_one = jnp.sum(grad_normed_one, axis=0)
@@ -330,50 +712,65 @@
     grad_gain_two = jnp.sum(grad_normed_two * standard_two, axis=0)
     grad_shift_two = jnp.sum(grad_normed_two, axis=0)
     grad_bias_down = jnp.sum(grad_branch, axis=0, dtype=jnp.float32)
-    all_parts = (
-        grad_w_base,
-        grad_patch_bias,
+    width = grad_patch_bias.shape[0]
+    small_rows = [
         grad_pos_base,
-        grad_gain_one,
-        grad_shift_one,
-        grad_w_query,
-        grad_bias_query,
-        grad_w_key,
-        grad_w_value,
-        grad_bias_value,
-        grad_w_out,
-        grad_bias_out,
-        grad_gain_two,
-        grad_shift_two,
-        grad_w_up,
-        grad_bias_up,
-        grad_w_down,
-        grad_bias_down,
-    )
-    summed = lax.psum_scatter(flatten_grads(all_parts), "dp", scatter_dimension=0, tiled=True)
-    gathered = lax.all_gather(summed / replicas, "dp", axis=0, tiled=True)
-    results = restore_grads(gathered, all_parts)
+        grad_patch_bias[None],
+        grad_gain_one[None],
+        grad_shift_one[None],
+        grad_bias_out[None],
+        grad_gain_two[None],
+        grad_shift_two[None],
+        grad_bias_down[None],
+        jnp.concatenate([grad_bias_query, grad_bias_value])[None],
+        grad_bias_up.reshape(-1, width),
+    ]
+    small = jnp.concatenate(small_rows, axis=0)
+    used = small.shape[0]
+    small = jnp.pad(small, ((0, -used % 128), (0, 0)))
+    parts = [grad_w_down, grad_w_up, grad_w_qkv, grad_w_base, grad_w_out, small]
+    beyond = replicas // 16
+    step = 1
+    while step < beyond:
+        swap = [(i, (i // 16 ^ step) * 16 + i % 16) for i in range(replicas)]
+        parts = [part + lax.ppermute(part, "dp", swap) for part in parts]
+        step *= 2
+    out_shapes = [
+        (2 * grad_w_base.shape[0], grad_w_base.shape[1]),
+        grad_w_down.shape,
+        grad_w_up.shape,
+        w_query.shape,
+        w_key.shape,
+        w_value.shape,
+        grad_w_out.shape,
+        small.shape,
+    ]
+    synced = sync_grads(parts, out_shapes, [[1], [2], [3, 4, 5], [0], [6], [7]], replicas)
+    base_s, down_s, up_s, query_s, key_s, value_s, out_s, small_s = synced
+    points = pos_rows.shape[1]
+    row = lambda k: small_s[points + k]
+    cut = grad_bias_query.shape[0]
     return (
         output,
         pixel_grad,
-        results[0],
-        results[1],
-        results[2],
-        results[3],
-        results[4],
-        results[5],
-        results[6],
-        results[7],
-        results[8],
-        results[9],
-        results[10],
-        results[11],
-        results[12],
-        results[13],
-        results[14],
-        results[15],
-        results[16],
-        results[17],
+        base_s,
+        row(0),
+        small_s[:points].T,
+        row(1),
+        row(2),
+        query_s,
+        row(7)[:cut],
+        key_s,
+        value_s,
+        row(7)[cut:],
+        out_s,
+        row(3),
+        row(4),
+        row(5),
+        up_s,
+        small_s[points + 8 : used].reshape(-1),
+        down_s,
+        row(6),
     )
 
 

time: 1980 us -> 883 us (0.45)
  waiting for transfers between devices: 1160 us -> 3.52 us
  Pallas kernels: 0 us -> 294 us
  local copies, waits for them, and re-layouts: 451 us -> 263 us
    unnamed x7 -> x0, waiting for transfers between devices: 1120 us -> none
    pallas_call x0 -> x1, Pallas kernels: none -> 294 us  [sync_grads(): pl.pallas_call(kernel, out_shape=[jax.ShapeDtypeStruct(s, jnp.float32) fo...]
    unnamed x230 -> x213, local copies, waits for them, and re-layouts: 149 us -> 36.9 us
    reshape x10 -> x2, local copies, waits for them, and re-layouts: 40.3 us -> 0.62 us  [the longest x1 0.61 us: local(): small_s[points + 8:used].reshape(-1)]
    psum x3 -> x0, waiting for transfers between devices: 38.8 us -> none  [the longest x1 22.6 us: local(): lax.psum(jnp.dot(mixed, w_out, preferred_element_type=jnp.float32), 'tens...]
    slice x12 -> x3, local copies, waits for them, and re-layouts: 37.3 us -> 3.73 us  [the longest x1 1.67 us: local(): row = lambda k: small_s[points + k]]
  transfers between devices with their start and end apart: 5 -> 4, of which waited for: 4 -> 2; matrix products, arithmetic and copies ran while one was open for 10% -> 5% of each run, Pallas kernels for 0% -> 0%
where the time goes in v1:
time: 883 us; the launch traced here: 869 us
  Pallas kernels  294 us (33%)
  local copies, waits for them, and re-layouts  263 us (30%)
  matrix products  200 us (23%)
  other arithmetic  103 us (12%)
    pallas_call x1, Pallas kernels, sync_grads(): pl.pallas_call(kernel, out_shape=[jax.ShapeDtypeStruct(s, jnp.float32) fo...  294 us
    reshape x1, local copies, waits for them, and re-layouts, local(): grid_table = grid_table.reshape(images * GMAX * GMAX, 3 * BASE * BASE)  55.3 us
    convert_element_type x1, local copies, waits for them, and re-layouts, local(): grid_table = jnp.einsum('irxa,icryb->ixycab', mixer_grid, halves.reshape(...  54.5 us
    reshape x1, local copies, waits for them, and re-layouts, local(): grad_table.reshape(images, GMAX, GMAX, 3, BASE, BASE)  45.6 us
    unnamed x213, local copies, waits for them, and re-layouts  36.9 us
    scatter-add x1, other arithmetic, local(): grad_table = jnp.zeros((images * GMAX * GMAX, 3 * BASE * BASE), jnp.float...  29.1 us
    dot_general x1, matrix products, local(): jnp.einsum('irxa,ixycab->icryb', mixer_grid, grad_table.reshape(images, G...  20 us
    convert_element_type x2, other arithmetic, one_block(): grad_scores = (attn_probs * (grad_probs - inner_sum)).astype(jnp.bfloat16)  19.3 us
  transfers between devices with their start and end apart: 4, of which 2 were waited for; matrix products, arithmetic and copies ran while one was open for 5% of the time, Pallas kernels for 0%

profile of v1, /device:TPU:0, one launch (start us, length us, event | category | flops | bytes accessed | tf_op | source)
XLA Modules:
  0.0 868.8 jit_solution(6048845062137385302)
XLA Ops:
  15.9 17.8 %convert_bitcast_fusion = bf16[2,30,30,3,32,32]{4,5,1,2,3,0:T(8,128)(2,1)} fusion(bf16[2,3,240,30,32,1]{2,4,5,3,1,0:T(8,128)(2,1)S(1)} %bitcast.193, s32[30,32]{1,0:T(8,128)S(1)} %add_select_fusion, s32[2,240]{1,0:T(2,128)S(1)} %and_select_fusion.4, bf16[2,240,32]{1,2,0:T(8,128)(2,1)S(1)} %copy.88), kind=kOutput, calls=%fused_computation.52 | convolution fusion | flops 2660659200 | bytes 13860480 | tf_op jit(solution)/shard_map/irxa,icryb->ixycab/dot_general | solution.py:575
  33.7 54.5 %copy.89 = bf16[2,30,30,3,32,32]{5,4,3,2,1,0:T(8,128)(2,1)} copy(bf16[2,30,30,3,32,32]{4,5,1,2,3,0:T(8,128)(2,1)} %convert_bitcast_fusion) | data formatting | bytes 22118400 | tf_op jit(solution)/shard_map/convert_element_type | solution.py:580
  88.2 55.3 %reshape.641 = bf16[1800,3072]{1,0:T(8,128)(2,1)} reshape(bf16[2,30,30,3,32,32]{5,4,3,2,1,0:T(8,128)(2,1)} %copy.89) | data formatting | bytes 22118400 | tf_op jit(solution)/shard_map/reshape | solution.py:581
  145.1 6.7 reshape.642
  151.8 7.6 copy.90
  159.4 18.0 %gather_fusion.1 = bf16[1024,3072]{1,0:T(8,128)(2,1)} fusion(bf16[1800,3072]{1,0:T(8,128)(2,1)} %reshape.641, s32[1024]{0:T(1024)S(1)} %broadcast_clamp_fusion.1), kind=kCustom, calls=%fused_computation.1 | custom fusion | bytes 12587008 | tf_op jit(solution)/shard_map/jit(_take)/gather | solution.py:582
  177.4 6.8 gather_fusion.2
  184.2 9.4 %fusion.98 = f32[1024,768]{0,1:T(8,128)S(1)} fusion(bf16[768,3072]{1,0:T(8,128)(2,1)} %param.35, bf16[1024,3072]{1,0:T(8,128)(2,1)} %gather_fusion.1, pred[1024]{0:T(1024)(128)(4,1)S(1)} %get-tuple-element.373, bf16[1024]{0:T(1024)(128)(2,1)S(1)} %get-tuple-element.377), kind=kOutput, calls=%fused_computation.217 | convolution fusion | flops 4838129664 | bytes 14158848 | tf_op jit(solution)/shard_map/tf,df->td/dot_general | solution.py:585
  210.9 25.2 %while.27 = (s32[]{:T(128)}, bf16[2,512,6,64]{1,3,2,0:T(8,128)(2,1)}, f32[2,6,512]{2,1,0:T(8,128)S(1)}, s32[2,512]{1,0:T(2,128)S(1)}, s32[1024]{0:T(1024)S(1)}, ...) while((s32[]{:T(128)}, ...), condition=%wide.region_9.10_spmd, body=%wide.region_6.9_spmd.sunk | while | flops 843576320 | bytes 45866112 | solution.py:473
  257.3 7.3 convert_reduce_fusion
  299.3 74.7 %while.28 = (s32[]{:T(128)}, f32[1024,6,64]{0,2,1:T(8,128)S(1)}, f32[1024,6,64]{0,2,1:T(8,128)}, bf16[2,512,6,64]{1,3,2,0:T(8,128)(2,1)}, bf16[2,512,6,64]{1,3,2...) while((s32[]{:T(128)}, f32[1024,6,64]{0,2,1:T(8,128)S(1)}, ...), condition=%wide.region_16.17_spmd.clone, body=%wide.region_14.16_spmd.clone.sunk | while | flops 2063135744 | bytes 217685808 | solution.py:519
  302.7 7.9 multiply_reduce_fusion.8
  310.6 9.6 %multiply_convert_fusion.6 = bf16[6,512,1024]{2,1,0:T(8,128)(2,1)} fusion(f32[6,512,1024]{2,1,0:T(8,128)} %get-tuple-element.512, f32[6,512,1024]{2,1,0:T(8,128)S(1)} %fusion.188, f32[6,512]{1,0:T(8,128)S(1)} %get-tuple-element.513, f32[6,512]{1,0:T(8,128)S(1)} %dynamic-slice_bitcast_fusion.2, pred[512,1024]{1,0:T(8,128)(4,1)S(1)} %broadcast_compare_fusion.6), kind=kLoop, calls=%fused_computation.22.clone.1 | loop fusion | flops 18874368 | bytes 32006144 | tf_op jit(solution)/shard_map/while/body/eval_jaxpr/convert_element_type | solution.py:497
  339.3 7.9 multiply_reduce_fusion.8
  347.2 9.6 %multiply_convert_fusion.6 = bf16[6,512,1024]{2,1,0:T(8,128)(2,1)} fusion(f32[6,512,1024]{2,1,0:T(8,128)} %get-tuple-element.512, f32[6,512,1024]{2,1,0:T(8,128)S(1)} %fusion.188, f32[6,512]{1,0:T(8,128)S(1)} %get-tuple-element.513, f32[6,512]{1,0:T(8,128)S(1)} %dynamic-slice_bitcast_fusion.2, pred[512,1024]{1,0:T(8,128)(4,1)S(1)} %broadcast_compare_fusion.6), kind=kLoop, calls=%fused_computation.22.clone.1 | loop fusion | flops 18874368 | bytes 32006144 | tf_op jit(solution)/shard_map/while/body/eval_jaxpr/convert_element_type | solution.py:497
  384.2 7.9 fusion.99.refs_1_
  392.1 9.5 %fusion.57.refs_0_ = f32[1536,768]{1,0:T(8,128)} fusion(bf16[1024,768]{0,1:T(8,128)(2,1)S(1)} %copy-done.14, f32[1024]{0:T(1024)S(1)} %copy-done.53, f32[1024,1536]{1,0:T(8,128)} %copy-done.98, f32[1536]{0:T(1024)S(1)} %copy-done.80), kind=kOutput, calls=%fused_computation.110 | convolution fusion | flops 2434007040 | bytes 12593152 | tf_op jit(solution)/shard_map/tf,td->fd/dot_general | solution.py:630
  427.1 294.0 %sync_grads.1 = (f32[768,3072]{1,0:T(8,128)}, f32[1536,768]{1,0:T(8,128)}, f32[768,1536]{1,0:T(8,128)}, f32[768,384]{1,0:T(8,128)}, f32[768,384]{1,0:T(8,128)}, ...) custom-call(f32[1536,768]{1,0:T(8,128)} %fusion.57.refs_0_, f32[768,1536]{1,0:T(8,128)} %fusion.99.refs_1_, ...), custom_call_target="tpu_custom_call" | custom-call | tf_op jit(solution)/shard_map/sync_grads/pallas_call | solution.py:423
  726.5 10.5 %fusion.110 = f32[1024,3072]{1,0:T(8,128)} fusion(bf16[1024,768]{0,1:T(8,128)(2,1)S(1)} %get-tuple-element.359, bf16[768,3072]{1,0:T(8,128)(2,1)} %param.35), kind=kOutput, calls=%fused_computation.228 | convolution fusion | flops 4831838208 | bytes 18874368 | tf_op jit(solution)/shard_map/td,df->tf/dot_general | solution.py:675
  737.6 29.1 %scatter_custom_fusion = f32[1800,3072]{1,0:T(8,128)} fusion(s32[1024]{0:T(1024)} %bitcast.219, f32[1024,3072]{1,0:T(8,128)} %fusion.110, f32[]{:T(128)} %constant.188.clone.1, f32[1024]{0:T(1024)S(1)} %copy-done.53), kind=kCustom, calls=%fused_computation.53 | custom fusion | flops 6291456 | bytes 34705920 | tf_op jit(solution)/shard_map/scatter-add | solution.py:681
  766.6 12.8 %convert_element_type.208 = bf16[1800,3072]{1,0:T(8,128)(2,1)} convert(f32[1800,3072]{1,0:T(8,128)} %scatter_custom_fusion) | non-fusion elementwise | flops 5529600 | bytes 33177600 | tf_op jit(solution)/shard_map/convert_element_type | solution.py:682
  779.4 45.6 %reshape.645 = bf16[2,30,30,3,32,32]{5,4,3,2,1,0:T(8,128)(2,1)} reshape(bf16[1800,3072]{1,0:T(8,128)(2,1)} %convert_element_type.208) | data formatting | bytes 22118400 | tf_op jit(solution)/shard_map/reshape | solution.py:687
  825.0 20.0 %fusion.47 = bf16[2,3,240,30,32]{2,4,1,3,0:T(8,128)(2,1)} fusion(bf16[2,30,30,3,32,32]{5,4,3,2,1,0:T(8,128)(2,1)} %reshape.645, s32[30,32]{1,0:T(8,128)S(1)} %copy-done.46, s32[2,240]{1,0:T(2,128)S(1)} %copy-done.56, bf16[2,240,32]{1,2,0:T(8,128)(2,1)S(1)} %copy-done.44), kind=kOutput, calls=%fused_computation.91 | convolution fusion | flops 2656512000 | bytes 13860480 | tf_op jit(solution)/shard_map/irxa,ixycab->icryb/dot_general | solution.py:684
  849.8 8.8 %copy.161 = f32[768,3072]{1,0:T(8,128)} copy(f32[768,3072]{1,0:T(8,128)} %get-tuple-element.602) | data formatting | bytes 18874368
  (379 shorter events, 208.9 us)
Async XLA Ops:
  0.7 256.6 %copy-start = (bf16[1536,768]{1,0:T(8,128)(2,1)S(1)}, bf16[1536,768]{1,0:T(8,128)(2,1)}, u32[]{:S(2)}) copy-start(bf16[1536,768]{1,0:T(8,128)(2,1)} %param.51) | copy-start | bytes 7077892
  0.7 14.2 %copy-start.36 = (bf16[2,3,240,240]{3,2,1,0:T(8,128)(2,1)S(1)}, bf16[2,3,240,240]{3,2,1,0:T(8,128)(2,1)}, u32[]{:S(2)}) copy-start(bf16[2,3,240,240]{3,2,1,0:T(8,128)(2,1)} %param.29) | copy-start | bytes 2073604
  4.2 11.7 %copy-start.45 = (s32[30,32]{1,0:T(8,128)}, s32[30,32]{1,0:T(8,128)S(1)}, u32[]{:S(2)}) copy-start(s32[30,32]{1,0:T(8,128)S(1)} %add_select_fusion) | copy-start | bytes 11524
  12.7 20.9 %copy-start.43 = (bf16[2,240,32]{1,2,0:T(8,128)(2,1)}, bf16[2,240,32]{1,2,0:T(8,128)(2,1)S(1)}, u32[]{:S(2)}) copy-start(bf16[2,240,32]{1,2,0:T(8,128)(2,1)S(1)} %copy.88) | copy-start | bytes 92164
  13.6 20.0 %copy-start.55 = (s32[2,240]{1,0:T(2,128)}, s32[2,240]{1,0:T(2,128)S(1)}, u32[]{:S(2)}) copy-start(s32[2,240]{1,0:T(2,128)S(1)} %and_select_fusion.4) | copy-start | bytes 5764
  88.2 55.3 %copy-start.95 = (s32[2]{0:T(128)S(1)}, s32[2]{0:T(128)}, u32[]{:S(2)}) copy-start(s32[2]{0:T(128)} %param.32) | copy-start | bytes 28
  88.2 55.3 %copy-start.97 = (s32[2]{0:T(128)S(1)}, s32[2]{0:T(128)}, u32[]{:S(2)}) copy-start(s32[2]{0:T(128)} %param.31) | copy-start | bytes 28
  144.2 49.4 %copy-start.69 = (bf16[1024]{0:T(1024)(128)(2,1)}, bf16[1024]{0:T(1024)(128)(2,1)S(1)}, u32[]{:S(2)}) copy-start(bf16[1024]{0:T(1024)(128)(2,1)S(1)} %get-tuple-element.377) | copy-start | bytes 6148
  144.3 39.9 %copy-start.93 = (pred[1024]{0:T(1024)(128)(4,1)}, pred[1024]{0:T(1024)(128)(4,1)S(1)}, u32[]{:S(2)}) copy-start(pred[1024]{0:T(1024)(128)(4,1)S(1)} %get-tuple-element.373) | copy-start | bytes 3076
  144.3 49.3 %copy-start.76 = (pred[1024]{0:T(1024)(128)(4,1)}, pred[1024]{0:T(1024)(128)(4,1)S(1)}, u32[]{:S(2)}) copy-start(pred[1024]{0:T(1024)(128)(4,1)S(1)} %get-tuple-element.372) | copy-start | bytes 3076
  241.1 6.1 collective-permute-start
  241.5 39.4 %copy-start.63 = (f32[768]{0:T(1024)}, f32[768]{0:T(1024)S(1)}, u32[]{:S(2)}) copy-start(f32[768]{0:T(1024)S(1)} %convert_element_type.189) | copy-start | bytes 9220
  244.2 25.1 %copy-start.79 = (f32[1536]{0:T(1024)}, f32[1536]{0:T(1024)S(1)}, u32[]{:S(2)}) copy-start(f32[1536]{0:T(1024)S(1)} %convert_element_type.192) | copy-start | bytes 18436
  251.4 29.5 %copy-start.59 = (f32[1024]{0:T(1024)}, f32[1024]{0:T(1024)S(1)}, u32[]{:S(2)}) copy-start(f32[1024]{0:T(1024)S(1)} %broadcast_multiply_fusion) | copy-start | bytes 12292
  254.2 26.7 %copy-start.65 = (f32[1024]{0:T(1024)}, f32[1024]{0:T(1024)S(1)}, u32[]{:S(2)}) copy-start(f32[1024]{0:T(1024)S(1)} %fusion.88) | copy-start | bytes 12292
  257.3 12.0 %copy-start.98 = (f32[1024,1536]{1,0:T(8,128)}, f32[1024,1536]{1,0:T(8,128)S(1)}, u32[]{:S(2)}) copy-start(f32[1024,1536]{1,0:T(8,128)S(1)} %fusion.100) | copy-start | bytes 18874372
  268.9 6.0 collective-permute-start.2
  274.2 6.8 collective-permute-start.1
  383.7 28.6 %collective-permute-start.3 = (f32[1024,768]{0,1:T(8,128)}, f32[1024,768]{0,1:T(8,128)}, u32[]{:S(2)}, u32[]{:S(2)}) collective-permute-start(f32[1024,768]{0,1:T(8,128)} %add_add_fusion.2), channel_id=1, source_target_pairs={{0,1},{1,0},{2,3},{3,2},{4,5},{5,4},{6,7},{7,6},{8,9},{9,8},{10,11... | collective-permute-start | bytes 9437192 | tf_op jit(solution)/shard_map/ppermute | solution.py:444
  779.4 45.6 %copy-start.44 = (bf16[2,240,32]{1,2,0:T(8,128)(2,1)S(1)}, bf16[2,240,32]{1,2,0:T(8,128)(2,1)}, u32[]{:S(2)}) copy-start(bf16[2,240,32]{1,2,0:T(8,128)(2,1)} %copy-done.43) | copy-start | bytes 92164
  779.4 45.6 %copy-start.46 = (s32[30,32]{1,0:T(8,128)S(1)}, s32[30,32]{1,0:T(8,128)}, u32[]{:S(2)}) copy-start(s32[30,32]{1,0:T(8,128)} %copy-done.45) | copy-start | bytes 11524
  779.4 45.6 %copy-start.56 = (s32[2,240]{1,0:T(2,128)S(1)}, s32[2,240]{1,0:T(2,128)}, u32[]{:S(2)}) copy-start(s32[2,240]{1,0:T(2,128)} %copy-done.55) | copy-start | bytes 5764
  849.8 12.8 %slice-start.4 = ((s8[4718592]{0:T(1024)(128)(4,1)}), s8[4194304]{0:T(1024)(128)(4,1)S(1)}, s32[]{:S(2)}) async-start(s8[4718592]{0:T(1024)(128)(4,1)} %bitcast.202), calls=%async_computation.4 | async-start | bytes 8388608
  849.8 12.8 %slice-start.5 = ((s8[4718592]{0:T(1024)(128)(4,1)}), s8[524288]{0:T(1024)(128)(4,1)S(1)}, s32[]{:S(2)}) async-start(s8[4718592]{0:T(1024)(128)(4,1)} %bitcast.202), calls=%async_computation.5 | async-start | bytes 1048576
  (92 other events, 403.4 us)

commit v2 on v1

--- a/solution.py
+++ b/solution.py
@@ -9,9 +9,8 @@
 from jax.sharding import PartitionSpec as P
 
 HD = 64
-BASE = 32
-RES = 240
-GMAX = 30
+VMEM = pl.BlockSpec(memory_space=pltpu.VMEM)
+SMEM = pl.BlockSpec(memory_space=pltpu.SMEM)
 
 
 def standardize(values):
@@ -20,34 +19,314 @@
     return centered * lax.rsqrt(spread + 1e-06)
 
 
-def token_layout(patch_size, counts, offsets, rows_total):
+def row_segments(counts, offsets, rows_total):
     row_ids = jnp.arange(rows_total, dtype=jnp.int32)
     inside = (row_ids[:, None] >= offsets[None, :]) & (
         row_ids[:, None] < (offsets + counts)[None, :]
     )
     inside_int = inside.astype(jnp.int32)
     valid_int = jnp.sum(inside_int, axis=1)
-    image_slots = jnp.arange(patch_size.shape[0], dtype=jnp.int32)
+    image_slots = jnp.arange(counts.shape[0], dtype=jnp.int32)
     image_index = jnp.sum(inside_int * image_slots[None, :], axis=1)
-    row_start = jnp.sum(inside_int * offsets[None, :], axis=1)
-    grid_sides = jnp.sum(inside_int * (RES // patch_size)[None, :], axis=1) + (1 - valid_int)
-    within = (row_ids - row_start) * valid_int
-    grid_row = within // grid_sides
-    grid_col = within % grid_sides
-    table_row = image_index * (GMAX * GMAX) + grid_row * GMAX + grid_col
-    pos_row = grid_sides * (GMAX * GMAX) + within
-    segment = image_index + (1 - valid_int) * patch_size.shape[0]
-    return (table_row, pos_row, segment, valid_int)
-
-
-def resize_matrix(kernel_table, patch_side):
-    row_ids = jnp.arange(RES, dtype=jnp.int32)
-    col_ids = jnp.arange(GMAX * BASE, dtype=jnp.int32)
-    kernel = jnp.take(kernel_table, patch_side, axis=0)
-    picked = jnp.take(kernel, row_ids % patch_side, axis=0)
-    tiled_rows = jnp.tile(picked, (1, GMAX))
-    same_block = (row_ids // patch_side)[:, None] == (col_ids // BASE)[None, :]
-    return jnp.where(same_block, tiled_rows, jnp.zeros_like(tiled_rows))
+    return image_index + (1 - valid_int) * counts.shape[0], valid_int
+
+
+SIDES = (8, 24, 30, 40, 48)
+FINE = 8
+
+
+def spread_tables(table, side, base):
+    entry = lax.broadcasted_iota(jnp.int32, (base, base * base), 0)
+    place = lax.broadcasted_iota(jnp.int32, (base, base * base), 1)
+    repeat = (place // base == entry).astype(jnp.bfloat16)
+    tile = (place % base == entry).astype(jnp.bfloat16)
+    wide = jnp.dot(table, repeat, preferred_element_type=jnp.float32)
+    long = jnp.dot(table, tile, preferred_element_type=jnp.float32)
+    return wide[:side], long[:side]
+
+
+def fill_pairs(pair_ref, table, side, base):
+    wide, long = spread_tables(table, side, base)
+    for s in range(side):
+        pair_ref[s * side : (s + 1) * side, :] = wide * long[s : s + 1]
+
+
+def nt(left, right):
+    return lax.dot_general(left, right, (((1,), (1,)), ((), ())), preferred_element_type=jnp.float32)
+
+
+def tn(left, right):
+    return lax.dot_general(left, right, (((0,), (0,)), ((), ())), preferred_element_type=jnp.float32)
+
+
+def nn(left, right):
+    return jnp.dot(left, right, preferred_element_type=jnp.float32)
+
+
+def embed_kernel(
+    sizes, pix, table, pos, weight, bias, pos_base, emb, tokens, patches, mixed_weight, line, pair, half_emb
+):
+    base = table.shape[2]
+    area = base * base
+    res = pix.shape[2]
+    channels = pix.shape[1]
+
+    @pl.loop(0, 2)
+    def _(slot):
+        for side in SIDES:
+            grid = res // side
+            count = grid * grid
+
+            @pl.when(sizes[slot] == side)
+            def _():
+                fill_pairs(pair, table[slot], side, base)
+                pairs = pair[: side * side, :].astype(jnp.bfloat16)
+                total = nt(pos[slot, :count, :], pos_base[...]) + bias[...]
+                for c in range(channels):
+                    for x in range(grid):
+                        block = pix[slot, c, x * side : (x + 1) * side, :]
+                        line[x * res : (x + 1) * res, :side] = block.T[:res]
+                    patch = jnp.concatenate(
+                        [line[pl.ds(s, count, stride=side), :side] for s in range(side)], axis=1
+                    ).astype(jnp.bfloat16)
+                    columns = slice(c * area, (c + 1) * area)
+                    if side == FINE:
+                        span = slice(c * side * side, (c + 1) * side * side)
+                        mixed = nt(pairs, weight[:, columns]).astype(jnp.bfloat16)
+                        mixed_weight[span, :] = mixed
+                        patches[:count, span] = patch
+                        total += nn(patch, mixed)
+                    else:
+                        token = nn(patch, pairs).astype(jnp.bfloat16)
+                        tokens[slot, :count, columns] = token
+                        total += nt(token, weight[:, columns])
+                half_emb[slot, :count, :] = total
+
+    for side in SIDES:
+        count = (res // side) ** 2
+
+        @pl.when(sizes[0] == side)
+        def _():
+            tail = emb.shape[0] - count
+            emb[:count, :] = half_emb[0, :count, :]
+            emb[count:, :] = jnp.broadcast_to(bias[...], (tail, emb.shape[1]))
+            for second in SIDES[1:]:
+                more = (res // second) ** 2
+
+                @pl.when(sizes[1] == second)
+                def _():
+                    emb[count : count + more, :] = half_emb[1, :more, :]
+
+
+def pixel_kernel(
+    sizes, grad, table, pos, weight, tokens, patches, mixed_weight, core_ref,
+    pixel_grad, grad_weight, grad_pos, line, pair, rows_ref
+):
+    base = table.shape[2]
+    area = base * base
+    res = pixel_grad.shape[2]
+    channels = pixel_grad.shape[1]
+    half = grad_weight.shape[0]
+    mine = pl.multiple_of(core_ref[0] * half, 128)
+    low = jnp.bfloat16
+
+    big = (res // FINE) ** 2
+    rows_ref[0, :big, :] = grad[:big, :]
+    most = (res // SIDES[1]) ** 2
+    for side in SIDES:
+        count = (res // side) ** 2
+
+        @pl.when(sizes[0] == side)
+        def _():
+            rows_ref[1, :most, :] = grad[count : count + most, :]
+
+    grad_weight[...] = jnp.zeros_like(grad_weight)
+    grad_pos[...] = jnp.zeros_like(grad_pos)
+
+    @pl.loop(0, 2)
+    def _(slot):
+        for side in SIDES:
+            grid = res // side
+            count = grid * grid
+
+            @pl.when(sizes[slot] == side)
+            def _():
+                fill_pairs(pair, table[slot], side, base)
+                pairs = pair[: side * side, :].astype(low)
+                rows = rows_ref[slot, :count, :].astype(low)
+                part = rows_ref[slot, :count, pl.ds(mine, half)].astype(low)
+                grad_pos[...] += tn(pos[slot, :count, :], rows)
+                for c in range(channels):
+                    columns = slice(c * area, (c + 1) * area)
+                    if side == FINE:
+                        span = slice(c * side * side, (c + 1) * side * side)
+                        patch = nt(rows, mixed_weight[span, :])
+                        gathered = tn(patches[:count, span], part).astype(low)
+                        grad_weight[:, columns] += tn(gathered, pairs)
+                    else:
+                        token = nn(rows, weight[:, columns]).astype(low)
+                        patch = nt(token, pairs)
+                        grad_weight[:, columns] += tn(part, tokens[slot, :count, columns])
+                    for s in range(side):
+                        line[pl.ds(s, count, stride=side), :side] = patch[
+                            :, s * side : (s + 1) * side
+                        ]
+                    for x in range(grid):
+                        block = line[x * res : (x + 1) * res, :side]
+                        pixel_grad[slot, c, x * side : (x + 1) * side, :] = block.T
+
+def embed(patch_size, pixels, table, pos, w_base, patch_bias, pos_base, rows_total):
+    images, channels, res, _ = pixels.shape
+    width, features = w_base.shape
+    fine = (res // FINE) ** 2
+    small = (res // SIDES[1]) ** 2
+    side = table.shape[1]
+    wide = jnp.pad(pixels.astype(jnp.float32), ((0, 0), (0, 0), (0, 0), (0, -res % 128)))
+    return pl.pallas_call(
+        embed_kernel,
+        out_shape=[
+            jax.ShapeDtypeStruct((rows_total, width), jnp.float32),
+            jax.ShapeDtypeStruct((images, small + 4, features), jnp.bfloat16),
+            jax.ShapeDtypeStruct((fine + 12, channels * FINE * FINE), jnp.bfloat16),
+            jax.ShapeDtypeStruct((channels * FINE * FINE, width), jnp.bfloat16),
+        ],
+        in_specs=[SMEM] + [VMEM] * 6,
+        out_specs=[VMEM] * 4,
+        scratch_shapes=[
+            pltpu.VMEM((res * res // FINE, 128), jnp.float32),
+            pltpu.VMEM((side * side, features // channels), jnp.float32),
+            pltpu.VMEM((images, fine + 4, width), jnp.float32),
+        ],
+        compiler_params=pltpu.CompilerParams(vmem_limit_bytes=60 << 20),
+        name="embed",
+    )(patch_size, wide, table, pos, w_base, patch_bias.astype(jnp.float32)[None], pos_base)
+
+
+def pixel_back(patch_size, grad, table, pos, w_base, tokens, patches, mixed_weight, core, shape):
+    images, channels, res, _ = shape
+    width, features = w_base.shape
+    fine = (res // FINE) ** 2
+    side = table.shape[1]
+    return pl.pallas_call(
+        pixel_kernel,
+        out_shape=[
+            jax.ShapeDtypeStruct(shape, jnp.float32),
+            jax.ShapeDtypeStruct((width // 2, features), jnp.float32),
+            jax.ShapeDtypeStruct((pos.shape[2], width), jnp.float32),
+        ],
+        in_specs=[SMEM] + [VMEM] * 7 + [SMEM],
+        out_specs=[VMEM] * 3,
+        scratch_shapes=[
+            pltpu.VMEM((res * res // FINE, 128), jnp.float32),
+            pltpu.VMEM((side * side, features // channels), jnp.float32),
+            pltpu.VMEM((images, fine + 4, width), jnp.float32),
+        ],
+        compiler_params=pltpu.CompilerParams(vmem_limit_bytes=60 << 20),
+        name="pixel_back",
+    )(patch_size, grad, table, pos, w_base, tokens, patches, mixed_weight, core)
+
+
+PAIR = 2 * HD
+
+
+def pair_halves(rows):
+    lane = lax.broadcasted_iota(jnp.int32, (rows, PAIR), 1)
+    return [lane < HD, lane >= HD]
+
+
+def attend_kernel(scale, query, key, value, segment, segment_row, mixed):
+    rows = query.shape[0]
+    halves = pair_halves(rows)
+    same = segment[...] == segment_row[...]
+    both = []
+    for h in range(2):
+        own = jnp.where(halves[h], query[...], jnp.zeros_like(query))
+        scores = jnp.where(same, nt(own, key[...]) * scale, -1000000000.0)
+        weights = jnp.exp(scores - jnp.max(scores, axis=1, keepdims=True))
+        inverse = 1.0 / jnp.sum(weights, axis=1, keepdims=True)
+        both.append(nn((weights * inverse).astype(jnp.bfloat16), value[...]))
+    mixed[...] = jnp.where(halves[0], both[0], both[1]).astype(jnp.bfloat16)
+
+
+def attend(qkv, segment, block):
+    rows, width = qkv.shape
+    heads = width // 3 // PAIR
+    kernel = functools.partial(attend_kernel, 1.0 / math.sqrt(HD))
+    return pl.pallas_call(
+        kernel,
+        grid=(heads, rows // block),
+        out_shape=jax.ShapeDtypeStruct((rows, width // 3), jnp.bfloat16),
+        in_specs=[
+            pl.BlockSpec((block, PAIR), lambda j, i: (i, j)),
+            pl.BlockSpec((rows, PAIR), lambda j, i: (0, heads + j)),
+            pl.BlockSpec((rows, PAIR), lambda j, i: (0, 2 * heads + j)),
+            pl.BlockSpec((block, 1), lambda j, i: (i, 0)),
+            pl.BlockSpec((1, rows), lambda j, i: (0, 0)),
+        ],
+        out_specs=pl.BlockSpec((block, PAIR), lambda j, i: (i, j)),
+        compiler_params=pltpu.CompilerParams(vmem_limit_bytes=48 << 20),
+        name="attend",
+    )(qkv, qkv, qkv, segment[:, None], segment[None, :])
+
+
+def attend_back_kernel(scale, query, key, value, grad_mixed, segment, segment_row, grad_qkv, grad_key, grad_value):
+    block = query.shape[0]
+    third = grad_qkv.shape[1] // 3
+    pair = pl.program_id(0)
+    step = pl.program_id(1)
+    halves = pair_halves(block)
+    same = segment[...] == segment_row[...]
+
+    @pl.when(step == 0)
+    def _():
+        grad_key[...] = jnp.zeros_like(grad_key)
+        grad_value[...] = jnp.zeros_like(grad_value)
+
+    both = []
+    for h in range(2):
+        own = jnp.where(halves[h], query[...], jnp.zeros_like(query))
+        grad = jnp.where(halves[h], grad_mixed[...], jnp.zeros_like(grad_mixed))
+        scores = jnp.where(same, nt(key[...], own) * scale, -1000000000.0)
+        weights = jnp.exp(scores - jnp.max(scores, axis=0, keepdims=True))
+        probs = weights * (1.0 / jnp.sum(weights, axis=0, keepdims=True))
+        grad_probs = nt(value[...], grad)
+        inner = jnp.sum(probs * grad_probs, axis=0, keepdims=True)
+        grad_scores = (probs * (grad_probs - inner)).astype(jnp.bfloat16)
+        grad_value[...] += nn(probs.astype(jnp.bfloat16), grad)
+        grad_key[...] += nn(grad_scores, own)
+        both.append(tn(grad_scores, key[...]))
+    here = pl.ds(pl.multiple_of(step * block, block), block)
+    column = pl.multiple_of(pair * PAIR, PAIR)
+    grad_query = jnp.where(halves[0], both[0], both[1]) * scale
+    grad_qkv[here, pl.ds(column, PAIR)] = grad_query.astype(jnp.bfloat16)
+
+    @pl.when(step == pl.num_programs(1) - 1)
+    def _():
+        grad_qkv[:, pl.ds(third + column, PAIR)] = (grad_key[...] * scale).astype(jnp.bfloat16)
+        grad_qkv[:, pl.ds(2 * third + column, PAIR)] = grad_value[...].astype(jnp.bfloat16)
+
+
+def attend_back(qkv, grad_mixed, segment, block):
+    rows, width = qkv.shape
+    heads = width // 3 // PAIR
+    kernel = functools.partial(attend_back_kernel, 1.0 / math.sqrt(HD))
+    return pl.pallas_call(
+        kernel,
+        grid=(heads, rows // block),
+        out_shape=jax.ShapeDtypeStruct((rows, width), jnp.bfloat16),
+        in_specs=[
+            pl.BlockSpec((block, PAIR), lambda j, i: (i, j)),
+            pl.BlockSpec((rows, PAIR), lambda j, i: (0, heads + j)),
+            pl.BlockSpec((rows, PAIR), lambda j, i: (0, 2 * heads + j)),
+            pl.BlockSpec((block, PAIR), lambda j, i: (i, j)),
+            pl.BlockSpec((rows, 1), lambda j, i: (0, 0)),
+            pl.BlockSpec((1, block), lambda j, i: (0, i)),
+        ],
+        out_specs=pl.BlockSpec((rows, width), lambda j, i: (0, 0)),
+        scratch_shapes=[pltpu.VMEM((rows, PAIR), jnp.float32), pltpu.VMEM((rows, PAIR), jnp.float32)],
+        compiler_params=pltpu.CompilerParams(vmem_limit_bytes=48 << 20),
+        name="attend_back",
+    )(qkv, qkv, qkv, grad_mixed, segment[:, None], segment[None, :])
 
 
 LINE = 4
@@ -442,95 +721,6 @@
 
 def tensor_sum(partial):
     return partial + lax.ppermute(partial, "tensor", [(0, 1), (1, 0)])
-
-
-def masked_scores(block_queries, block_segment, key_rows, segment):
-    score_scale = 1.0 / math.sqrt(block_queries.shape[-1])
-    scores = (
-        jnp.einsum("qhd,khd->hqk", block_queries, key_rows, preferred_element_type=jnp.float32)
-        * score_scale
-    )
-    same_image = block_segment[:, None] == segment[None, :]
-    return jnp.where(same_image[None, :, :], scores, -1000000000.0)
-
-
-def attention_forward(queries, key_rows, value_rows, segment, block_rows):
-    row_count, head_count, head_size = queries.shape
-    block_count = row_count // block_rows
-
-    def one_block(pieces):
-        block_queries, block_segment = pieces
-        scores = masked_scores(block_queries, block_segment, key_rows, segment)
-        row_max = jnp.max(scores, axis=-1, keepdims=True)
-        weights = jnp.exp(scores - row_max)
-        row_total = jnp.sum(weights, axis=-1, keepdims=True)
-        probs_low = (weights / row_total).astype(jnp.bfloat16)
-        output = jnp.einsum(
-            "hqk,khd->qhd", probs_low, value_rows, preferred_element_type=jnp.float32
-        )
-        return (output, (row_max + jnp.log(row_total))[:, :, 0])
-
-    outputs, log_totals = lax.map(
-        one_block,
-        (
-            queries.reshape(block_count, block_rows, head_count, head_size),
-            segment.reshape(block_count, block_rows),
-        ),
-    )
-    return (outputs.reshape(row_count, head_count * head_size), log_totals)
-
-
-def attention_backward(queries, key_rows, value_rows, segment, log_totals, grad_mixed, block_rows):
-    row_count, head_count, head_size = queries.shape
-    block_count = row_count // block_rows
-    score_scale = 1.0 / math.sqrt(head_size)
-
-    def one_block(carried, pieces):
-        grad_keys, grad_values = carried
-        block_queries, block_segment, block_grad, block_log = pieces
-        scores = masked_scores(block_queries, block_segment, key_rows, segment)
-        attn_probs = jnp.exp(scores - block_log[:, :, None])
-        grad_probs = jnp.einsum(
-            "qhd,khd->hqk", block_grad, value_rows, preferred_element_type=jnp.float32
-        )
-        inner_sum = jnp.sum(attn_probs * grad_probs, axis=-1, keepdims=True)
-        grad_scores = (attn_probs * (grad_probs - inner_sum)).astype(jnp.bfloat16)
-        grad_queries = (
-            jnp.einsum("hqk,khd->qhd", grad_scores, key_rows, preferred_element_type=jnp.float32)
-            * score_scale
-        )
-        grad_keys = (
-            grad_keys
-            + jnp.einsum(
-                "hqk,qhd->khd", grad_scores, block_queries, preferred_element_type=jnp.float32
-            )
-            * score_scale
-        )
-        grad_values = grad_values + jnp.einsum(
-            "hqk,qhd->khd",
-            attn_probs.astype(jnp.bfloat16),
-            block_grad,
-            preferred_element_type=jnp.float32,
-        )
-        return ((grad_keys, grad_values), grad_queries)
-
-    zero_rows = jnp.zeros((row_count, head_count, head_size), jnp.float32)
-    shaped = (block_count, block_rows, head_count, head_size)
-    (grad_keys, grad_values), grad_queries = lax.scan(
-        one_block,
-        (zero_rows, zero_rows),
-        (
-            queries.reshape(shaped),
-            segment.reshape(block_count, block_rows),
-            grad_mixed.reshape(shaped),
-            log_totals,
-        ),
-    )
-    return (
-        grad_queries.reshape(row_count, head_count * head_size),
-        grad_keys.reshape(row_count, head_count * head_size),
-        grad_values.reshape(row_count, head_count * head_size),
-    )
 
 
 def local(
@@ -560,72 +750,39 @@
     bias_down,
     cotangent,
 ):
+    wide = lambda value: value.astype(jnp.float32)
     rows_total = cotangent.shape[0]
-    images = pixels.shape[0]
-    block_rows = min(512, rows_total)
-    heads_local = w_query.shape[1] // HD
-    table_row, pos_row, segment, valid_int = token_layout(patch_size, counts, offsets, rows_total)
-    valid_rows = valid_int.astype(jnp.float32)[:, None]
-    valid_low = valid_rows.astype(jnp.bfloat16)
-    mixers = jax.vmap(resize_matrix, in_axes=(None, 0))(resize_table, patch_size)
-    mixer_grid = mixers.reshape(images, RES, GMAX, BASE)
-    halves = jnp.einsum(
-        "icrs,isg->icrg", pixels, mixers, preferred_element_type=jnp.float32
+    replicas = lax.axis_size("dp")
+    core = lax.axis_index("tensor")
+    segment, valid_int = row_segments(counts, offsets, rows_total)
+    valid_rows = wide(valid_int)[:, None]
+    table = jnp.take(resize_table, patch_size, axis=0)
+    pos = jnp.take(pos_table, pixels.shape[2] // patch_size, axis=0)
+    embedded, tokens, patches, mixed_weight = embed(
+        patch_size, pixels, table, pos, w_base, patch_bias, pos_base, rows_total
+    )
+    w_qkv = jnp.concatenate([w_query, w_key, w_value], axis=1)
+    bias_qkv = jnp.concatenate([bias_query, jnp.zeros_like(bias_query), bias_value])
+    standard_one, standard_back_one = jax.vjp(standardize, embedded)
+    normed_one = (standard_one * wide(gain_one) + wide(shift_one)).astype(jnp.bfloat16)
+    qkv = (
+        jnp.dot(normed_one, w_qkv, preferred_element_type=jnp.float32) + wide(bias_qkv)
     ).astype(jnp.bfloat16)
-    grid_table = jnp.einsum(
-        "irxa,icryb->ixycab",
-        mixer_grid,
-        halves.reshape(images, 3, RES, GMAX, BASE),
-        preferred_element_type=jnp.float32,
-    ).astype(jnp.bfloat16)
-    grid_table = grid_table.reshape(images * GMAX * GMAX, 3 * BASE * BASE)
-    base_tokens = jnp.take(grid_table, table_row, axis=0) * valid_low
-    pos_rows = jnp.take(pos_table.reshape(-1, pos_table.shape[2]), pos_row, axis=0) * valid_low
-    embedded = (
-        jnp.einsum("tf,df->td", base_tokens, w_base, preferred_element_type=jnp.float32)
-        + patch_bias.astype(jnp.float32)
-        + jnp.einsum("tp,dp->td", pos_rows, pos_base, preferred_element_type=jnp.float32)
-    )
-    standard_one, standard_back_one = jax.vjp(standardize, embedded)
-    normed_one = (
-        standard_one * gain_one.astype(jnp.float32) + shift_one.astype(jnp.float32)
-    ).astype(jnp.bfloat16)
-    queries = (
-        jnp.dot(normed_one, w_query, preferred_element_type=jnp.float32)
-        + bias_query.astype(jnp.float32)
-    ).astype(jnp.bfloat16)
-    key_rows = jnp.dot(normed_one, w_key, preferred_element_type=jnp.float32).astype(jnp.bfloat16)
-    value_rows = (
-        jnp.dot(normed_one, w_value, preferred_element_type=jnp.float32)
-        + bias_value.astype(jnp.float32)
-    ).astype(jnp.bfloat16)
-    shaped = (rows_total, heads_local, HD)
-    mixed_wide, log_totals = attention_forward(
-        queries.reshape(shaped),
-        key_rows.reshape(shaped),
-        value_rows.reshape(shaped),
-        segment,
-        block_rows,
-    )
-    mixed = mixed_wide.astype(jnp.bfloat16)
-    attended = tensor_sum(
-        jnp.dot(mixed, w_out, preferred_element_type=jnp.float32)
-    ) + bias_out.astype(jnp.float32)
+    mixed = attend(qkv, segment, rows_total)
+    attended = tensor_sum(jnp.dot(mixed, w_out, preferred_element_type=jnp.float32)) + wide(
+        bias_out
+    )
     middle = embedded + attended
     standard_two, standard_back_two = jax.vjp(standardize, middle)
-    normed_two = (
-        standard_two * gain_two.astype(jnp.float32) + shift_two.astype(jnp.float32)
-    ).astype(jnp.bfloat16)
-    hidden = jnp.dot(normed_two, w_up, preferred_element_type=jnp.float32) + bias_up.astype(
-        jnp.float32
-    )
+    normed_two = (standard_two * wide(gain_two) + wide(shift_two)).astype(jnp.bfloat16)
+    hidden = jnp.dot(normed_two, w_up, preferred_element_type=jnp.float32) + wide(bias_up)
     activated_wide, gelu_back = jax.vjp(jax.nn.gelu, hidden)
     activated = activated_wide.astype(jnp.bfloat16)
-    branch = tensor_sum(
-        jnp.dot(activated, w_down, preferred_element_type=jnp.float32)
-    ) + bias_down.astype(jnp.float32)
+    branch = tensor_sum(jnp.dot(activated, w_down, preferred_element_type=jnp.float32)) + wide(
+        bias_down
+    )
     output = ((middle + branch) * valid_rows).astype(jnp.bfloat16)
-    grad_out = cotangent.astype(jnp.float32) * valid_rows
+    grad_out = wide(cotangent) * valid_rows
     grad_branch = grad_out.astype(jnp.bfloat16)
     grad_w_down = jnp.einsum(
         "tf,td->fd", activated, grad_branch, preferred_element_type=jnp.float32
@@ -639,73 +796,35 @@
     grad_normed_two = tensor_sum(
         jnp.einsum("tf,df->td", grad_hidden, w_up, preferred_element_type=jnp.float32)
     )
-    grad_middle = grad_out + standard_back_two(grad_normed_two * gain_two.astype(jnp.float32))[0]
+    grad_middle = grad_out + standard_back_two(grad_normed_two * wide(gain_two))[0]
     grad_attended = grad_middle.astype(jnp.bfloat16)
     grad_w_out = jnp.einsum("te,td->ed", mixed, grad_attended, preferred_element_type=jnp.float32)
     grad_mixed = jnp.einsum(
         "td,ed->te", grad_attended, w_out, preferred_element_type=jnp.float32
     ).astype(jnp.bfloat16)
-    grad_q_wide, grad_k_wide, grad_v_wide = attention_backward(
-        queries.reshape(shaped),
-        key_rows.reshape(shaped),
-        value_rows.reshape(shaped),
-        segment,
-        log_totals,
-        grad_mixed.reshape(shaped),
-        block_rows,
-    )
-    grad_queries = grad_q_wide.astype(jnp.bfloat16)
-    grad_keys = grad_k_wide.astype(jnp.bfloat16)
-    grad_values = grad_v_wide.astype(jnp.bfloat16)
-    grad_qkv = jnp.concatenate([grad_queries, grad_keys, grad_values], axis=1)
+    grad_qkv = attend_back(qkv, grad_mixed, segment, rows_total)
     grad_w_qkv = jnp.einsum("td,te->de", normed_one, grad_qkv, preferred_element_type=jnp.float32)
-    grad_bias_query = jnp.sum(grad_queries, axis=0, dtype=jnp.float32)
-    grad_bias_value = jnp.sum(grad_values, axis=0, dtype=jnp.float32)
-    back_terms = (
-        jnp.einsum("te,de->td", grad_queries, w_query, preferred_element_type=jnp.float32)
-        + jnp.einsum("te,de->td", grad_keys, w_key, preferred_element_type=jnp.float32)
-        + jnp.einsum("te,de->td", grad_values, w_value, preferred_element_type=jnp.float32)
-    )
-    grad_normed_one = tensor_sum(back_terms)
-    grad_embedded = (
-        grad_middle + standard_back_one(grad_normed_one * gain_one.astype(jnp.float32))[0]
-    )
+    grad_bias_qkv = jnp.sum(grad_qkv, axis=0, dtype=jnp.float32)
+    cut = bias_query.shape[0]
+    grad_bias_query, grad_bias_value = grad_bias_qkv[:cut], grad_bias_qkv[2 * cut :]
+    grad_normed_one = tensor_sum(
+        jnp.einsum("te,de->td", grad_qkv, w_qkv, preferred_element_type=jnp.float32)
+    )
+    grad_embedded = grad_middle + standard_back_one(grad_normed_one * wide(gain_one))[0]
     grad_embedded_low = grad_embedded.astype(jnp.bfloat16)
-    grad_tokens = (
-        jnp.einsum("td,df->tf", grad_embedded_low, w_base, preferred_element_type=jnp.float32)
-        * valid_rows
-    )
-    grad_table = (
-        jnp.zeros((images * GMAX * GMAX, 3 * BASE * BASE), jnp.float32)
-        .at[table_row]
-        .add(grad_tokens)
-        .astype(jnp.bfloat16)
-    )
-    grad_half = jnp.einsum(
-        "irxa,ixycab->icryb",
-        mixer_grid,
-        grad_table.reshape(images, GMAX, GMAX, 3, BASE, BASE),
-        preferred_element_type=jnp.float32,
-    ).astype(jnp.bfloat16)
-    pixel_grad = jnp.einsum(
-        "icrg,isg->icrs",
-        grad_half.reshape(images, 3, RES, GMAX * BASE),
-        mixers,
-        preferred_element_type=jnp.float32,
-    )
-    replicas = lax.axis_size("dp")
-    core = lax.axis_index("tensor")
-    half_width = grad_embedded_low.shape[1] // 2
-    grad_embedded_half = lax.dynamic_slice_in_dim(
-        grad_embedded_low, core * half_width, half_width, axis=1
-    )
-    grad_w_base = jnp.einsum(
-        "td,tf->df", grad_embedded_half, base_tokens, preferred_element_type=jnp.float32
+    pixel_grad, grad_w_base, grad_pos_base = pixel_back(
+        patch_size,
+        grad_embedded,
+        table,
+        pos,
+        w_base,
+        tokens,
+        patches,
+        mixed_weight,
+        core[None],
+        pixels.shape,
     )
     grad_patch_bias = jnp.sum(grad_embedded_low, axis=0, dtype=jnp.float32)
-    grad_pos_base = jnp.einsum(
-        "td,tp->pd", grad_embedded_low, pos_rows, preferred_element_type=jnp.float32
-    )
     grad_gain_one = jnp.sum(grad_normed_one * standard_one, axis=0)
     grad_shift_one = jnp.sum(grad_normed_one, axis=0)
     grad_bias_out = jnp.sum(grad_attended, axis=0, dtype=jnp.float32)
@@ -747,9 +866,8 @@
     ]
     synced = sync_grads(parts, out_shapes, [[1], [2], [3, 4, 5], [0], [6], [7]], replicas)
     base_s, down_s, up_s, query_s, key_s, value_s, out_s, small_s = synced
-    points = pos_rows.shape[1]
+    points = pos.shape[2]
     row = lambda k: small_s[points + k]
-    cut = grad_bias_query.shape[0]
     return (
         output,
         pixel_grad,

time: 883 us -> 508 us (0.58); the launches traced: 869 us -> 504 us
  local copies, waits for them, and re-layouts: 263 us -> 41.7 us
  matrix products: 200 us -> 44.4 us
  Pallas kernels: 294 us -> 377 us
  other arithmetic: 103 us -> 27.5 us
    dot_general x29 -> x2, matrix products: 151 us -> 7.88 us  [the longest x1 3.94 us: local(): jnp.dot(normed_one, w_qkv, preferred_element_type=jnp.float32)]
    reshape x4 -> x0, local copies, waits for them, and re-layouts: 115 us -> none  [the longest x1 55.3 us: local(): grid_table = grid_table.reshape(images * GMAX * GMAX, 3 * BASE * BASE)]
    pallas_call x0 -> x4, Pallas kernels: none -> 83.8 us  [the longest x1 26.6 us: embed(): pl.pallas_call(embed_kernel, out_shape=[jax.ShapeDtypeStruct((rows_total,...]
    convert_element_type x6 -> x0, local copies, waits for them, and re-layouts: 64.7 us -> none  [the longest x1 54.5 us: local(): grid_table = jnp.einsum('irxa,icryb->ixycab', mixer_grid, halves.reshape(...]
    convert_element_type x16 -> x9, other arithmetic: 33.3 us -> 1.4 us  [local(): wide = lambda value: value.astype(jnp.float32)]
    scatter-add x1 -> x0, other arithmetic: 29.1 us -> none  [local(): grad_table = jnp.zeros((images * GMAX * GMAX, 3 * BASE * BASE), jnp.float...]
    gather x5 -> x4, local copies, waits for them, and re-layouts: 30.4 us -> 3.06 us  [the longest x2 2.4 us: local(): pos = jnp.take(pos_table, pixels.shape[2] // patch_size, axis=0)]
    reduce_sum x6 -> x2, other arithmetic: 12.9 us -> 1.14 us  [the longest x1 0.75 us: row_segments(): valid_int = jnp.sum(inside_int, axis=1)]
  transfers between devices with their start and end apart: 4 -> 4, of which waited for: 2 -> 3; matrix products, arithmetic and copies ran while one was open for 5% -> 5% of each run, Pallas kernels for 0% -> 0%
where the time goes in v2:
time: 508 us; the launch traced here: 504 us
  Pallas kernels  377 us (74%)
  matrix products  44.4 us (9%)
  local copies, waits for them, and re-layouts  41.7 us (8%)
  other arithmetic  27.5 us (5%)
  waiting for transfers between devices  10.5 us (2%)
    pallas_call x1, Pallas kernels, sync_grads(): pl.pallas_call(kernel, out_shape=[jax.ShapeDtypeStruct(s, jnp.float32) fo...  293 us
    unnamed x89, local copies, waits for them, and re-layouts  28.4 us
    pallas_call x1, Pallas kernels, embed(): pl.pallas_call(embed_kernel, out_shape=[jax.ShapeDtypeStruct((rows_total,...  26.6 us
    pallas_call x1, Pallas kernels, attend_back(): pl.pallas_call(kernel, grid=(heads, rows // block), out_shape=jax.ShapeDt...  24.5 us
    pallas_call x1, Pallas kernels, pixel_back(): pl.pallas_call(pixel_kernel, out_shape=[jax.ShapeDtypeStruct(shape, jnp.f...  17.9 us
    pallas_call x1, Pallas kernels, attend(): pl.pallas_call(kernel, grid=(heads, rows // block), out_shape=jax.ShapeDt...  14.8 us
    ppermute x4, waiting for transfers between devices, tensor_sum(): return partial + lax.ppermute(partial, 'tensor', [(0, 1), (1, 0)])  10.5 us
  transfers between devices with their start and end apart: 4, of which 3 were waited for; matrix products, arithmetic and copies ran while one was open for 5% of the time, Pallas kernels for 0%

profile of v2, /device:TPU:0, one launch (start us, length us, event | category | flops | bytes accessed | tf_op | source)
XLA Modules:
  0.0 504.4 jit_solution(18192486772141557907)
XLA Ops:
  13.4 2.5 pad_convert_fusion.pix
  18.4 26.6 %embed.1 = (f32[1024,768]{1,0:T(8,128)}, bf16[2,104,3072]{2,1,0:T(8,128)(2,1)}, bf16[912,192]{1,0:T(8,128)(2,1)}, bf16[192,768]{1,0:T(8,128)(2,1)}) custom-call(s32[2]{0:T(128)} %sizes.3, f32[2,3,240,256]{3,2,1,0:T(8,128)} %pad_convert_fusion.pix, bf16[2,48,32]{2,1,0:T(8,128)(2,1)} %broadcast_select_fusion.1.table, ...), custom_call_target="tpu_custom_call" | custom-call | tf_op jit(solution)/shard_map/embed/pallas_call | solution.py:185
  47.3 2.5 multiply_reduce_fusion.5
  51.6 3.9 add_convert_fusion.query.key.value
  55.6 14.8 %attend.1 = bf16[1024,384]{1,0:T(8,128)(2,1)S(1)} custom-call(bf16[1024,1152]{1,0:T(8,128)(2,1)S(1)} %add_convert_fusion.query.key.value, bf16[1024,1152]{1,0:T(8,128)(2,1)S(1)} %add_convert_fusion.query.key.value, bf16[1024,1152]{1,0:T(8,128)(2,1)S(1)} %add_convert_fusion.query.key.value, s32[1024,1]{1,0:T(8,128)S(1)} %copy.60.segment, s32[1,1024]{1,0:T(1,128)S(1)} %bitcast.24), custom_call_target="tpu_custom_call" | custom-call | tf_op jit(solution)/shard_map/attend/pallas_call | solution.py:255
  72.0 5.2 %collective-permute-done = f32[1024,768]{1,0:T(8,128)S(1)} collective-permute-done((f32[1024,768]{1,0:T(8,128)S(1)}, f32[1024,768]{1,0:T(8,128)S(1)}, u32[]{:S(2)}, u32[]{:S(2)}) %collective-permute-start) | collective-permute-done | bytes 3145760 | tf_op jit(solution)/shard_map/ppermute | solution.py:723
  78.3 2.2 copy-done.30
  80.6 3.9 multiply_convert_fusion
  84.6 7.0 %convert_reduce_fusion = (f32[1536]{0:T(1024)S(1)}, bf16[1024,1536]{1,0:T(8,128)(2,1)S(1)}) fusion(f32[1024,1536]{1,0:T(8,128)S(1)} %get-tuple-element.89, f32[1536]{0:T(1024)S(1)} %convert_element_type.104, bf16[1536,768]{1,0:T(8,128)(2,1)S(1)} %copy-done.31, bf16[1024,768]{1,0:T(8,128)(2,1)S(1)} %copy-done.12, f32[1024]{0:T(1024)S(1)} %get-tuple-element.85), kind=kOutput, calls=%fused_computation.11 | convolution fusion | flops 2454452736 | bytes 13385728 | tf_op jit(solution)/shard_map/td,fd->tf/dot_general | solution.py:790
  91.6 2.6 fusion.28
  94.6 2.6 fusion.27
  97.5 2.5 collective-permute-done.2
  101.7 2.8 collective-permute-done.1
  104.4 2.8 fusion.22
  110.3 24.5 %attend_back.1 = bf16[1024,1152]{1,0:T(8,128)(2,1)S(1)} custom-call(bf16[1024,1152]{1,0:T(8,128)(2,1)S(1)} %add_convert_fusion.query.key.value, bf16[1024,1152]{1,0:T(8,128)(2,1)S(1)} %add_convert_fusion.query.key.value, bf16[1024,1152]{1,0:T(8,128)(2,1)S(1)} %add_convert_fusion.query.key.value, bf16[1024,384]{1,0:T(8,128)(2,1)S(1)} %convolution_convert_fusion.grad_mixed, ...), custom_call_target="tpu_custom_call" | custom-call | tf_op jit(solution)/shard_map/attend_back/pallas_call | solution.py:313
  134.8 3.9 fusion.29
  139.1 7.4 %fusion.11.refs_0_ = f32[1536,768]{1,0:T(8,128)} fusion(bf16[1024,1536]{1,0:T(8,128)(2,1)} %copy-done.34, bf16[1024,768]{1,0:T(8,128)(2,1)} %param.49, f32[1024]{0:T(1024)S(1)} %get-tuple-element.85), kind=kOutput, calls=%fused_computation.75 | convolution fusion | flops 2418278400 | bytes 9441280 | tf_op jit(solution)/shard_map/tf,td->fd/dot_general | solution.py:787
  146.5 4.8 fusion.18.refs_1_
  153.7 4.4 fusion.17.refs_2_
  158.0 3.7 multiply_reduce_fusion.1
  166.3 17.9 %pixel_back.1 = (f32[2,3,240,240]{3,2,1,0:T(8,128)}, f32[384,3072]{1,0:T(8,128)}, f32[49,768]{1,0:T(8,128)}) custom-call(s32[2]{0:T(128)} %sizes.3, f32[1024,768]{1,0:T(8,128)} %get-tuple-element.70.grad, bf16[2,48,32]{2,1,0:T(8,128)(2,1)} %broadcast_select_fusion.1.table, bf16[2,900,49]{2,1,0:T(8,128)(2,1)} %broadcast_select_fusion.pos, ...), custom_call_target="tpu_custom_call" | custom-call | tf_op jit(solution)/shard_map/pixel_back/pallas_call | solution.py:210
  186.0 293.4 %sync_grads.1 = (f32[768,3072]{1,0:T(8,128)}, f32[1536,768]{1,0:T(8,128)}, f32[768,1536]{1,0:T(8,128)}, f32[768,384]{1,0:T(8,128)}, f32[768,384]{1,0:T(8,128)}, ...) custom-call(f32[1536,768]{1,0:T(8,128)} %fusion.11.refs_0_, f32[768,1536]{1,0:T(8,128)} %fusion.18.refs_1_, ...), custom_call_target="tpu_custom_call" | custom-call | tf_op jit(solution)/shard_map/sync_grads/pallas_call | solution.py:702
  485.4 8.8 %copy.74 = f32[768,3072]{1,0:T(8,128)} copy(f32[768,3072]{1,0:T(8,128)} %get-tuple-element.116) | data formatting | bytes 18874368
  498.3 2.4 copy.79
  (154 shorter events, 49.6 us)
Async XLA Ops:
  0.7 7.6 %copy-start = (bf16[31,900,49]{1,0,2:T(8,128)(2,1)S(1)}, bf16[31,900,49]{1,0,2:T(8,128)(2,1)}, u32[]{:S(2)}) copy-start(bf16[31,900,49]{1,0,2:T(8,128)(2,1)} %param.30) | copy-start | bytes 8202604
  10.3 5.7 %copy-start.19 = (bf16[768,384]{1,0:T(8,128)(2,1)S(1)}, bf16[768,384]{1,0:T(8,128)(2,1)}, u32[]{:S(2)}) copy-start(bf16[768,384]{1,0:T(8,128)(2,1)} %param.36) | copy-start | bytes 1769476
  13.4 42.1 %copy-start.2 = (s32[1024,1]{1,0:T(8,128)}, s32[1024,1]{1,0:T(8,128)S(1)}, u32[]{:S(2)}) copy-start(s32[1024,1]{1,0:T(8,128)S(1)} %copy.60.segment) | copy-start | bytes 12292
  45.0 4.8 copy-start.20
  45.0 5.7 %copy-start.21 = (bf16[768,384]{1,0:T(8,128)(2,1)S(1)}, bf16[768,384]{1,0:T(8,128)(2,1)}, u32[]{:S(2)}) copy-start(bf16[768,384]{1,0:T(8,128)(2,1)} %param.39) | copy-start | bytes 1769476
  47.2 4.3 copy-start.28
  47.2 4.3 copy-start.4
  55.6 14.8 %copy-start.18 = (bf16[384,768]{1,0:T(8,128)(2,1)S(1)}, bf16[384,768]{1,0:T(8,128)(2,1)}, u32[]{:S(2)}) copy-start(bf16[384,768]{1,0:T(8,128)(2,1)} %param.41) | copy-start | bytes 1769476
  71.4 5.8 %collective-permute-start = (f32[1024,768]{1,0:T(8,128)S(1)}, f32[1024,768]{1,0:T(8,128)S(1)}, u32[]{:S(2)}, u32[]{:S(2)}) collective-permute-start(f32[1024,768]{1,0:T(8,128)S(1)} %fusion.26), channel_id=1, source_target_pairs={{0,1},{1,0},{2,3},{3,2},{4,5},{5,4},{6,7},{7,6},{8,9},{9,8},{10,11... | collective-permute-start | bytes 9437192 | tf_op jit(solution)/shard_map/ppermute | solution.py:723
  77.8 26.7 %copy-start.6 = (f32[1024,768]{1,0:T(8,128)}, f32[1024,768]{1,0:T(8,128)S(1)}, u32[]{:S(2)}) copy-start(f32[1024,768]{1,0:T(8,128)S(1)} %get-tuple-element.78) | copy-start | bytes 9437188
  84.5 10.1 %copy-start.34 = (bf16[1024,1536]{1,0:T(8,128)(2,1)}, bf16[1024,1536]{1,0:T(8,128)(2,1)S(1)}, u32[]{:S(2)}) copy-start(bf16[1024,1536]{1,0:T(8,128)(2,1)S(1)} %get-tuple-element.88) | copy-start | bytes 9437188
  94.2 5.7 %collective-permute-start.2 = (f32[1024,768]{1,0:T(8,128)S(1)}, f32[1024,768]{1,0:T(8,128)S(1)}, u32[]{:S(2)}, u32[]{:S(2)}) collective-permute-start(f32[1024,768]{1,0:T(8,128)S(1)} %fusion.28), channel_id=1, source_target_pairs={{0,1},{1,0},{2,3},{3,2},{4,5},{5,4},{6,7},{7,6},{8,9},{9,8},{10,11... | collective-permute-start | bytes 9437192 | tf_op jit(solution)/shard_map/ppermute | solution.py:723
  97.2 7.2 %collective-permute-start.1 = (f32[1024,768]{1,0:T(8,128)S(1)}, f32[1024,768]{1,0:T(8,128)S(1)}, u32[]{:S(2)}, u32[]{:S(2)}) collective-permute-start(f32[1024,768]{1,0:T(8,128)S(1)} %fusion.27), channel_id=1, source_target_pairs={{0,1},{1,0},{2,3},{3,2},{4,5},{5,4},{6,7},{7,6},{8,9},{9,8},{10,11... | collective-permute-start | bytes 9437192 | tf_op jit(solution)/shard_map/ppermute | solution.py:723
  108.9 25.9 %copy-start.10 = (bf16[1024,768]{1,0:T(8,128)(2,1)}, bf16[1024,768]{1,0:T(8,128)(2,1)S(1)}, u32[]{:S(2)}) copy-start(bf16[1024,768]{1,0:T(8,128)(2,1)S(1)} %get-tuple-element.68) | copy-start | bytes 4718596
  110.3 24.5 %copy-start.22 = (bf16[768,1152]{1,0:T(8,128)(2,1)S(1)}, bf16[768,1152]{1,0:T(8,128)(2,1)}, u32[]{:S(2)}) copy-start(bf16[768,1152]{1,0:T(8,128)(2,1)} %constant_dynamic-update-slice_fusion) | copy-start | bytes 5308420
  138.7 19.3 %collective-permute-start.3 = (f32[1024,768]{1,0:T(8,128)}, f32[1024,768]{1,0:T(8,128)}, u32[]{:S(2)}, u32[]{:S(2)}) collective-permute-start(f32[1024,768]{1,0:T(8,128)} %fusion.29), channel_id=1, source_target_pairs={{0,1},{1,0},{2,3},{3,2},{4,5},{5,4},{6,7},{7,6},{8,9},{9,8},{10,11... | collective-permute-start | bytes 9437192 | tf_op jit(solution)/shard_map/ppermute | solution.py:723
  139.1 7.5 %copy-start.7 = (f32[1024,768]{1,0:T(8,128)S(1)}, f32[1024,768]{1,0:T(8,128)}, u32[]{:S(2)}) copy-start(f32[1024,768]{1,0:T(8,128)} %copy-done.6) | copy-start | bytes 9437188
  139.1 7.5 %copy-start.33 = (bf16[1024,1536]{1,0:T(8,128)(2,1)S(1)}, bf16[1024,1536]{1,0:T(8,128)(2,1)}, u32[]{:S(2)}) copy-start(bf16[1024,1536]{1,0:T(8,128)(2,1)} %copy-done.32) | copy-start | bytes 9437188
  146.5 5.3 %copy-start.11 = (bf16[1024,768]{1,0:T(8,128)(2,1)S(1)}, bf16[1024,768]{1,0:T(8,128)(2,1)}, u32[]{:S(2)}) copy-start(bf16[1024,768]{1,0:T(8,128)(2,1)} %copy-done.10) | copy-start | bytes 4718596
  485.4 12.8 %slice-start.2 = ((s8[4718592]{0:T(1024)(128)(4,1)}), s8[4194304]{0:T(1024)(128)(4,1)S(1)}, s32[]{:S(2)}) async-start(s8[4718592]{0:T(1024)(128)(4,1)} %bitcast.28), calls=%async_computation.2 | async-start | bytes 8388608
  485.4 8.8 %copy-start.17 = (f32[768,384]{1,0:T(8,128)S(1)}, f32[768,384]{1,0:T(8,128)}, u32[]{:S(2)}) copy-start(f32[768,384]{1,0:T(8,128)} %get-tuple-element.121) | copy-start | bytes 3538948
  485.4 9.8 %copy-start.16 = (f32[768,384]{1,0:T(8,128)S(1)}, f32[768,384]{1,0:T(8,128)}, u32[]{:S(2)}) copy-start(f32[768,384]{1,0:T(8,128)} %get-tuple-element.123) | copy-start | bytes 3538948
  485.4 12.8 %slice-start.3 = ((s8[4718592]{0:T(1024)(128)(4,1)}), s8[524288]{0:T(1024)(128)(4,1)S(1)}, s32[]{:S(2)}) async-start(s8[4718592]{0:T(1024)(128)(4,1)} %bitcast.28), calls=%async_computation.3 | async-start | bytes 1048576
  498.3 5.7 %copy-start.1 = (bf16[31,900,49]{1,0,2:T(8,128)(2,1)S(1)}, bf16[31,900,49]{1,0,2:T(8,128)(2,1)}, u32[]{:S(2)}) copy-start(bf16[31,900,49]{1,0,2:T(8,128)(2,1)} %param.30) | copy-start | bytes 8202604
  (19 other events, 49.1 us)

commit v3 on v2

v3 whole, which is shorter than its diff:
```python
import functools
import math

import jax
import jax.numpy as jnp
from jax import lax
from jax.experimental import pallas as pl
from jax.experimental.pallas import tpu as pltpu
from jax.sharding import PartitionSpec as P

HD = 64
VMEM = pl.BlockSpec(memory_space=pltpu.VMEM)
SMEM = pl.BlockSpec(memory_space=pltpu.SMEM)


def standardize(values):
    centered = values - jnp.mean(values, axis=-1, keepdims=True)
    spread = jnp.mean(centered * centered, axis=-1, keepdims=True)
    return centered * lax.rsqrt(spread + 1e-06)


FINE = 8
COARSE = (24, 30, 40, 48)


def nt(left, right):
    return lax.dot_general(left, right, (((1,), (1,)), ((), ())), preferred_element_type=jnp.float32)


def tn(left, right):
    return lax.dot_general(left, right, (((0,), (0,)), ((), ())), preferred_element_type=jnp.float32)


def nn(left, right):
    return jnp.dot(left, right, preferred_element_type=jnp.float32)


def up_to(value, step):
    return value + -value % step


def loop(count, body, unroll):
    if unroll:
        for i in range(count):
            body(i)
    else:
        pl.loop(0, count)(body)


def aligned(start, side):
    return pl.multiple_of(start, 8) if side % 8 == 0 and not isinstance(start, int) else start


def fill_pairs(pair, long, table, side):
    base = table.shape[1]
    entry = lax.broadcasted_iota(jnp.int32, (base, base * base), 0)
    place = lax.broadcasted_iota(jnp.int32, (base, base * base), 1)
    repeat = (place // base == entry).astype(jnp.bfloat16)
    tile = (place % base == entry).astype(jnp.bfloat16)
    wide = nn(table, repeat)[:side]
    long[...] = nn(table, tile)

    def one(s):
        pair[pl.ds(aligned(s * side, side), side), :] = wide * long[pl.ds(s, 1), :]

    loop(side, one, True)


def cut_patches(line, pix, image, channel, side, grid, res):
    def one(x):
        block = pix[image, channel, pl.ds(aligned(x * side, side), side), :]
        line[pl.ds(aligned(x * res, 8), res), :side] = block.T[:res]

    loop(grid, one, True)
    return jnp.concatenate(
        [line[pl.ds(s, grid * grid, stride=side), :side] for s in range(side)], axis=1
    ).astype(jnp.bfloat16)


def place_patches(line, pixel_grad, image, channel, patch, side, grid, res):
    for s in range(side):
        line[pl.ds(s, grid * grid, stride=side), :side] = patch[:, s * side : (s + 1) * side]

    def one(x):
        block = line[pl.ds(aligned(x * res, 8), res), :side]
        pixel_grad[image, channel, pl.ds(aligned(x * side, side), side), :] = block.T

    loop(grid, one, True)


def embed_kernel(
    sizes,
    order,
    pix,
    table,
    pos_fine,
    pos,
    weight,
    bias,
    pos_base,
    emb,
    tokens,
    patches,
    mixed_weight,
    line,
    pair,
    long,
):
    area = table.shape[2] ** 2
    channels, res = pix.shape[1:3]
    grid = res // FINE
    count = grid * grid
    start = up_to(count, 16)
    stride = tokens.shape[1]
    low = jnp.bfloat16
    emb[...] = jnp.broadcast_to(bias[...], emb.shape)

    fill_pairs(pair, long, table[0], FINE)
    fine_pairs = pair[: FINE * FINE, :].astype(low)
    emb[:count, :] += nt(pos_fine[...], pos_base[...])

    @functools.partial(loop, channels, unroll=True)
    def _(c):
        columns = pl.ds(c * area, area)
        patch = cut_patches(line, pix, order[0], c, FINE, grid, res)
        mixed = nt(fine_pairs, weight[:, columns]).astype(low)
        mixed_weight[c] = mixed
        patches[c, :count, :] = patch
        emb[:count, :] += nn(patch, mixed)

    @pl.loop(1, 4)
    def _(slot):
        row = pl.multiple_of(start + (slot - 1) * stride, 8)
        for side in COARSE:
            grid = res // side
            count = grid * grid

            @pl.when(sizes[slot] == side)
            def _():
                fill_pairs(pair, long, table[slot], side)
                here = pl.ds(row, count)
                emb[here, :] += nt(pos[slot - 1, :count, :], pos_base[...])

                @functools.partial(loop, channels, unroll=True)
                def _(c):
                    columns = pl.ds(c * area, area)
                    patch = cut_patches(line, pix, order[slot], c, side, grid, res)
                    token = nn(patch, pair[: side * side, :].astype(low)).astype(low)
                    tokens[slot - 1, :count, columns] = token
                    emb[here, :] += nt(token, weight[:, columns])


def embed(sizes, order, pix, table, pos_fine, pos, w_base, patch_bias, pos_base, rows):
    _, channels, res, _ = pix.shape
    width, features = w_base.shape
    fine = (res // FINE) ** 2
    side = table.shape[1]
    area = features // channels
    return pl.pallas_call(
        embed_kernel,
        out_shape=[
            jax.ShapeDtypeStruct((rows, width), jnp.float32),
            jax.ShapeDtypeStruct((3, up_to(pos.shape[1], 8), features), jnp.bfloat16),
            jax.ShapeDtypeStruct((channels, up_to(fine, 16), FINE * FINE), jnp.bfloat16),
            jax.ShapeDtypeStruct((channels, FINE * FINE, width), jnp.bfloat16),
        ],
        in_specs=[SMEM] * 2 + [VMEM] * 7,
        out_specs=[VMEM] * 4,
        scratch_shapes=[
            pltpu.VMEM((res * res // FINE, 128), jnp.float32),
            pltpu.VMEM((side * side, area), jnp.float32),
            pltpu.VMEM((side, area), jnp.float32),
        ],
        compiler_params=pltpu.CompilerParams(vmem_limit_bytes=48 << 20),
        name="embed",
    )(
        sizes,
        order,
        pix,
        table,
        pos_fine,
        pos,
        w_base,
        patch_bias.astype(jnp.float32)[None],
        pos_base,
    )


def pixel_kernel(
    sizes,
    place,
    grad,
    table,
    pos_fine,
    pos,
    weight,
    tokens,
    patches,
    mixed_weight,
    pixel_grad,
    grad_weight,
    grad_pos,
    line,
    pair,
    long,
):
    area = table.shape[2] ** 2
    channels, res = pixel_grad.shape[1:3]
    half = grad_weight.shape[0]
    part = grad_weight.shape[1] // channels
    core_columns = pl.ds(pl.multiple_of(place[0] * half, 128), half)
    side_start = place[1] * part
    is_fine = place[2]
    grid = res // FINE
    count = grid * grid
    start = up_to(count, 16)
    stride = tokens.shape[1]
    low = jnp.bfloat16

    fill_pairs(pair, long, table[0], FINE)
    some_pairs = pair[: FINE * FINE, pl.ds(pl.multiple_of(side_start, 128), part)].astype(low)
    rows = grad[:count, :].astype(low)
    some = grad[:count, core_columns].astype(low)
    grad_pos[...] = tn(pos_fine[...], rows)

    @pl.loop(0, channels)
    def _(c):
        gathered = tn(patches[c, :count, :], some).astype(low)
        grad_weight[:, pl.ds(pl.multiple_of(c * part, 128), part)] = tn(gathered, some_pairs)

        @pl.when(is_fine == 1)
        def _():
            patch = nt(grad[:count, :].astype(low), mixed_weight[c])
            place_patches(line, pixel_grad, 0, c, patch, FINE, grid, res)

    @pl.loop(1, 4)
    def _(slot):
        row = pl.multiple_of(start + (slot - 1) * stride, 8)
        wanted = jnp.where(slot == 1, is_fine, 1 - is_fine)
        image = jnp.where(slot == 1, 1, slot - 2)
        for side in COARSE:
            grid = res // side
            count = grid * grid

            @pl.when(sizes[slot] == side)
            def _():
                here = pl.ds(row, count)
                rows = grad[here, :].astype(low)
                some = grad[here, core_columns].astype(low)
                grad_pos[...] += tn(pos[slot - 1, :count, :], rows)

                @pl.loop(0, channels)
                def _(c):
                    columns = pl.ds(pl.multiple_of(c * area + side_start, 128), part)
                    grad_weight[:, pl.ds(pl.multiple_of(c * part, 128), part)] += tn(
                        some, tokens[slot - 1, :count, columns]
                    )

                @pl.when(wanted == 1)
                def _():
                    fill_pairs(pair, long, table[slot], side)

                    @pl.loop(0, channels)
                    def _(c):
                        columns = pl.ds(pl.multiple_of(c * area, area), area)
                        token = nn(grad[here, :].astype(low), weight[:, columns]).astype(low)
                        patch = nt(token, pair[: side * side, :].astype(low))
                        place_patches(line, pixel_grad, image, c, patch, side, grid, res)


def pixel_back(
    sizes, place, grad, table, pos_fine, pos, w_base, tokens, patches, mixed_weight, shape
):
    _, channels, res, _ = shape
    width, features = w_base.shape
    side = table.shape[1]
    return pl.pallas_call(
        pixel_kernel,
        out_shape=[
            jax.ShapeDtypeStruct(shape, jnp.float32),
            jax.ShapeDtypeStruct((width // 2, features // 2), jnp.float32),
            jax.ShapeDtypeStruct((pos.shape[2], width), jnp.float32),
        ],
        in_specs=[SMEM] * 2 + [VMEM] * 8,
        out_specs=[VMEM] * 3,
        scratch_shapes=[
            pltpu.VMEM((res * res // FINE, 128), jnp.float32),
            pltpu.VMEM((side * side, features // channels), jnp.float32),
            pltpu.VMEM((side, features // channels), jnp.float32),
        ],
        compiler_params=pltpu.CompilerParams(vmem_limit_bytes=48 << 20),
        name="pixel_back",
    )(sizes, place, grad, table, pos_fine, pos, w_base, tokens, patches, mixed_weight)


PAIR = 2 * HD


def pair_halves(rows):
    lane = lax.broadcasted_iota(jnp.int32, (rows, PAIR), 1)
    return [lane < HD, lane >= HD]


def attend_block(scale, query, key, value, mask):
    halves = pair_halves(query.shape[0])
    both = []
    for h in range(2):
        own = jnp.where(halves[h], query, jnp.zeros_like(query))
        scores = jnp.where(mask, nt(own, key) * scale, -1000000000.0)
        weights = jnp.exp(scores - jnp.max(scores, axis=1, keepdims=True))
        inverse = 1.0 / jnp.sum(weights, axis=1, keepdims=True)
        both.append(nn((weights * inverse).astype(jnp.bfloat16), value))
    return jnp.where(halves[0], both[0], both[1]).astype(jnp.bfloat16)


def block_masks(fine, start, rows, segment, segment_row, axis):
    inside = lax.broadcasted_iota(jnp.int32, (start, start), axis) < fine
    same = segment[start:rows, :] == segment_row[:, : rows - start]
    return inside, same


def attend_kernel(scale, fine, start, query, key, value, segment, segment_row, mixed):
    rows = query.shape[0]
    masks = block_masks(fine, start, rows, segment, segment_row, 1)
    for here, mask in zip((slice(0, start), slice(start, rows)), masks):
        mixed[here, :] = attend_block(scale, query[here, :], key[here, :], value[here, :], mask)


def attend(qkv, segment, fine, start):
    rows, width = qkv.shape
    heads = width // 3 // PAIR
    kernel = functools.partial(attend_kernel, 1.0 / math.sqrt(HD), fine, start)
    column = lambda k: pl.BlockSpec((rows, PAIR), lambda j: (0, k * heads + j))
    return pl.pallas_call(
        kernel,
        grid=(heads,),
        out_shape=jax.ShapeDtypeStruct((rows, width // 3), jnp.bfloat16),
        in_specs=[
            column(0),
            column(1),
            column(2),
            pl.BlockSpec((rows, 1), lambda j: (0, 0)),
            pl.BlockSpec((1, rows - start), lambda j: (0, 0)),
        ],
        out_specs=column(0),
        compiler_params=pltpu.CompilerParams(vmem_limit_bytes=48 << 20),
        name="attend",
    )(qkv, qkv, qkv, segment[:, None], segment[None, start:])


def attend_back_block(scale, query, key, value, grad_mixed, mask):
    halves = pair_halves(query.shape[0])
    grad_query, grad_key, grad_value = [], 0.0, 0.0
    for h in range(2):
        own = jnp.where(halves[h], query, jnp.zeros_like(query))
        grad = jnp.where(halves[h], grad_mixed, jnp.zeros_like(grad_mixed))
        scores = jnp.where(mask, nt(key, own) * scale, -1000000000.0)
        weights = jnp.exp(scores - jnp.max(scores, axis=0, keepdims=True))
        probs = weights * (1.0 / jnp.sum(weights, axis=0, keepdims=True))
        grad_probs = nt(value, grad)
        inner = jnp.sum(probs * grad_probs, axis=0, keepdims=True)
        grad_scores = (probs * (grad_probs - inner)).astype(jnp.bfloat16)
        grad_value = grad_value + nn(probs.astype(jnp.bfloat16), grad)
        grad_key = grad_key + nn(grad_scores, own)
        grad_query.append(tn(grad_scores, key))
    grad_query = jnp.where(halves[0], grad_query[0], grad_query[1])
    low = lambda value: value.astype(jnp.bfloat16)
    return low(grad_query * scale), low(grad_key * scale), low(grad_value)


def attend_back_kernel(
    scale, fine, start, query, key, value, grad_mixed, segment, segment_row, grad_qkv
):
    rows = query.shape[0]
    third = grad_qkv.shape[1] // 3
    column = pl.multiple_of(pl.program_id(0) * PAIR, PAIR)
    masks = block_masks(fine, start, rows, segment, segment_row, 0)
    for here, mask in zip((slice(0, start), slice(start, rows)), masks):
        grads = attend_back_block(
            scale, query[here, :], key[here, :], value[here, :], grad_mixed[here, :], mask
        )
        for k in range(3):
            grad_qkv[here, pl.ds(k * third + column, PAIR)] = grads[k]


def attend_back(qkv, grad_mixed, segment, fine, start):
    rows, width = qkv.shape
    heads = width // 3 // PAIR
    kernel = functools.partial(attend_back_kernel, 1.0 / math.sqrt(HD), fine, start)
    column = lambda k: pl.BlockSpec((rows, PAIR), lambda j: (0, k * heads + j))
    return pl.pallas_call(
        kernel,
        grid=(heads,),
        out_shape=jax.ShapeDtypeStruct((rows, width), jnp.bfloat16),
        in_specs=[
            column(0),
            column(1),
            column(2),
            column(0),
            pl.BlockSpec((rows, 1), lambda j: (0, 0)),
            pl.BlockSpec((1, rows - start), lambda j: (0, 0)),
        ],
        out_specs=pl.BlockSpec((rows, width), lambda j: (0, 0)),
        compiler_params=pltpu.CompilerParams(vmem_limit_bytes=48 << 20),
        name="attend_back",
    )(qkv, qkv, qkv, grad_mixed, segment[:, None], segment[None, start:])


LINE = 4
MESH_ID = pl.DeviceIdType.MESH
PIECE_ROWS = 192
PIECE_COLS = 384
CROSS_EVERY = 4
SEMS = 48


class Piece:
    def __init__(self, source, row, col, rows, cols, target, out_row, out_col, swap, cross):
        self.source, self.row, self.col, self.rows, self.cols = source, row, col, rows, cols
        self.target, self.out_row, self.out_col = target, out_row, out_col
        self.swap, self.cross = swap, cross


def sync_kernel(pieces, scale, in_count, out_count, *refs):
    grads = refs[:in_count]
    outs = refs[in_count : in_count + out_count]
    acc, land, land_right, land_left, sems = refs[in_count + out_count :]
    device = lax.axis_index("dp")
    core = lax.axis_index("tensor")
    place_x = lax.rem(device, 2)
    place_y = lax.rem(device // 2, 2)
    place_z = lax.rem(device // 4, LINE)
    mirror = LINE - 1 - place_z
    beside_x = (device + 1 - 2 * place_x, core)
    beside_y = (device + 2 - 4 * place_y, core)
    sibling = (device, 1 - core)
    up = (device + 4, core)
    down = (device - 4, core)

    barrier = pltpu.get_barrier_semaphore()
    for partner in (beside_x, beside_y, sibling):
        pl.semaphore_signal(barrier, inc=1, device_id=partner, device_id_type=MESH_ID)

    @pl.when(place_z < LINE - 1)
    def _():
        pl.semaphore_signal(barrier, inc=1, device_id=up, device_id_type=MESH_ID)

    @pl.when(place_z > 0)
    def _():
        pl.semaphore_signal(barrier, inc=1, device_id=down, device_id_type=MESH_ID)

    inner = (place_z + LINE - 1) // LINE + (2 * (LINE - 1) - place_z) // LINE
    pl.semaphore_wait(barrier, 3 + inner)

    def rows_at(ref, start, size, column, width):
        return ref.at[pl.ds(pl.multiple_of(start, 8), size), pl.ds(pl.multiple_of(column, 128), width)]

    def remote(src, dst, send, recv, where):
        return pltpu.make_async_remote_copy(
            src_ref=src,
            dst_ref=dst,
            send_sem=send,
            recv_sem=recv,
            device_id=where,
            device_id_type=MESH_ID,
        )

    def add_rows(total, start, extra, size, width, factor=None):
        step = 24 if size % 24 == 0 else 8

        @pl.loop(0, size // step)
        def _(i):
            here = pl.ds(pl.multiple_of(start + i * step, 8), step)
            there = pl.ds(pl.multiple_of(i * step, 8), step)
            value = total[here, :width] + extra[there, :width]
            total[here, :width] = value if factor is None else value * factor

    def build(number, piece):
        half, chunk, width = piece.rows // 2, piece.rows // 8, piece.cols
        grad, out = grads[piece.source], outs[piece.target]
        mine = acc.at[number]
        sem = lambda k: sems.at[number, k]

        def out_at(x, owner, row, size):
            return rows_at(out, piece.out_row(x, owner) + row, size, piece.out_col(x), width)

        def y_copy():
            return remote(
                rows_at(grad, piece.row + (1 - place_y) * half, half, piece.col, width),
                land.at[number, :half, :width],
                sem(0),
                sem(1),
                beside_y,
            )

        def load():
            return pltpu.make_async_copy(
                rows_at(grad, piece.row + place_y * half, half, piece.col, width),
                mine.at[:half, :width],
                sem(2),
            )

        def right(k):
            return remote(
                rows_at(mine, (LINE - k + place_z) * chunk, chunk, 0, width),
                land_right.at[number, k - 1, :chunk, :width],
                sem(2 + k),
                sem(5 + k),
                up,
            )

        def left(k):
            return remote(
                rows_at(mine, (k - 1 - mirror) * chunk, chunk, 0, width),
                land_left.at[number, k - 1, :chunk, :width],
                sem(8 + k),
                sem(11 + k),
                down,
            )

        def got(slots, k, first, where):
            here = slots.at[number, k - 1, :chunk, :width]
            return remote(here, here, sem(first + k), sem(first + 3 + k), where)

        def send_line(k):
            @pl.when((place_z <= k - 1) & (place_z < LINE - 1))
            def _():
                right(k).start()

            @pl.when((mirror <= k - 1) & (mirror < LINE - 1))
            def _():
                left(k).start()

        def wait_line(k):
            @pl.when((place_z >= 1) & (place_z <= k))
            def _():
                got(land_right, k, 2, down).wait_recv()
                add_rows(
                    mine, (LINE - 1 - k + place_z) * chunk, land_right.at[number, k - 1], chunk, width
                )

            @pl.when((mirror >= 1) & (mirror <= k))
            def _():
                got(land_left, k, 8, up).wait_recv()
                add_rows(mine, (k - mirror) * chunk, land_left.at[number, k - 1], chunk, width)

        def own_chunk():
            return rows_at(mine, place_z * chunk, chunk, 0, width)

        def store():
            return pltpu.make_async_copy(
                own_chunk(), out_at(place_x, core, place_y * half + place_z * chunk, chunk), sem(17)
            )

        def share_out():
            return remote(
                own_chunk(),
                out_at(place_x, core, place_y * half + place_z * chunk, chunk),
                sem(15),
                sem(16),
                beside_x if piece.cross else beside_y,
            )

        def share_in():
            if piece.cross:
                there = out_at(1 - place_x, core, place_y * half + place_z * chunk, chunk)
                return remote(there, there, sem(15), sem(16), beside_x)
            there = out_at(place_x, core, (1 - place_y) * half + place_z * chunk, chunk)
            return remote(there, there, sem(15), sem(16), beside_y)

        def spread(k, position, where, first):
            copies = []
            for b in range(2):
                if piece.cross:
                    here = out_at(b, core, place_y * half + position * chunk, chunk)
                else:
                    here = out_at(place_x, core, b * half + position * chunk, chunk)
                at = first + 2 * (k - 1) + b
                copies.append(remote(here, here, sem(at), sem(at + 6), where))
            return copies

        def send_spread(k):
            @pl.when((place_z >= k - 1) & (place_z < LINE - 1))
            def _():
                for copy in spread(k, place_z - (k - 1), up, 18):
                    copy.start()

            @pl.when((mirror >= k - 1) & (mirror < LINE - 1))
            def _():
                for copy in spread(k, place_z + (k - 1), down, 30):
                    copy.start()

        def wait_spread(k):
            @pl.when(place_z >= k)
            def _():
                for copy in spread(k, place_z - k, down, 18):
                    copy.wait_recv()

            @pl.when(mirror >= k)
            def _():
                for copy in spread(k, place_z + k, up, 30):
                    copy.wait_recv()

        def last(outgoing):
            if piece.cross:
                row = (place_y if outgoing else 1 - place_y) * half
                views = [out_at(b, core, row, half) for b in range(2)]
                return [
                    remote(v, v, sem(42 + b), sem(44 + b), beside_y) for b, v in enumerate(views)
                ]
            view = out_at(place_x if outgoing else 1 - place_x, core, 0, piece.rows)
            return [remote(view, view, sem(42), sem(44), beside_x)]

        def swap(owner):
            views = [out_at(b, owner, 0, piece.rows) for b in range(2)]
            return [remote(v, v, sem(46 + b), sem(48 + b), sibling) for b, v in enumerate(views)]

        def stage_0():
            y_copy().start()
            load().start()

        def stage_1():
            load().wait()
            y_copy().wait_recv()
            add_rows(mine, 0, land.at[number], half, width)
            send_line(1)

        def stage_2():
            wait_line(1)
            send_line(2)

        def stage_3():
            wait_line(2)
            send_line(3)

        def stage_4():
            wait_line(3)

            @pl.loop(0, chunk // 8)
            def _(i):
                here = pl.ds(pl.multiple_of(place_z * chunk + i * 8, 8), 8)
                mine[here, :width] = mine[here, :width] * scale

            share_out().start()
            store().start()

        def stage_5():
            store().wait()
            share_in().wait_recv()
            send_spread(1)

        def stage_6():
            wait_spread(1)
            send_spread(2)

        def stage_7():
            wait_spread(2)
            send_spread(3)

        def stage_8():
            wait_spread(3)
            for copy in last(True):
                copy.start()

        def stage_9():
            for copy in last(False):
                copy.wait_recv()
            if piece.swap:
                for copy in swap(core):
                    copy.start()

        def stage_10():
            if piece.swap:
                for copy in swap(1 - core):
                    copy.wait_recv()
                for copy in swap(core):
                    copy.wait_send()
            y_copy().wait_send()
            share_out().wait_send()
            for copy in last(True):
                copy.wait_send()
            for k in range(1, LINE):

                @pl.when((place_z <= k - 1) & (place_z < LINE - 1))
                def _():
                    right(k).wait_send()

                @pl.when((mirror <= k - 1) & (mirror < LINE - 1))
                def _():
                    left(k).wait_send()

                @pl.when((place_z >= k - 1) & (place_z < LINE - 1))
                def _():
                    for copy in spread(k, place_z - (k - 1), up, 18):
                        copy.wait_send()

                @pl.when((mirror >= k - 1) & (mirror < LINE - 1))
                def _():
                    for copy in spread(k, place_z + (k - 1), down, 30):
                        copy.wait_send()

        return [
            stage_0,
            stage_1,
            stage_2,
            stage_3,
            stage_4,
            stage_5,
            stage_6,
            stage_7,
            stage_8,
            stage_9,
            stage_10,
        ]

    lines = [build(number, piece) for number, piece in enumerate(pieces)]
    groups = [lines[i : i + GROUP] for i in range(0, len(lines), GROUP)]
    depth = len(lines[0])
    for j in range(min(AHEAD, len(groups))):
        for line in groups[j]:
            line[0]()
    late = depth - 2
    for tick in range(len(groups) + depth - 1):
        if tick + AHEAD < len(groups):
            for line in groups[tick + AHEAD]:
                line[0]()
        active = range(max(0, tick - depth + 1), min(tick, len(groups)))
        for j in [j for j in active if tick - j < late] + [j for j in active if tick - j >= late]:
            for line in groups[j]:
                line[tick - j]()


GROUP = 1
AHEAD = 1


def sync_plan(grads, outs):
    pieces = []
    for source, (rows, cols) in enumerate(grads):
        start = 0
        for target, width, row_x, row_core, col_x, block in outs[source]:
            tall = min(PIECE_ROWS, rows)
            wide = min(PIECE_COLS, width) if block is None else width
            for row in range(0, rows, tall):
                for col in range(0, width, wide) if block is None else range(1):
                    out_col = col if block is None else block
                    pieces.append(
                        Piece(
                            source,
                            row,
                            start + col,
                            tall,
                            wide,
                            target,
                            lambda x, core, row=row, a=row_x, b=row_core: row + x * a + core * b,
                            lambda x, c=out_col, a=col_x: c + x * a,
                            row_core != 0,
                            len(pieces) % CROSS_EVERY == CROSS_EVERY - 1,
                        )
                    )
            start += width
    return pieces


def sync_grads(grads, out_shapes, outs, replicas):
    pieces = sync_plan([g.shape for g in grads], outs)
    count = len(pieces)
    high = max(p.rows for p in pieces)
    wide = max(p.cols for p in pieces)
    kernel = functools.partial(sync_kernel, pieces, 1.0 / replicas, len(grads), len(out_shapes))
    vmem = lambda *dims: pltpu.VMEM(dims, jnp.float32)
    return pl.pallas_call(
        kernel,
        out_shape=[jax.ShapeDtypeStruct(s, jnp.float32) for s in out_shapes],
        in_specs=[pl.BlockSpec(memory_space=pl.ANY)] * len(grads),
        out_specs=[pl.BlockSpec(memory_space=pl.ANY)] * len(out_shapes),
        scratch_shapes=[
            vmem(count, high // 2, wide),
            vmem(count, high // 2, wide),
            vmem(count, LINE - 1, high // 8, wide),
            vmem(count, LINE - 1, high // 8, wide),
            pltpu.SemaphoreType.DMA((count, SEMS + 2)),
        ],
        compiler_params=pltpu.CompilerParams(
            collective_id=0, has_side_effects=True, vmem_limit_bytes=56 << 20
        ),
        name="sync_grads",
    )(*grads)


def tensor_sum(partial):
    return partial + lax.ppermute(partial, "tensor", [(0, 1), (1, 0)])


def from_partner(mine, core, replicas):
    there = [(i, i ^ 1) for i in range(replicas)]
    direct = lax.ppermute(mine, "dp", there)
    across = lax.ppermute(direct, "tensor", [(0, 1), (1, 0)])
    return direct, across


def merged_rows(fine_rows, light_rows, second, counts, start, stride, rows):
    width = fine_rows.shape[1]
    small = stride - stride % 4
    keep = jnp.arange(stride, dtype=jnp.int32)[:, None]
    fine = fine_rows.shape[0]
    padded = jnp.pad(light_rows, ((0, stride), (0, 0)))
    third = padded[:stride]
    fourth = lax.dynamic_slice_in_dim(padded, counts[2], stride, axis=0)
    blocks = [
        jnp.pad(fine_rows, ((0, start - fine), (0, 0))),
        jnp.pad(second, ((0, stride - second.shape[0]), (0, 0))),
        jnp.where(keep < counts[2], third, 0.0),
        jnp.where(keep < counts[3], fourth, 0.0),
        jnp.zeros((rows - start - 3 * stride, width), fine_rows.dtype),
    ]
    return jnp.concatenate(blocks, axis=0)


def own_rows(merged, is_fine, counts, fine, start, stride, rows):
    width = merged.shape[1]
    coarse = counts[1]
    heavy = jnp.concatenate(
        [
            merged[:fine],
            merged[start : start + stride],
            jnp.zeros((rows - fine - stride, width), merged.dtype),
        ],
        axis=0,
    )
    row = jnp.arange(rows, dtype=jnp.int32)[:, None]
    third = jnp.pad(merged[start + stride : start + 2 * stride], ((0, rows - stride), (0, 0)))
    fourth = jnp.pad(merged[start + 2 * stride : start + 3 * stride], ((stride, rows), (0, 0)))
    fourth = lax.dynamic_slice_in_dim(fourth, stride - counts[2], rows, axis=0)
    light = jnp.where(row < counts[2], third, fourth)
    used = jnp.where(is_fine, fine + coarse, counts[2] + counts[3])
    return jnp.where(row < used, jnp.where(is_fine, heavy, light), jnp.zeros_like(heavy))


def local(
    pixels,
    patch_size,
    counts,
    offsets,
    resize_table,
    pos_table,
    w_base,
    patch_bias,
    pos_base,
    gain_one,
    shift_one,
    w_query,
    bias_query,
    w_key,
    w_value,
    bias_value,
    w_out,
    bias_out,
    gain_two,
    shift_two,
    w_up,
    bias_up,
    w_down,
    bias_down,
    cotangent,
):
    wide = lambda value: value.astype(jnp.float32)
    images, channels, res, _ = pixels.shape
    rows_total = cotangent.shape[0]
    replicas = lax.axis_size("dp")
    core = lax.axis_index("tensor")
    side_x = lax.rem(lax.axis_index("dp"), 2)
    fine = (res // FINE) ** 2
    small = (res // COARSE[0]) ** 2
    start = up_to(fine, 16)
    stride = up_to(small, 8)
    rows = up_to(start + 3 * stride, 16)

    lane = jnp.arange(up_to(res, 128), dtype=jnp.int32)
    own_pix = jnp.pad(wide(pixels), ((0, 0), (0, 0), (0, 0), (0, -res % 128)))
    own_pix = jnp.where(lane == res, wide(patch_size)[:, None, None, None], own_pix)
    direct, across = from_partner(
        lax.dynamic_index_in_dim(own_pix, core, 0, keepdims=False), core, replicas
    )
    pix = jnp.concatenate([own_pix, direct[None], across[None]], axis=0)
    half_rows = rows_total // 2
    own_cotangent = wide(cotangent)
    cot_direct, cot_across = from_partner(
        lax.dynamic_slice_in_dim(own_cotangent, core * half_rows, half_rows, axis=0),
        core,
        replicas,
    )
    is_fine = patch_size[0] == FINE
    other = jnp.where(core == 0, jnp.array([2, 3], jnp.int32), jnp.array([3, 2], jnp.int32))
    order = jnp.where(
        is_fine,
        jnp.concatenate([jnp.array([0, 1], jnp.int32), other]),
        jnp.concatenate([other, jnp.array([0, 1], jnp.int32)]),
    )
    found = jnp.concatenate([patch_size, jnp.stack([direct[0, 0, res], across[0, 0, res]]).astype(jnp.int32)])
    sizes = jnp.take(found, order)
    counts4 = (res // sizes) ** 2
    table = jnp.take(resize_table, sizes, axis=0)
    pos_fine = pos_table[res // FINE, :fine]
    pos = jnp.take(pos_table[:, :small], res // sizes[1:], axis=0)

    row = jnp.arange(rows, dtype=jnp.int32)
    slot = jnp.where(row < start, 0, (row - start) // stride + 1)
    first = jnp.where(slot == 0, 0, start + (slot - 1) * stride)
    limit = jnp.where(
        slot == 0,
        counts4[0],
        jnp.where(slot == 1, counts4[1], jnp.where(slot == 2, counts4[2], counts4[3])),
    )
    valid = (slot < 4) & (row - first < limit)
    segment = jnp.where(valid, slot, 4)
    valid_rows = wide(valid)[:, None]

    embedded, tokens, patches, mixed_weight = embed(
        sizes, order, pix, table, pos_fine, pos, w_base, patch_bias, pos_base, rows
    )
    w_qkv = jnp.concatenate([w_query, w_key, w_value], axis=1)
    bias_qkv = jnp.concatenate([bias_query, jnp.zeros_like(bias_query), bias_value])
    standard_one, standard_back_one = jax.vjp(standardize, embedded)
    normed_one = (standard_one * wide(gain_one) + wide(shift_one)).astype(jnp.bfloat16)
    qkv = (
        jnp.dot(normed_one, w_qkv, preferred_element_type=jnp.float32) + wide(bias_qkv)
    ).astype(jnp.bfloat16)
    mixed = attend(qkv, segment, fine, start)
    attended = tensor_sum(jnp.dot(mixed, w_out, preferred_element_type=jnp.float32)) + wide(
        bias_out
    )
    middle = embedded + attended
    standard_two, standard_back_two = jax.vjp(standardize, middle)
    normed_two = (standard_two * wide(gain_two) + wide(shift_two)).astype(jnp.bfloat16)
    hidden = jnp.dot(normed_two, w_up, preferred_element_type=jnp.float32) + wide(bias_up)
    activated_wide, gelu_back = jax.vjp(jax.nn.gelu, hidden)
    activated = activated_wide.astype(jnp.bfloat16)
    branch = tensor_sum(jnp.dot(activated, w_down, preferred_element_type=jnp.float32)) + wide(
        bias_down
    )
    output = own_rows(
        (middle + branch).astype(jnp.bfloat16), is_fine, counts4, fine, start, stride, rows_total
    )
    other_cotangent = jnp.where(
        core == 0,
        jnp.concatenate([cot_direct, cot_across]),
        jnp.concatenate([cot_across, cot_direct]),
    )
    fine_cotangent = jnp.where(is_fine, own_cotangent, other_cotangent)
    light_cotangent = jnp.where(
        is_fine, other_cotangent[: 2 * stride], own_cotangent[: 2 * stride]
    )
    grad_out = (
        merged_rows(
            fine_cotangent[:fine],
            light_cotangent,
            fine_cotangent[fine : fine + small],
            counts4,
            start,
            stride,
            rows,
        )
        * valid_rows
    )
    grad_branch = grad_out.astype(jnp.bfloat16)
    own_part = lambda value: lax.dynamic_slice_in_dim(
        value, side_x * (value.shape[1] // 2), value.shape[1] // 2, axis=1
    )
    grad_w_down = jnp.einsum(
        "tf,td->fd", own_part(activated), grad_branch, preferred_element_type=jnp.float32
    )
    grad_activated = jnp.einsum(
        "td,fd->tf", grad_branch, w_down, preferred_element_type=jnp.float32
    )
    grad_hidden = gelu_back(grad_activated)[0].astype(jnp.bfloat16)
    grad_w_up = jnp.einsum(
        "td,tf->df", own_part(normed_two), grad_hidden, preferred_element_type=jnp.float32
    )
    grad_bias_up = jnp.sum(grad_hidden, axis=0, dtype=jnp.float32)
    grad_normed_two = tensor_sum(
        jnp.einsum("tf,df->td", grad_hidden, w_up, preferred_element_type=jnp.float32)
    )
    grad_middle = grad_out + standard_back_two(grad_normed_two * wide(gain_two))[0]
    grad_attended = grad_middle.astype(jnp.bfloat16)
    grad_w_out = jnp.einsum(
        "te,td->ed", own_part(mixed), grad_attended, preferred_element_type=jnp.float32
    )
    grad_mixed = jnp.einsum(
        "td,ed->te", grad_attended, w_out, preferred_element_type=jnp.float32
    ).astype(jnp.bfloat16)
    grad_qkv = attend_back(qkv, grad_mixed, segment, fine, start)
    grad_w_qkv = jnp.einsum(
        "td,te->de", own_part(normed_one), grad_qkv, preferred_element_type=jnp.float32
    )
    grad_bias_qkv = jnp.sum(grad_qkv, axis=0, dtype=jnp.float32)
    cut = bias_query.shape[0]
    grad_bias_query, grad_bias_value = grad_bias_qkv[:cut], grad_bias_qkv[2 * cut :]
    grad_normed_one = tensor_sum(
        jnp.einsum("te,de->td", grad_qkv, w_qkv, preferred_element_type=jnp.float32)
    )
    grad_embedded = grad_middle + standard_back_one(grad_normed_one * wide(gain_one))[0]
    grad_embedded_low = grad_embedded.astype(jnp.bfloat16)
    pixel_grad, grad_w_base, grad_pos_base = pixel_back(
        sizes,
        jnp.stack([core, side_x, is_fine.astype(jnp.int32)]),
        grad_embedded,
        table,
        pos_fine,
        pos,
        w_base,
        tokens,
        patches,
        mixed_weight,
        pixels.shape,
    )
    grad_patch_bias = jnp.sum(grad_embedded_low, axis=0, dtype=jnp.float32)
    grad_gain_one = jnp.sum(grad_normed_one * standard_one, axis=0)
    grad_shift_one = jnp.sum(grad_normed_one, axis=0)
    grad_bias_out = jnp.sum(grad_attended, axis=0, dtype=jnp.float32)
    grad_gain_two = jnp.sum(grad_normed_two * standard_two, axis=0)
    grad_shift_two = jnp.sum(grad_normed_two, axis=0)
    grad_bias_down = jnp.sum(grad_branch, axis=0, dtype=jnp.float32)
    width = grad_patch_bias.shape[0]
    small_rows = [
        grad_pos_base,
        grad_patch_bias[None],
        grad_gain_one[None],
        grad_shift_one[None],
        grad_bias_out[None],
        grad_gain_two[None],
        grad_shift_two[None],
        grad_bias_down[None],
        jnp.concatenate([grad_bias_query, grad_bias_value])[None],
        grad_bias_up.reshape(-1, width),
    ]
    bundle = jnp.concatenate(small_rows, axis=0)
    used = bundle.shape[0]
    bundle = jnp.pad(bundle, ((0, -used % 128), (0, 0)))
    bundle_part = lax.dynamic_slice_in_dim(
        bundle, side_x * (bundle.shape[0] // 2), bundle.shape[0] // 2, axis=0
    )
    parts = [grad_w_down, grad_w_up, grad_w_qkv, grad_w_base, grad_w_out, bundle_part]
    beyond = replicas // 16
    step = 1
    while step < beyond:
        swap = [(i, (i // 16 ^ step) * 16 + i % 16) for i in range(replicas)]
        parts = [part + lax.ppermute(part, "dp", swap) for part in parts]
        step *= 2
    area = w_base.shape[1] // channels
    base_shape = (2 * grad_w_base.shape[0], w_base.shape[1])
    ff = w_down.shape[0]
    deep = w_up.shape[0]
    out_shapes = [
        base_shape,
        w_down.shape,
        w_up.shape,
        w_query.shape,
        w_key.shape,
        w_value.shape,
        w_out.shape,
        bundle.shape,
    ]
    outs = [
        [(1, width, ff // 2, 0, 0, None)],
        [(2, ff, deep // 2, 0, 0, None)],
        [(3 + k, cut, deep // 2, 0, 0, None) for k in range(3)],
        [(0, area // 2, 0, width // 2, area // 2, area * c) for c in range(channels)],
        [(6, width, cut // 2, 0, 0, None)],
        [(7, width, bundle.shape[0] // 2, 0, 0, None)],
    ]
    synced = sync_grads(parts, out_shapes, outs, replicas)
    base_s, down_s, up_s, query_s, key_s, value_s, out_s, small_s = synced
    points = pos.shape[2]
    line = lambda k: small_s[points + k]
    return (
        output,
        pixel_grad,
        base_s,
        line(0),
        small_s[:points].T,
        line(1),
        line(2),
        query_s,
        line(7)[:cut],
        key_s,
        value_s,
        line(7)[cut:],
        out_s,
        line(3),
        line(4),
        line(5),
        up_s,
        small_s[points + 8 : used].reshape(-1),
        down_s,
        line(6),
    )


def solution(mesh):
    in_specs = (
        P("dp", None, None, None),
        P("dp"),
        P("dp"),
        P("dp"),
        P(),
        P(),
        P(),
        P(),
        P(),
        P(),
        P(),
        P(None, "tensor"),
        P("tensor"),
        P(None, "tensor"),
        P(None, "tensor"),
        P("tensor"),
        P("tensor", None),
        P(),
        P(),
        P(),
        P(None, "tensor"),
        P("tensor"),
        P("tensor", None),
        P(),
        P("dp", None),
    )
    out_specs = (
        P("dp", None),
        P("dp", None, None, None),
        P(),
        P(),
        P(),
        P(),
        P(),
        P(None, "tensor"),
        P("tensor"),
        P(None, "tensor"),
        P(None, "tensor"),
        P("tensor"),
        P("tensor", None),
        P(),
        P(),
        P(),
        P(None, "tensor"),
        P("tensor"),
        P("tensor", None),
        P(),
    )
    return jax.shard_map(local, mesh=mesh, in_specs=in_specs, out_specs=out_specs, check_vma=False)
```

time: 508 us -> 518 us (1.020); the launches traced: 504 us -> 509 us
  Pallas kernels: 377 us -> 322 us
  other arithmetic: 27.5 us -> 56.7 us
  local copies, waits for them, and re-layouts: 41.7 us -> 53.1 us
  waiting for transfers between devices: 10.5 us -> 17.1 us
  between operations: 1.65 us -> 7.25 us
    pallas_call x1, Pallas kernels: 293 us -> 238 us  [sync_grads(): pl.pallas_call(kernel, out_shape=[jax.ShapeDtypeStruct(s, jnp.float32) fo...]
    ppermute x0 -> x4, waiting for transfers between devices: none -> 11.4 us  [the longest x2 11.4 us: from_partner(): direct = lax.ppermute(mine, 'dp', there)]
    select_n x3 -> x12, other arithmetic: 2.37 us -> 13.6 us  [the longest x1 3.85 us: local(): fine_cotangent = jnp.where(is_fine, own_cotangent, other_cotangent)]
    dot_general x1, matrix products: 3.94 us -> 11.8 us  [local(): jnp.dot(normed_two, w_up, preferred_element_type=jnp.float32)]
    dot_general x4, matrix products: 18.5 us -> 12.8 us  [the longest x1 5.4 us: local(): jnp.einsum('tf,td->fd', own_part(activated), grad_branch, preferred_eleme...]
    unnamed x89 -> x160, local copies, waits for them, and re-layouts: 28.4 us -> 31.7 us
  transfers between devices with their start and end apart: 4 -> 8, of which waited for: 3 -> 3; matrix products, arithmetic and copies ran while one was open for 5% -> 16% of each run, Pallas kernels for 0% -> 7%
where the time goes in v3:
time: 518 us; the launch traced here: 509 us
  Pallas kernels  322 us (62%)
  other arithmetic  56.7 us (11%)
  local copies, waits for them, and re-layouts  53.1 us (10%)
  matrix products  47.9 us (9%)
  waiting for transfers between devices  17.1 us (3%)
  between operations  7.25 us (1%)
    pallas_call x1, Pallas kernels, sync_grads(): pl.pallas_call(kernel, out_shape=[jax.ShapeDtypeStruct(s, jnp.float32) fo...  238 us
    unnamed x160, local copies, waits for them, and re-layouts  31.7 us
    pallas_call x1, Pallas kernels, attend_back(): pl.pallas_call(kernel, grid=(heads,), out_shape=jax.ShapeDtypeStruct((row...  25.9 us
    pallas_call x1, Pallas kernels, embed(): pl.pallas_call(embed_kernel, out_shape=[jax.ShapeDtypeStruct((rows, width...  23.7 us
    pallas_call x1, Pallas kernels, pixel_back(): pl.pallas_call(pixel_kernel, out_shape=[jax.ShapeDtypeStruct(shape, jnp.f...  21.1 us
    pallas_call x1, Pallas kernels, attend(): pl.pallas_call(kernel, grid=(heads,), out_shape=jax.ShapeDtypeStruct((row...  13.2 us
    dot_general x1, matrix products, local(): jnp.dot(normed_two, w_up, preferred_element_type=jnp.float32)  11.8 us
    reduce_sum x4, other arithmetic, standardize(): centered = values - jnp.mean(values, axis=-1, keepdims=True)  11.6 us
  transfers between devices with their start and end apart: 8, of which 3 were waited for; matrix products, arithmetic and copies ran while one was open for 16% of the time, Pallas kernels for 7%

profile of v3, /device:TPU:0, one launch (start us, length us, event | category | flops | bytes accessed | tf_op | source)
XLA Modules:
  0.0 508.6 jit_solution(17546539561611035700)
XLA Ops:
  6.0 2.9 collective-permute-start
  8.9 3.4 convert_element_type.123
  15.1 11.4 %collective-permute-done = f32[3,240,256]{2,1,0:T(8,128)} collective-permute-done((f32[3,240,256]{2,1,0:T(8,128)}, f32[3,240,256]{2,1,0:T(8,128)}, u32[]{:S(2)}, u32[]{:S(2)}) %collective-permute-start) | collective-permute-done | bytes 737312 | tf_op jit(solution)/shard_map/ppermute | solution.py:797
  44.8 3.7 pad_maximum_fusion.pix
  48.6 23.7 %embed.1 = (f32[1232,768]{1,0:T(8,128)}, bf16[3,104,3072]{2,1,0:T(8,128)(2,1)S(1)}, bf16[3,912,64]{2,1,0:T(8,128)(2,1)S(1)}, bf16[3,64,768]{2,1,0:T(8,128)(2,1)S(1)}) custom-call(s32[4]{0:T(128)S(1)} %get-tuple-element.86.sizes, s32[4]{0:T(128)S(1)} %get-tuple-element.87.order, f32[4,3,240,256]{3,2,1,0:T(8,128)} %pad_maximum_fusion.pix, ...), custom_call_target="tpu_custom_call" | custom-call | tf_op jit(solution)/shard_map/embed/pallas_call | solution.py:159
  90.0 13.2 %attend.1 = bf16[1232,384]{1,0:T(8,128)(2,1)S(1)} custom-call(bf16[1232,1152]{1,0:T(8,128)(2,1)S(1)} %fusion.7.query.key.value, bf16[1232,1152]{1,0:T(8,128)(2,1)S(1)} %fusion.7.query.key.value, bf16[1232,1152]{1,0:T(8,128)(2,1)S(1)} %fusion.7.query.key.value, s32[1232,1]{1,0:T(8,128)S(1)} %and_select_fusion.segment, s32[1,320]{1,0:T(1,128)S(1)} %broadcast_in_dim.205.segment_row), custom_call_target="tpu_custom_call" | custom-call | tf_op jit(solution)/shard_map/attend/pallas_call | solution.py:334
  103.3 3.0 fusion.58
  109.6 3.9 broadcast_select_fusion
  116.6 5.5 %fusion.60 = f32[1232,1536]{1,0:T(8,128)} fusion(bf16[1232,768]{1,0:T(8,128)(2,1)S(1)} %get-tuple-element.68, bf16[1536,768]{1,0:T(8,128)(2,1)S(1)} %copy-done.66), kind=kOutput, calls=%fused_computation.163 | convolution fusion | flops 2906652672 | bytes 11821056 | tf_op jit(solution)/shard_map/td,fd->tf/dot_general | solution.py:973
  122.2 3.8 fusion.54
  127.3 11.8 %convert_reduce_fusion = (f32[1536]{0:T(1024)}, bf16[1232,1536]{1,0:T(8,128)(2,1)S(1)}, bf16[1232,1536]{1,0:T(8,128)(2,1)S(1)}) fusion(f32[1232,1536]{1,0:T(8,128)} %fusion.60, f32[1536]{0:T(1024)S(1)} %convert_element_type.119, bf16[1232,768]{1,0:T(8,128)(2,1)S(1)} %add_convert_fusion.1, bf16[768,1536]{1,0:T(8,128)(2,1)S(1)} %copy-done), kind=kOutput, calls=%fused_computation.14 | convolution fusion | flops 2953959936 | bytes 19402752 | tf_op jit(solution)/shard_map/dot_general | solution.py:936
  139.0 3.1 fusion.61
  142.7 3.1 fusion.59
  146.0 3.0 collective-permute-done.6
  154.3 3.7 fusion.53
  160.5 25.9 %attend_back.1 = bf16[1232,1152]{1,0:T(8,128)(2,1)S(1)} custom-call(bf16[1232,1152]{1,0:T(8,128)(2,1)} %copy-done.2, bf16[1232,1152]{1,0:T(8,128)(2,1)} %copy-done.2, bf16[1232,1152]{1,0:T(8,128)(2,1)} %copy-done.2, bf16[1232,384]{1,0:T(8,128)(2,1)S(1)} %convolution_convert_fusion.grad_mixed, s32[1232,1]{1,0:T(8,128)S(1)} %and_select_fusion.segment, ...), custom_call_target="tpu_custom_call" | custom-call | tf_op jit(solution)/shard_map/attend_back/pallas_call | solution.py:391
  186.4 4.5 fusion.62
  195.3 5.4 %fusion.9.refs_0_ = f32[768,768]{1,0:T(8,128)} fusion(bf16[1232,768]{1,0:T(8,128)(2,1)} %copy-done.29, bf16[1232,1536]{1,0:T(8,128)(2,1)} %copy-done.70, s32[]{:T(128)S(6)} %select_n.356), kind=kOutput, calls=%fused_computation.41 | convolution fusion | flops 1453326336 | bytes 6144004 | tf_op jit(solution)/shard_map/tf,td->fd/dot_general | solution.py:970
  200.8 3.2 fusion.16.refs_1_
  207.9 2.9 fusion.13
  213.6 4.3 multiply_reduce_fusion.1
  222.6 21.1 %pixel_back.1 = (f32[2,3,240,240]{3,2,1,0:T(8,128)}, f32[384,1536]{1,0:T(8,128)S(1)}, f32[49,768]{1,0:T(8,128)S(1)}) custom-call(s32[4]{0:T(128)S(1)} %copy-done.17, s32[3]{0:T(128)S(1)} %pad_add_fusion.1.place, f32[1232,768]{1,0:T(8,128)} %get-tuple-element.72.grad, bf16[4,48,32]{2,1,0:T(8,128)(2,1)S(1)} %copy-done.13, bf16[900,49]{1,0:T(8,128)(2,1)S(1)} %bitcast.46, ...), custom_call_target="tpu_custom_call" | custom-call | tf_op jit(solution)/shard_map/pixel_back/pallas_call | solution.py:277
  245.9 238.1 %sync_grads.1 = (f32[768,3072]{1,0:T(8,128)}, f32[1536,768]{1,0:T(8,128)}, f32[768,1536]{1,0:T(8,128)}, f32[768,384]{1,0:T(8,128)}, f32[768,384]{1,0:T(8,128)}, ...) custom-call(f32[768,768]{1,0:T(8,128)} %fusion.9.refs_0_, f32[384,1536]{1,0:T(8,128)} %fusion.16.refs_1_, ...), custom_call_target="tpu_custom_call" | custom-call | tf_op jit(solution)/shard_map/sync_grads/pallas_call | solution.py:772
  489.9 8.8 %copy.70 = f32[768,3072]{1,0:T(8,128)} copy(f32[768,3072]{1,0:T(8,128)} %get-tuple-element.127) | data formatting | bytes 18874368
  (275 shorter events, 88.1 us)
Async XLA Ops:
  0.7 126.6 %copy-start = (bf16[768,1536]{1,0:T(8,128)(2,1)S(1)}, bf16[768,1536]{1,0:T(8,128)(2,1)}, u32[]{:S(2)}) copy-start(bf16[768,1536]{1,0:T(8,128)(2,1)} %param.47) | copy-start | bytes 7077892
  6.0 20.6 %collective-permute-start = (f32[3,240,256]{2,1,0:T(8,128)}, f32[3,240,256]{2,1,0:T(8,128)}, u32[]{:S(2)}, u32[]{:S(2)}) collective-permute-start(f32[3,240,256]{2,1,0:T(8,128)} %dynamic-slice_bitcast_fusion), channel_id=1, source_target_pairs={{0,2},{2,0},{4,6},{6,4},{8,10},{10,8},{12,14},{14,12},{16,18},{18,... | collective-permute-start | bytes 2211848 | tf_op jit(solution)/shard_map/ppermute | solution.py:797
  8.9 19.1 %copy-start.60 = (bf16[768]{0:T(1024)(128)(2,1)S(1)}, bf16[768]{0:T(1024)(128)(2,1)}, u32[]{:S(2)}) copy-start(bf16[768]{0:T(1024)(128)(2,1)} %param.34) | copy-start | bytes 4612
  8.9 19.1 %copy-start.54 = (bf16[768]{0:T(1024)(128)(2,1)S(1)}, bf16[768]{0:T(1024)(128)(2,1)}, u32[]{:S(2)}) copy-start(bf16[768]{0:T(1024)(128)(2,1)} %param.36) | copy-start | bytes 4612
  8.9 19.1 %copy-start.55 = (bf16[768]{0:T(1024)(128)(2,1)S(1)}, bf16[768]{0:T(1024)(128)(2,1)}, u32[]{:S(2)}) copy-start(bf16[768]{0:T(1024)(128)(2,1)} %param.37) | copy-start | bytes 4612
  8.9 19.1 %copy-start.43 = (bf16[768,49]{0,1:T(8,128)(2,1)S(1)}, bf16[768,49]{0,1:T(8,128)(2,1)}, u32[]{:S(2)}) copy-start(bf16[768,49]{0,1:T(8,128)(2,1)} %param.35) | copy-start | bytes 225796
  12.3 18.8 %slice-start.2 = ((bf16[31,900,49]{1,0,2:T(8,128)(2,1)}), bf16[31,100,49]{1,0,2:T(8,128)(2,1)S(1)}, s32[]{:S(2)}) async-start(bf16[31,900,49]{1,0,2:T(8,128)(2,1)} %param.32), calls=%async_computation.2 | async-start | bytes 802816 | tf_op jit(solution)/shard_map/slice | solution.py:905
  12.3 19.8 %copy-start.62 = (bf16[384]{0:T(512)(128)(2,1)S(1)}, bf16[384]{0:T(512)(128)(2,1)}, u32[]{:S(2)}) copy-start(bf16[384]{0:T(512)(128)(2,1)} %param.42) | copy-start | bytes 2308
  12.3 19.8 %copy-start.63 = (bf16[384]{0:T(512)(128)(2,1)S(1)}, bf16[384]{0:T(512)(128)(2,1)}, u32[]{:S(2)}) copy-start(bf16[384]{0:T(512)(128)(2,1)} %param.39) | copy-start | bytes 2308
  15.0 71.6 %collective-permute-start.4 = (f32[512,768]{1,0:T(8,128)}, f32[512,768]{1,0:T(8,128)}, u32[]{:S(2)}, u32[]{:S(2)}) collective-permute-start(f32[512,768]{1,0:T(8,128)} %constant_dynamic-slice_fusion), channel_id=1, source_target_pairs={{0,2},{2,0},{4,6},{6,4},{8,10},{10,8},{12,14},{14,12},{16,18},{18,... | collective-permute-start | bytes 4718600 | tf_op jit(solution)/shard_map/ppermute | solution.py:797
  26.5 10.3 %collective-permute-start.1 = (f32[3,240,256]{2,1,0:T(8,128)}, f32[3,240,256]{2,1,0:T(8,128)}, u32[]{:S(2)}, u32[]{:S(2)}) collective-permute-start(f32[3,240,256]{2,1,0:T(8,128)} %collective-permute-done), channel_id=1, source_target_pairs={{0,1},{1,0},{2,3},{3,2},{4,5},{5,4},{6,7},{7,6},{8,9},{9,8},{10,11... | collective-permute-start | bytes 2211848 | tf_op jit(solution)/shard_map/ppermute | solution.py:798
  28.0 55.0 %copy-start.46 = (f32[768]{0:T(1024)}, f32[768]{0:T(1024)S(1)}, u32[]{:S(2)}) copy-start(f32[768]{0:T(1024)S(1)} %convert_element_type.110) | copy-start | bytes 9220
  28.5 20.1 %copy-start.6 = (bf16[1,900,49]{2,1,0:T(8,128)(2,1)}, bf16[1,900,49]{2,1,0:T(8,128)(2,1)S(1)}, u32[]{:S(2)}) copy-start(bf16[1,900,49]{2,1,0:T(8,128)(2,1)S(1)} %copy.55) | copy-start | bytes 264604
  40.4 31.9 %copy-start.16 = (s32[4]{0:T(128)}, s32[4]{0:T(128)S(1)}, u32[]{:S(2)}) copy-start(s32[4]{0:T(128)S(1)} %get-tuple-element.86.sizes) | copy-start | bytes 52
  48.5 23.8 %copy-start.12 = (bf16[4,48,32]{2,1,0:T(8,128)(2,1)}, bf16[4,48,32]{2,1,0:T(8,128)(2,1)S(1)}, u32[]{:S(2)}) copy-start(bf16[4,48,32]{2,1,0:T(8,128)(2,1)S(1)} %broadcast_select_fusion.2.table) | copy-start | bytes 36868
  86.7 16.6 %copy-start.2 = (bf16[1232,1152]{1,0:T(8,128)(2,1)}, bf16[1232,1152]{1,0:T(8,128)(2,1)S(1)}, u32[]{:S(2)}) copy-start(bf16[1232,1152]{1,0:T(8,128)(2,1)S(1)} %fusion.7.query.key.value) | copy-start | bytes 8515588
  86.7 22.9 %collective-permute-start.5 = (f32[512,768]{1,0:T(8,128)}, f32[512,768]{1,0:T(8,128)}, u32[]{:S(2)}, u32[]{:S(2)}) collective-permute-start(f32[512,768]{1,0:T(8,128)} %collective-permute-done.4), channel_id=1, source_target_pairs={{0,1},{1,0},{2,3},{3,2},{4,5},{5,4},{6,7},{7,6},{8,9},{9,8},{10,11... | collective-permute-start | bytes 4718600 | tf_op jit(solution)/shard_map/ppermute | solution.py:798
  90.0 13.2 %copy-start.25 = (bf16[384,768]{1,0:T(8,128)(2,1)S(1)}, bf16[384,768]{1,0:T(8,128)(2,1)}, u32[]{:S(2)}) copy-start(bf16[384,768]{1,0:T(8,128)(2,1)} %param.43) | copy-start | bytes 1769476
  106.3 15.8 %collective-permute-start.2 = (f32[1232,768]{1,0:T(8,128)}, f32[1232,768]{1,0:T(8,128)}, u32[]{:S(2)}, u32[]{:S(2)}) collective-permute-start(f32[1232,768]{1,0:T(8,128)} %fusion.58), channel_id=1, source_target_pairs={{0,1},{1,0},{2,3},{3,2},{4,5},{5,4},{6,7},{7,6},{8,9},{9,8},{10,11... | collective-permute-start | bytes 11354120 | tf_op jit(solution)/shard_map/ppermute | solution.py:792
  142.2 6.8 %collective-permute-start.6 = (f32[1232,768]{1,0:T(8,128)S(1)}, f32[1232,768]{1,0:T(8,128)S(1)}, u32[]{:S(2)}, u32[]{:S(2)}) collective-permute-start(f32[1232,768]{1,0:T(8,128)S(1)} %fusion.61), channel_id=1, source_target_pairs={{0,1},{1,0},{2,3},{3,2},{4,5},{5,4},{6,7},{7,6},{8,9},{9,8},{10,11... | collective-permute-start | bytes 11354120 | tf_op jit(solution)/shard_map/ppermute | solution.py:792
  145.9 8.5 %collective-permute-start.3 = (f32[1232,768]{1,0:T(8,128)S(1)}, f32[1232,768]{1,0:T(8,128)S(1)}, u32[]{:S(2)}, u32[]{:S(2)}) collective-permute-start(f32[1232,768]{1,0:T(8,128)S(1)} %fusion.59), channel_id=1, source_target_pairs={{0,1},{1,0},{2,3},{3,2},{4,5},{5,4},{6,7},{7,6},{8,9},{9,8},{10,11... | collective-permute-start | bytes 11354120 | tf_op jit(solution)/shard_map/ppermute | solution.py:792
  159.3 27.1 %copy-start.21 = (f32[1232,768]{1,0:T(8,128)}, f32[1232,768]{1,0:T(8,128)S(1)}, u32[]{:S(2)}) copy-start(f32[1232,768]{1,0:T(8,128)S(1)} %get-tuple-element.70) | copy-start | bytes 11354116
  160.5 25.9 %copy-start.40 = (bf16[768,1152]{1,0:T(8,128)(2,1)S(1)}, bf16[768,1152]{1,0:T(8,128)(2,1)}, u32[]{:S(2)}) copy-start(bf16[768,1152]{1,0:T(8,128)(2,1)} %copy-done.38) | copy-start | bytes 5308420
  191.0 22.6 %collective-permute-start.7 = (f32[1232,768]{1,0:T(8,128)}, f32[1232,768]{1,0:T(8,128)}, u32[]{:S(2)}, u32[]{:S(2)}) collective-permute-start(f32[1232,768]{1,0:T(8,128)} %fusion.62), channel_id=1, source_target_pairs={{0,1},{1,0},{2,3},{3,2},{4,5},{5,4},{6,7},{7,6},{8,9},{9,8},{10,11... | collective-permute-start | bytes 11354120 | tf_op jit(solution)/shard_map/ppermute | solution.py:792
  (58 other events, 228.5 us)

commit v4 on v3

--- a/solution.py
+++ b/solution.py
@@ -102,6 +102,7 @@
     tokens,
     patches,
     mixed_weight,
+    fine_pairs,
     line,
     pair,
     long,
@@ -114,16 +115,17 @@
     stride = tokens.shape[1]
     low = jnp.bfloat16
     emb[...] = jnp.broadcast_to(bias[...], emb.shape)
+    tokens[...] = jnp.zeros_like(tokens)
 
     fill_pairs(pair, long, table[0], FINE)
-    fine_pairs = pair[: FINE * FINE, :].astype(low)
+    fine_pairs[...] = pair[: FINE * FINE, :].astype(low)
     emb[:count, :] += nt(pos_fine[...], pos_base[...])
 
     @functools.partial(loop, channels, unroll=True)
     def _(c):
         columns = pl.ds(c * area, area)
         patch = cut_patches(line, pix, order[0], c, FINE, grid, res)
-        mixed = nt(fine_pairs, weight[:, columns]).astype(low)
+        mixed = nt(fine_pairs[...], weight[:, columns]).astype(low)
         mixed_weight[c] = mixed
         patches[c, :count, :] = patch
         emb[:count, :] += nn(patch, mixed)
@@ -163,9 +165,10 @@
             jax.ShapeDtypeStruct((3, up_to(pos.shape[1], 8), features), jnp.bfloat16),
             jax.ShapeDtypeStruct((channels, up_to(fine, 16), FINE * FINE), jnp.bfloat16),
             jax.ShapeDtypeStruct((channels, FINE * FINE, width), jnp.bfloat16),
+            jax.ShapeDtypeStruct((FINE * FINE, area), jnp.bfloat16),
         ],
         in_specs=[SMEM] * 2 + [VMEM] * 7,
-        out_specs=[VMEM] * 4,
+        out_specs=[VMEM] * 5,
         scratch_shapes=[
             pltpu.VMEM((res * res // FINE, 128), jnp.float32),
             pltpu.VMEM((side * side, area), jnp.float32),
@@ -186,111 +189,60 @@
     )
 
 
-def pixel_kernel(
-    sizes,
-    place,
-    grad,
-    table,
-    pos_fine,
-    pos,
-    weight,
-    tokens,
-    patches,
-    mixed_weight,
-    pixel_grad,
-    grad_weight,
-    grad_pos,
-    line,
-    pair,
-    long,
-):
+def pixel_kernel(sizes, is_fine, grad, table, weight, mixed_weight, pixel_grad, line, pair, long):
     area = table.shape[2] ** 2
     channels, res = pixel_grad.shape[1:3]
-    half = grad_weight.shape[0]
-    part = grad_weight.shape[1] // channels
-    core_columns = pl.ds(pl.multiple_of(place[0] * half, 128), half)
-    side_start = place[1] * part
-    is_fine = place[2]
-    grid = res // FINE
-    count = grid * grid
-    start = up_to(count, 16)
-    stride = tokens.shape[1]
+    start = up_to((res // FINE) ** 2, 16)
+    stride = up_to((res // COARSE[0]) ** 2, 8)
     low = jnp.bfloat16
 
-    fill_pairs(pair, long, table[0], FINE)
-    some_pairs = pair[: FINE * FINE, pl.ds(pl.multiple_of(side_start, 128), part)].astype(low)
-    rows = grad[:count, :].astype(low)
-    some = grad[:count, core_columns].astype(low)
-    grad_pos[...] = tn(pos_fine[...], rows)
-
-    @pl.loop(0, channels)
-    def _(c):
-        gathered = tn(patches[c, :count, :], some).astype(low)
-        grad_weight[:, pl.ds(pl.multiple_of(c * part, 128), part)] = tn(gathered, some_pairs)
-
-        @pl.when(is_fine == 1)
-        def _():
+    @pl.when(is_fine[0] == 1)
+    def _():
+        grid = res // FINE
+        count = grid * grid
+        for c in range(channels):
             patch = nt(grad[:count, :].astype(low), mixed_weight[c])
             place_patches(line, pixel_grad, 0, c, patch, FINE, grid, res)
 
     @pl.loop(1, 4)
     def _(slot):
         row = pl.multiple_of(start + (slot - 1) * stride, 8)
-        wanted = jnp.where(slot == 1, is_fine, 1 - is_fine)
+        wanted = jnp.where(slot == 1, is_fine[0], 1 - is_fine[0])
         image = jnp.where(slot == 1, 1, slot - 2)
         for side in COARSE:
             grid = res // side
             count = grid * grid
 
-            @pl.when(sizes[slot] == side)
+            @pl.when((sizes[slot] == side) & (wanted == 1))
             def _():
-                here = pl.ds(row, count)
-                rows = grad[here, :].astype(low)
-                some = grad[here, core_columns].astype(low)
-                grad_pos[...] += tn(pos[slot - 1, :count, :], rows)
+                fill_pairs(pair, long, table[slot], side)
+                rows = grad[pl.ds(row, count), :].astype(low)
 
                 @pl.loop(0, channels)
                 def _(c):
-                    columns = pl.ds(pl.multiple_of(c * area + side_start, 128), part)
-                    grad_weight[:, pl.ds(pl.multiple_of(c * part, 128), part)] += tn(
-                        some, tokens[slot - 1, :count, columns]
-                    )
-
-                @pl.when(wanted == 1)
-                def _():
-                    fill_pairs(pair, long, table[slot], side)
-
-                    @pl.loop(0, channels)
-                    def _(c):
-                        columns = pl.ds(pl.multiple_of(c * area, area), area)
-                        token = nn(grad[here, :].astype(low), weight[:, columns]).astype(low)
-                        patch = nt(token, pair[: side * side, :].astype(low))
-                        place_patches(line, pixel_grad, image, c, patch, side, grid, res)
-
-
-def pixel_back(
-    sizes, place, grad, table, pos_fine, pos, w_base, tokens, patches, mixed_weight, shape
-):
+                    columns = pl.ds(pl.multiple_of(c * area, area), area)
+                    token = nn(rows, weight[:, columns]).astype(low)
+                    patch = nt(token, pair[: side * side, :].astype(low))
+                    place_patches(line, pixel_grad, image, c, patch, side, grid, res)
+
+
+def pixel_back(sizes, is_fine, grad, table, w_base, mixed_weight, shape):
     _, channels, res, _ = shape
     width, features = w_base.shape
     side = table.shape[1]
     return pl.pallas_call(
         pixel_kernel,
-        out_shape=[
-            jax.ShapeDtypeStruct(shape, jnp.float32),
-            jax.ShapeDtypeStruct((width // 2, features // 2), jnp.float32),
-            jax.ShapeDtypeStruct((pos.shape[2], width), jnp.float32),
-        ],
-        in_specs=[SMEM] * 2 + [VMEM] * 8,
-        out_specs=[VMEM] * 3,
+        out_shape=jax.ShapeDtypeStruct(shape, jnp.float32),
+        in_specs=[SMEM] * 2 + [VMEM] * 4,
+        out_specs=VMEM,
         scratch_shapes=[
             pltpu.VMEM((res * res // FINE, 128), jnp.float32),
             pltpu.VMEM((side * side, features // channels), jnp.float32),
             pltpu.VMEM((side, features // channels), jnp.float32),
         ],
-        compiler_params=pltpu.CompilerParams(vmem_limit_bytes=48 << 20),
+        compiler_params=pltpu.CompilerParams(vmem_limit_bytes=40 << 20),
         name="pixel_back",
-    )(sizes, place, grad, table, pos_fine, pos, w_base, tokens, patches, mixed_weight)
+    )(sizes, is_fine, grad, table, w_base, mixed_weight)
 
 
 PAIR = 2 * HD
@@ -364,46 +316,7 @@
         grad_key = grad_key + nn(grad_scores, own)
         grad_query.append(tn(grad_scores, key))
     grad_query = jnp.where(halves[0], grad_query[0], grad_query[1])
-    low = lambda value: value.astype(jnp.bfloat16)
-    return low(grad_query * scale), low(grad_key * scale), low(grad_value)
-
-
-def attend_back_kernel(
-    scale, fine, start, query, key, value, grad_mixed, segment, segment_row, grad_qkv
-):
-    rows = query.shape[0]
-    third = grad_qkv.shape[1] // 3
-    column = pl.multiple_of(pl.program_id(0) * PAIR, PAIR)
-    masks = block_masks(fine, start, rows, segment, segment_row, 0)
-    for here, mask in zip((slice(0, start), slice(start, rows)), masks):
-        grads = attend_back_block(
-            scale, query[here, :], key[here, :], value[here, :], grad_mixed[here, :], mask
-        )
-        for k in range(3):
-            grad_qkv[here, pl.ds(k * third + column, PAIR)] = grads[k]
-
-
-def attend_back(qkv, grad_mixed, segment, fine, start):
-    rows, width = qkv.shape
-    heads = width // 3 // PAIR
-    kernel = functools.partial(attend_back_kernel, 1.0 / math.sqrt(HD), fine, start)
-    column = lambda k: pl.BlockSpec((rows, PAIR), lambda j: (0, k * heads + j))
-    return pl.pallas_call(
-        kernel,
-        grid=(heads,),
-        out_shape=jax.ShapeDtypeStruct((rows, width), jnp.bfloat16),
-        in_specs=[
-            column(0),
-            column(1),
-            column(2),
-            column(0),
-            pl.BlockSpec((rows, 1), lambda j: (0, 0)),
-            pl.BlockSpec((1, rows - start), lambda j: (0, 0)),
-        ],
-        out_specs=pl.BlockSpec((rows, width), lambda j: (0, 0)),
-        compiler_params=pltpu.CompilerParams(vmem_limit_bytes=48 << 20),
-        name="attend_back",
-    )(qkv, qkv, qkv, grad_mixed, segment[:, None], segment[None, start:])
+    return grad_query * scale, grad_key * scale, grad_value
 
 
 LINE = 4
@@ -421,10 +334,7 @@
         self.swap, self.cross = swap, cross
 
 
-def sync_kernel(pieces, scale, in_count, out_count, *refs):
-    grads = refs[:in_count]
-    outs = refs[in_count : in_count + out_count]
-    acc, land, land_right, land_left, sems = refs[in_count + out_count :]
+def move_pieces(pieces, scale, grads, outs, acc, land, land_right, land_left, sems, prepare):
     device = lax.axis_index("dp")
     core = lax.axis_index("tensor")
     place_x = lax.rem(device, 2)
@@ -452,9 +362,6 @@
     inner = (place_z + LINE - 1) // LINE + (2 * (LINE - 1) - place_z) // LINE
     pl.semaphore_wait(barrier, 3 + inner)
 
-    def rows_at(ref, start, size, column, width):
-        return ref.at[pl.ds(pl.multiple_of(start, 8), size), pl.ds(pl.multiple_of(column, 128), width)]
-
     def remote(src, dst, send, recv, where):
         return pltpu.make_async_remote_copy(
             src_ref=src,
@@ -465,6 +372,11 @@
             device_id_type=MESH_ID,
         )
 
+    work = prepare(core, place_x, sibling, remote)
+
+    def rows_at(ref, start, size, column, width):
+        return ref.at[pl.ds(pl.multiple_of(start, 8), size), pl.ds(pl.multiple_of(column, 128), width)]
+
     def add_rows(total, start, extra, size, width, factor=None):
         step = 24 if size % 24 == 0 else 8
 
@@ -486,7 +398,7 @@
 
         def y_copy():
             return remote(
-                rows_at(grad, piece.row + (1 - place_y) * half, half, piece.col, width),
+                rows_at(grad, piece.row(place_x) + (1 - place_y) * half, half, piece.col, width),
                 land.at[number, :half, :width],
                 sem(0),
                 sem(1),
@@ -495,7 +407,7 @@
 
         def load():
             return pltpu.make_async_copy(
-                rows_at(grad, piece.row + place_y * half, half, piece.col, width),
+                rows_at(grad, piece.row(place_x) + place_y * half, half, piece.col, width),
                 mine.at[:half, :width],
                 sem(2),
             )
@@ -724,6 +636,8 @@
         if tick + AHEAD < len(groups):
             for line in groups[tick + AHEAD]:
                 line[0]()
+        for job in work.pop(0) if work else ():
+            job()
         active = range(max(0, tick - depth + 1), min(tick, len(groups)))
         for j in [j for j in active if tick - j < late] + [j for j in active if tick - j >= late]:
             for line in groups[j]:
@@ -736,24 +650,25 @@
 
 def sync_plan(grads, outs):
     pieces = []
-    for source, (rows, cols) in enumerate(grads):
+    for source, (rows, cols, step_x) in enumerate(grads):
         start = 0
-        for target, width, row_x, row_core, col_x, block in outs[source]:
+        for target, width, row_x, row_core, col_x, out_start in outs[source]:
             tall = min(PIECE_ROWS, rows)
-            wide = min(PIECE_COLS, width) if block is None else width
+            wide = min(PIECE_COLS, width)
+            if width % wide:
+                wide = width // 2
             for row in range(0, rows, tall):
-                for col in range(0, width, wide) if block is None else range(1):
-                    out_col = col if block is None else block
+                for col in range(0, width, wide):
                     pieces.append(
                         Piece(
                             source,
-                            row,
+                            lambda x, row=row, a=step_x: row + x * a,
                             start + col,
                             tall,
                             wide,
                             target,
                             lambda x, core, row=row, a=row_x, b=row_core: row + x * a + core * b,
-                            lambda x, c=out_col, a=col_x: c + x * a,
+                            lambda x, c=out_start + col, a=col_x: c + x * a,
                             row_core != 0,
                             len(pieces) % CROSS_EVERY == CROSS_EVERY - 1,
                         )
@@ -762,30 +677,296 @@
     return pieces
 
 
-def sync_grads(grads, out_shapes, outs, replicas):
-    pieces = sync_plan([g.shape for g in grads], outs)
+QUERY_BLOCK = 384
+LN_ROWS = 112
+POINT_ROWS = 64
+
+
+def back_kernel(pieces, sizes, fine, start, points, counts, *refs):
+    replicas, given = counts
+    (
+        qkv,
+        grad_mixed,
+        segment,
+        segment_row,
+        normed_part,
+        w_qkv,
+        standard,
+        inverse,
+        grad_middle,
+        gain,
+        tokens,
+        patches,
+        fine_pairs,
+        pos_fine,
+        pos,
+        rest,
+    ) = refs[:16]
+    early = refs[16 : 16 + given]
+    refs = refs[16 + given :]
+    outs, grad_embedded, refs = refs[:sizes], refs[sizes], refs[sizes + 1 :]
+    (
+        grad_qkv,
+        grad_key,
+        grad_value,
+        partial,
+        arrived,
+        grad_w_qkv,
+        grad_w_base,
+        bundle,
+        acc,
+        land,
+        land_right,
+        land_left,
+        sems,
+        swap_sems,
+        chunk_standard,
+        chunk_middle,
+        chunk_sems,
+    ) = refs
+    rows, width = standard.shape
+    third = qkv.shape[1] // 3
+    scale = 1.0 / math.sqrt(HD)
+    low = lambda value: value.astype(jnp.bfloat16)
+    blocks = range(0, rows, LN_ROWS)
+
+    def prepare(core, place_x, sibling, remote):
+        def back_rows(pair, here, keys, mask):
+            column = lambda k: slice(k * third + pair * PAIR, k * third + (pair + 1) * PAIR)
+            return attend_back_block(
+                scale,
+                qkv[here, column(0)],
+                qkv[keys, column(1)],
+                qkv[keys, column(2)],
+                grad_mixed[here, column(0)],
+                mask,
+            )
+
+        def store_qkv(pair, k, here, value):
+            grad_qkv[here, k * third + pair * PAIR : k * third + (pair + 1) * PAIR] = low(value)
+
+        def fine_job(pair, begin):
+            def job():
+                here = slice(begin, min(begin + QUERY_BLOCK, start))
+                keys = slice(0, start)
+                inside = lax.broadcasted_iota(jnp.int32, (start, here.stop - begin), 0) < fine
+                grad_q, grad_k, grad_v = back_rows(pair, here, keys, inside)
+                store_qkv(pair, 0, here, grad_q)
+                if begin == 0:
+                    grad_key[...] = grad_k
+                    grad_value[...] = grad_v
+                else:
+                    grad_key[...] += grad_k
+                    grad_value[...] += grad_v
+                if here.stop == start:
+                    store_qkv(pair, 1, keys, grad_key[...])
+                    store_qkv(pair, 2, keys, grad_value[...])
+
+            return job
+
+        def coarse_job(pair):
+            def job():
+                here = slice(start, rows)
+                same = segment[here, :] == segment_row[...]
+                for k, value in enumerate(back_rows(pair, here, here, same)):
+                    store_qkv(pair, k, here, value)
+
+            return job
+
+        def weight_job():
+            grad_w_qkv[...] = tn(normed_part[...], grad_qkv[...])
+
+        def partial_job():
+            partial[...] = nt(grad_qkv[...], w_qkv[...])
+            swap().start()
+
+        def swap():
+            return remote(partial, arrived, swap_sems.at[0], swap_sems.at[1], sibling)
+
+        def chunk_copies(number):
+            here = pl.ds(pl.multiple_of(number * LN_ROWS, 8), LN_ROWS)
+            at = lax.rem(number, 2)
+            return [
+                pltpu.make_async_copy(standard.at[here], chunk_standard.at[at], chunk_sems.at[0, at]),
+                pltpu.make_async_copy(
+                    grad_middle.at[here], chunk_middle.at[at], chunk_sems.at[1, at]
+                ),
+            ]
+
+        def norm_job():
+            swap().wait()
+            for copy in chunk_copies(0):
+                copy.start()
+            for k in range(3):
+                bundle[points + k : points + k + 1, :] = jnp.zeros((1, width), jnp.float32)
+
+            @pl.loop(0, len(blocks))
+            def _(number):
+                @pl.when(number + 1 < len(blocks))
+                def _():
+                    for copy in chunk_copies(number + 1):
+                        copy.start()
+
+                for copy in chunk_copies(number):
+                    copy.wait()
+                at = lax.rem(number, 2)
+
+                @pl.loop(0, LN_ROWS // 16)
+                def _(i):
+                    inner = pl.ds(pl.multiple_of(i * 16, 8), 16)
+                    here = pl.ds(pl.multiple_of(number * LN_ROWS + i * 16, 8), 16)
+                    grad = partial[here, :] + arrived[here, :]
+                    z = chunk_standard[at, inner, :]
+                    up = grad * gain[...]
+                    mean = jnp.mean(up, axis=1, keepdims=True)
+                    along = jnp.mean(up * z, axis=1, keepdims=True)
+                    value = (
+                        chunk_middle[at, inner, :] + (up - mean - z * along) * inverse[here, :]
+                    )
+                    grad_embedded[here, :] = value
+                    column = lambda v: jnp.sum(v, axis=0, keepdims=True)
+                    bundle[points : points + 1, :] += column(low(value).astype(jnp.float32))
+                    bundle[points + 1 : points + 2, :] += column(grad * z)
+                    bundle[points + 2 : points + 3, :] += column(grad)
+
+        def base_job():
+            half = grad_w_base.shape[0]
+            channels = patches.shape[0]
+            part = grad_w_base.shape[1] // channels
+            area = 2 * part
+            columns = pl.ds(pl.multiple_of(core * half, 128), half)
+            stride = tokens.shape[1]
+            some = low(grad_embedded[:fine, columns])
+            wanted = fine_pairs[:, pl.ds(pl.multiple_of(place_x * part, 128), part)]
+            for c in range(channels):
+                gathered = low(tn(patches[c, :fine, :], some))
+                total = tn(gathered, wanted)
+                for k in range(3):
+                    begin = start + k * stride
+                    here = pl.ds(pl.multiple_of(c * area + place_x * part, 128), part)
+                    total += tn(low(grad_embedded[begin : begin + stride, columns]), tokens[k, :, here])
+                grad_w_base[:, c * part : (c + 1) * part] = total
+
+        def bundle_job():
+            gathered = tn(pos_fine[...], low(grad_embedded[:fine, :]))
+            count = pos.shape[1]
+            for k in range(3):
+                begin = start + k * tokens.shape[1]
+                gathered += tn(pos[k], low(grad_embedded[begin : begin + count, :]))
+            bundle[:points, :] = gathered
+            bundle[points + 3 : 2 * POINT_ROWS, :] = rest[points + 3 : 2 * POINT_ROWS, :]
+            sums = jnp.sum(grad_qkv[...].astype(jnp.float32), axis=0, keepdims=True)
+            bundle[points + 7 : points + 8, :third] = sums[:, :third]
+            bundle[points + 7 : points + 8, third : 2 * third] = sums[:, 2 * third :]
+
+        jobs = []
+        for pair in range(third // PAIR):
+            jobs += [[fine_job(pair, begin)] for begin in range(0, start, QUERY_BLOCK)]
+            jobs[-1].append(coarse_job(pair))
+        return jobs + [[partial_job], [weight_job], [norm_job], [base_job], [bundle_job]]
+
+    move_pieces(
+        pieces,
+        1.0 / replicas,
+        list(early) + [grad_w_qkv, grad_w_base, bundle],
+        outs,
+        acc,
+        land,
+        land_right,
+        land_left,
+        sems,
+        prepare,
+    )
+
+
+def back_and_sync(
+    qkv,
+    grad_mixed,
+    segment,
+    normed_part,
+    w_qkv,
+    standard,
+    inverse,
+    grad_middle,
+    gain,
+    tokens,
+    patches,
+    fine_pairs,
+    pos_fine,
+    pos,
+    rest,
+    early,
+    out_shapes,
+    grads,
+    outs,
+    fine,
+    start,
+    replicas,
+):
+    rows, width = standard.shape
+    channels = patches.shape[0]
+    pieces = sync_plan(grads, outs)
     count = len(pieces)
     high = max(p.rows for p in pieces)
     wide = max(p.cols for p in pieces)
-    kernel = functools.partial(sync_kernel, pieces, 1.0 / replicas, len(grads), len(out_shapes))
-    vmem = lambda *dims: pltpu.VMEM(dims, jnp.float32)
-    return pl.pallas_call(
+    points = pos.shape[2]
+    kernel = functools.partial(
+        back_kernel, pieces, len(out_shapes), fine, start, points, (replicas, len(early))
+    )
+    f32 = lambda *dims: pltpu.VMEM(dims, jnp.float32)
+    anywhere = pl.BlockSpec(memory_space=pl.ANY)
+    results = pl.pallas_call(
         kernel,
-        out_shape=[jax.ShapeDtypeStruct(s, jnp.float32) for s in out_shapes],
-        in_specs=[pl.BlockSpec(memory_space=pl.ANY)] * len(grads),
-        out_specs=[pl.BlockSpec(memory_space=pl.ANY)] * len(out_shapes),
+        out_shape=[jax.ShapeDtypeStruct(s, jnp.float32) for s in out_shapes]
+        + [jax.ShapeDtypeStruct((rows, width), jnp.float32)],
+        in_specs=[VMEM] * 6
+        + [anywhere, VMEM, anywhere]
+        + [VMEM] * 7
+        + [anywhere] * len(early),
+        out_specs=[anywhere] * len(out_shapes) + [VMEM],
         scratch_shapes=[
-            vmem(count, high // 2, wide),
-            vmem(count, high // 2, wide),
-            vmem(count, LINE - 1, high // 8, wide),
-            vmem(count, LINE - 1, high // 8, wide),
+            pltpu.VMEM(qkv.shape, jnp.bfloat16),
+            f32(start, PAIR),
+            f32(start, PAIR),
+            f32(rows, width),
+            f32(rows, width),
+            f32(width // 2, qkv.shape[1]),
+            f32(width // 2, channels * fine_pairs.shape[1] // 2),
+            f32(2 * POINT_ROWS, width),
+            f32(count, high // 2, wide),
+            f32(count, high // 2, wide),
+            f32(count, LINE - 1, high // 8, wide),
+            f32(count, LINE - 1, high // 8, wide),
             pltpu.SemaphoreType.DMA((count, SEMS + 2)),
+            pltpu.SemaphoreType.DMA((2,)),
+            f32(2, LN_ROWS, width),
+            f32(2, LN_ROWS, width),
+            pltpu.SemaphoreType.DMA((2, 2)),
         ],
         compiler_params=pltpu.CompilerParams(
-            collective_id=0, has_side_effects=True, vmem_limit_bytes=56 << 20
+            collective_id=0, has_side_effects=True, vmem_limit_bytes=63 << 20
         ),
-        name="sync_grads",
-    )(*grads)
+        name="back_and_sync",
+    )(
+        qkv,
+        grad_mixed,
+        segment[:, None],
+        segment[None, start:],
+        normed_part,
+        w_qkv,
+        standard,
+        inverse,
+        grad_middle,
+        gain,
+        tokens,
+        patches,
+        fine_pairs,
+        pos_fine,
+        pos,
+        rest,
+        *early,
+    )
+    return results[:-1], results[-1]
 
 
 def tensor_sum(partial):
@@ -916,12 +1097,14 @@
     segment = jnp.where(valid, slot, 4)
     valid_rows = wide(valid)[:, None]
 
-    embedded, tokens, patches, mixed_weight = embed(
+    embedded, tokens, patches, mixed_weight, fine_pairs = embed(
         sizes, order, pix, table, pos_fine, pos, w_base, patch_bias, pos_base, rows
     )
     w_qkv = jnp.concatenate([w_query, w_key, w_value], axis=1)
     bias_qkv = jnp.concatenate([bias_query, jnp.zeros_like(bias_query), bias_value])
-    standard_one, standard_back_one = jax.vjp(standardize, embedded)
+    centered = embedded - jnp.mean(embedded, axis=-1, keepdims=True)
+    inverse_one = lax.rsqrt(jnp.mean(centered * centered, axis=-1, keepdims=True) + 1e-06)
+    standard_one = centered * inverse_one
     normed_one = (standard_one * wide(gain_one) + wide(shift_one)).astype(jnp.bfloat16)
     qkv = (
         jnp.dot(normed_one, w_qkv, preferred_element_type=jnp.float32) + wide(bias_qkv)
@@ -989,70 +1172,29 @@
     grad_mixed = jnp.einsum(
         "td,ed->te", grad_attended, w_out, preferred_element_type=jnp.float32
     ).astype(jnp.bfloat16)
-    grad_qkv = attend_back(qkv, grad_mixed, segment, fine, start)
-    grad_w_qkv = jnp.einsum(
-        "td,te->de", own_part(normed_one), grad_qkv, preferred_element_type=jnp.float32
-    )
-    grad_bias_qkv = jnp.sum(grad_qkv, axis=0, dtype=jnp.float32)
-    cut = bias_query.shape[0]
-    grad_bias_query, grad_bias_value = grad_bias_qkv[:cut], grad_bias_qkv[2 * cut :]
-    grad_normed_one = tensor_sum(
-        jnp.einsum("te,de->td", grad_qkv, w_qkv, preferred_element_type=jnp.float32)
-    )
-    grad_embedded = grad_middle + standard_back_one(grad_normed_one * wide(gain_one))[0]
-    grad_embedded_low = grad_embedded.astype(jnp.bfloat16)
-    pixel_grad, grad_w_base, grad_pos_base = pixel_back(
-        sizes,
-        jnp.stack([core, side_x, is_fine.astype(jnp.int32)]),
-        grad_embedded,
-        table,
-        pos_fine,
-        pos,
-        w_base,
-        tokens,
-        patches,
-        mixed_weight,
-        pixels.shape,
-    )
-    grad_patch_bias = jnp.sum(grad_embedded_low, axis=0, dtype=jnp.float32)
-    grad_gain_one = jnp.sum(grad_normed_one * standard_one, axis=0)
-    grad_shift_one = jnp.sum(grad_normed_one, axis=0)
-    grad_bias_out = jnp.sum(grad_attended, axis=0, dtype=jnp.float32)
-    grad_gain_two = jnp.sum(grad_normed_two * standard_two, axis=0)
-    grad_shift_two = jnp.sum(grad_normed_two, axis=0)
-    grad_bias_down = jnp.sum(grad_branch, axis=0, dtype=jnp.float32)
-    width = grad_patch_bias.shape[0]
-    small_rows = [
-        grad_pos_base,
-        grad_patch_bias[None],
-        grad_gain_one[None],
-        grad_shift_one[None],
-        grad_bias_out[None],
-        grad_gain_two[None],
-        grad_shift_two[None],
-        grad_bias_down[None],
-        jnp.concatenate([grad_bias_query, grad_bias_value])[None],
-        grad_bias_up.reshape(-1, width),
-    ]
-    bundle = jnp.concatenate(small_rows, axis=0)
+    points = pos.shape[2]
+    width = grad_attended.shape[1]
+    bundle = jnp.concatenate(
+        [
+            jnp.zeros((points + 3, width), jnp.float32),
+            jnp.sum(grad_attended, axis=0, dtype=jnp.float32)[None],
+            jnp.sum(grad_normed_two * standard_two, axis=0)[None],
+            jnp.sum(grad_normed_two, axis=0)[None],
+            jnp.sum(grad_branch, axis=0, dtype=jnp.float32)[None],
+            jnp.zeros((1, width), jnp.float32),
+            grad_bias_up.reshape(-1, width),
+        ],
+        axis=0,
+    )
     used = bundle.shape[0]
-    bundle = jnp.pad(bundle, ((0, -used % 128), (0, 0)))
-    bundle_part = lax.dynamic_slice_in_dim(
-        bundle, side_x * (bundle.shape[0] // 2), bundle.shape[0] // 2, axis=0
-    )
-    parts = [grad_w_down, grad_w_up, grad_w_qkv, grad_w_base, grad_w_out, bundle_part]
-    beyond = replicas // 16
-    step = 1
-    while step < beyond:
-        swap = [(i, (i // 16 ^ step) * 16 + i % 16) for i in range(replicas)]
-        parts = [part + lax.ppermute(part, "dp", swap) for part in parts]
-        step *= 2
+    bundle = jnp.pad(bundle, ((0, 2 * POINT_ROWS - used), (0, 0)))
+    early = [grad_w_down, grad_w_up, grad_w_out]
     area = w_base.shape[1] // channels
-    base_shape = (2 * grad_w_base.shape[0], w_base.shape[1])
     ff = w_down.shape[0]
     deep = w_up.shape[0]
+    cut = bias_query.shape[0]
     out_shapes = [
-        base_shape,
+        w_base.shape,
         w_down.shape,
         w_up.shape,
         w_query.shape,
@@ -1061,17 +1203,62 @@
         w_out.shape,
         bundle.shape,
     ]
+    grads = [
+        (ff // 2, width, 0),
+        (deep // 2, ff, 0),
+        (cut // 2, width, 0),
+        (deep // 2, 3 * cut, 0),
+        (width // 2, w_base.shape[1] // 2, 0),
+        (POINT_ROWS, width, POINT_ROWS),
+    ]
     outs = [
-        [(1, width, ff // 2, 0, 0, None)],
-        [(2, ff, deep // 2, 0, 0, None)],
-        [(3 + k, cut, deep // 2, 0, 0, None) for k in range(3)],
+        [(1, width, ff // 2, 0, 0, 0)],
+        [(2, ff, deep // 2, 0, 0, 0)],
+        [(6, width, cut // 2, 0, 0, 0)],
+        [(3 + k, cut, deep // 2, 0, 0, 0) for k in range(3)],
         [(0, area // 2, 0, width // 2, area // 2, area * c) for c in range(channels)],
-        [(6, width, cut // 2, 0, 0, None)],
-        [(7, width, bundle.shape[0] // 2, 0, 0, None)],
+        [(7, width, POINT_ROWS, 0, 0, 0)],
     ]
-    synced = sync_grads(parts, out_shapes, outs, replicas)
+    synced, grad_embedded = back_and_sync(
+        qkv,
+        grad_mixed,
+        segment,
+        own_part(normed_one),
+        w_qkv,
+        standard_one,
+        inverse_one,
+        grad_middle,
+        wide(gain_one)[None],
+        tokens,
+        patches,
+        fine_pairs,
+        pos_fine,
+        pos,
+        bundle,
+        early,
+        out_shapes,
+        grads,
+        outs,
+        fine,
+        start,
+        replicas,
+    )
+    beyond = replicas // 16
+    step = 1
+    while step < beyond:
+        swap = [(i, (i // 16 ^ step) * 16 + i % 16) for i in range(replicas)]
+        synced = [part + lax.ppermute(part, "dp", swap) for part in synced]
+        step *= 2
+    pixel_grad = pixel_back(
+        sizes,
+        is_fine.astype(jnp.int32)[None],
+        grad_embedded,
+        table,
+        w_base,
+        mixed_weight,
+        pixels.shape,
+    )
     base_s, down_s, up_s, query_s, key_s, value_s, out_s, small_s = synced
-    points = pos.shape[2]
     line = lambda k: small_s[points + k]
     return (
         output,

time: 518 us -> 490 us (0.946)
  Pallas kernels: 322 us -> 309 us
  other arithmetic: 56.7 us -> 50.9 us
  waiting for transfers between devices: 17.1 us -> 11.4 us
    pallas_call x3 -> x2, Pallas kernels: 285 us -> 270 us  [the longest x1 258 us: back_and_sync(): pl.pallas_call(kernel, out_shape=[jax.ShapeDtypeStruct(s, jnp.float32) fo...]
    dot_general x2 -> x0, matrix products: 7.24 us -> none  [the longest x1 4.55 us: local(): jnp.einsum('te,de->td', grad_qkv, w_qkv, preferred_element_type=jnp.float32)]
    ppermute x4 -> x3, waiting for transfers between devices: 5.7 us -> 0.01 us  [tensor_sum(): return partial + lax.ppermute(partial, 'tensor', [(0, 1), (1, 0)])]
    reduce_sum x4 -> x2, other arithmetic: 11.6 us -> 8.71 us  [standardize(): centered = values - jnp.mean(values, axis=-1, keepdims=True)]
    reduce_sum x6 -> x5, other arithmetic: 12 us -> 10.6 us  [the longest x1 4.47 us: local(): jnp.sum(grad_normed_two * standard_two, axis=0)[None]]
    unnamed x160 -> x138, local copies, waits for them, and re-layouts: 31.7 us -> 30.5 us
  transfers between devices with their start and end apart: 8 -> 7, of which waited for: 3 -> 1; matrix products, arithmetic and copies ran while one was open for 16% -> 16% of each run, Pallas kernels for 7% -> 8%
where the time goes in v4:
time: 490 us; the launch traced here: 482 us
  Pallas kernels  309 us (63%)
  local copies, waits for them, and re-layouts  54.5 us (11%)
  other arithmetic  50.9 us (10%)
  matrix products  45.1 us (9%)
  waiting for transfers between devices  11.4 us (2%)
  between operations  7.25 us (1%)
    pallas_call x1, Pallas kernels, back_and_sync(): pl.pallas_call(kernel, out_shape=[jax.ShapeDtypeStruct(s, jnp.float32) fo...  258 us
    unnamed x138, local copies, waits for them, and re-layouts  30.5 us
    pallas_call x1, Pallas kernels, embed(): pl.pallas_call(embed_kernel, out_shape=[jax.ShapeDtypeStruct((rows, width...  25 us
    pallas_call x1, Pallas kernels, attend(): pl.pallas_call(kernel, grid=(heads,), out_shape=jax.ShapeDtypeStruct((row...  13.2 us
    pallas_call x1, Pallas kernels, pixel_back(): pl.pallas_call(pixel_kernel, out_shape=jax.ShapeDtypeStruct(shape, jnp.fl...  12.8 us
    ppermute x2, waiting for transfers between devices, from_partner(): direct = lax.ppermute(mine, 'dp', there)  11.4 us
    dot_general x1, matrix products, local(): jnp.dot(normed_two, w_up, preferred_element_type=jnp.float32)  11.1 us
  transfers between devices with their start and end apart: 7, of which 1 were waited for; matrix products, arithmetic and copies ran while one was open for 16% of the time, Pallas kernels for 8%

profile of v4, /device:TPU:0, one launch (start us, length us, event | category | flops | bytes accessed | tf_op | source)
XLA Modules:
  0.0 481.8 jit_solution(2353156236778043201)
XLA Ops:
  3.7 2.9 collective-permute-start
  6.6 3.4 convert_element_type.114
  12.8 11.4 %collective-permute-done = f32[3,240,256]{2,1,0:T(8,128)} collective-permute-done((f32[3,240,256]{2,1,0:T(8,128)}, f32[3,240,256]{2,1,0:T(8,128)}, u32[]{:S(2)}, u32[]{:S(2)}) %collective-permute-start) | collective-permute-done | bytes 737312 | tf_op jit(solution)/shard_map/ppermute | solution.py:978
  39.6 3.3 pad_maximum_fusion.pix
  43.1 25.0 %embed.1 = (f32[1232,768]{1,0:T(8,128)}, bf16[3,104,3072]{2,1,0:T(8,128)(2,1)S(1)}, bf16[3,912,64]{2,1,0:T(8,128)(2,1)S(1)}, bf16[3,64,768]{2,1,0:T(8,128)(2,1)S(1)}, bf16[64,1024]{1,0:T(8,128)(2,1)S(1)}) custom-call(s32[4]{0:T(128)S(1)} %get-tuple-element.78.sizes, s32[4]{0:T(128)S(1)} %get-tuple-element.79.order, f32[4,3,240,256]{3,2,1,0:T(8,128)} %pad_maximum_fusion.pix, ...), custom_call_target="tpu_custom_call" | custom-call | tf_op jit(solution)/shard_map/embed/pallas_call | solution.py:161
  73.9 2.8 multiply_reduce_fusion.3
  82.0 2.8 fusion.7.query.key.value.refs_0_
  85.5 2.8 and_select_fusion.segment.refs_2_
  88.4 13.2 %attend.1 = bf16[1232,384]{1,0:T(8,128)(2,1)S(1)} custom-call(bf16[1232,1152]{1,0:T(8,128)(2,1)S(1)} %fusion.7.query.key.value.refs_0_, bf16[1232,1152]{1,0:T(8,128)(2,1)S(1)} %fusion.7.query.key.value.refs_0_, bf16[1232,1152]{1,0:T(8,128)(2,1)S(1)} %fusion.7.query.key.value.refs_0_, s32[1232,1]{1,0:T(8,128)S(1)} %and_select_fusion.segment.refs_2_, ...), custom_call_target="tpu_custom_call" | custom-call | tf_op jit(solution)/shard_map/attend/pallas_call | solution.py:286
  101.6 3.0 fusion.52
  108.0 3.4 broadcast_select_fusion
  115.8 5.7 %fusion.54 = f32[1232,1536]{1,0:T(8,128)} fusion(bf16[1232,768]{1,0:T(8,128)(2,1)S(1)} %get-tuple-element.63, bf16[1536,768]{1,0:T(8,128)(2,1)S(1)} %copy-done.53), kind=kOutput, calls=%fused_computation.148 | convolution fusion | flops 2906652672 | bytes 11821056 | tf_op jit(solution)/shard_map/td,fd->tf/dot_general | solution.py:1156
  121.5 4.1 fusion.49
  128.6 11.1 %convert_reduce_fusion = (f32[1536]{0:T(1024)S(1)}, bf16[1232,1536]{1,0:T(8,128)(2,1)S(1)}, bf16[1232,1536]{1,0:T(8,128)(2,1)S(1)}) fusion(f32[1232,1536]{1,0:T(8,128)} %fusion.54, f32[1536]{0:T(1024)S(1)} %convert_element_type.110, bf16[1232,768]{1,0:T(8,128)(2,1)S(1)} %add_convert_fusion.1, bf16[768,1536]{1,0:T(8,128)(2,1)S(1)} %copy-done.52), kind=kOutput, calls=%fused_computation.14 | convolution fusion | flops 2953959936 | bytes 19402752 | tf_op jit(solution)/shard_map/dot_general | solution.py:1119
  139.8 5.0 %fusion.55 = f32[1232,768]{1,0:T(8,128)} fusion(bf16[1232,1536]{1,0:T(8,128)(2,1)S(1)} %get-tuple-element.61, bf16[768,1536]{1,0:T(8,128)(2,1)S(1)} %copy-done.52), kind=kOutput, calls=%fused_computation.149 | convolution fusion | flops 2906652672 | bytes 9928704 | tf_op jit(solution)/shard_map/tf,df->td/dot_general | solution.py:1165
  145.3 5.0 %fusion.53 = f32[1232,768]{1,0:T(8,128)} fusion(bf16[1232,1536]{1,0:T(8,128)(2,1)S(1)} %get-tuple-element.80, bf16[1536,768]{1,0:T(8,128)(2,1)S(1)} %copy-done.53), kind=kOutput, calls=%fused_computation.147 | convolution fusion | flops 2906652672 | bytes 9928704 | tf_op jit(solution)/shard_map/dot_general | solution.py:1122
  157.1 5.5 %fusion.9.refs_16_ = f32[768,768]{1,0:T(8,128)} fusion(bf16[1232,768]{1,0:T(8,128)(2,1)} %copy-done.26, bf16[1232,1536]{1,0:T(8,128)(2,1)} %copy-done.57, s32[]{:T(128)S(6)} %select_n.354), kind=kOutput, calls=%fused_computation.36 | convolution fusion | flops 1453326336 | bytes 6144004 | tf_op jit(solution)/shard_map/tf,td->fd/dot_general | solution.py:1153
  162.6 3.1 fusion.14.refs_17_
  165.7 4.5 multiply_reduce_fusion
  170.2 4.6 fusion.48
  182.1 257.7 %back_and_sync.1 = (f32[768,3072]{1,0:T(8,128)}, f32[1536,768]{1,0:T(8,128)}, f32[768,1536]{1,0:T(8,128)}, f32[768,384]{1,0:T(8,128)}, f32[768,384]{1,0:T(8,128)...) custom-call(bf16[1232,1152]{1,0:T(8,128)(2,1)} %copy-done.1, ...), custom_call_target="tpu_custom_call" | custom-call | tf_op jit(solution)/shard_map/back_and_sync/pallas_call | solution.py:918
  450.3 12.8 %pixel_back.1 = f32[2,3,240,240]{3,2,1,0:T(8,128)} custom-call(s32[4]{0:T(128)S(1)} %get-tuple-element.78.sizes, s32[1]{0:T(128)S(6)} %broadcast_in_dim.202.is_fine, f32[1232,768]{1,0:T(8,128)S(1)} %copy-done.4, bf16[4,48,32]{2,1,0:T(8,128)(2,1)S(1)} %broadcast_select_fusion.2.table, bf16[768,3072]{1,0:T(8,128)(2,1)S(1)} %copy-done.2, ...), custom_call_target="tpu_custom_call" | custom-call | tf_op jit(solution)/shard_map/pixel_back/pallas_call | solution.py:233
  463.1 4.2 fusion.13
  467.4 4.1 copy.71
  (241 shorter events, 72.9 us)
Async XLA Ops:
  0.7 100.9 %copy-start = (bf16[384,768]{1,0:T(8,128)(2,1)S(1)}, bf16[384,768]{1,0:T(8,128)(2,1)}, u32[]{:S(2)}) copy-start(bf16[384,768]{1,0:T(8,128)(2,1)} %param.43) | copy-start | bytes 1769476
  3.7 20.6 %collective-permute-start = (f32[3,240,256]{2,1,0:T(8,128)}, f32[3,240,256]{2,1,0:T(8,128)}, u32[]{:S(2)}, u32[]{:S(2)}) collective-permute-start(f32[3,240,256]{2,1,0:T(8,128)} %dynamic-slice_bitcast_fusion), channel_id=1, source_target_pairs={{0,2},{2,0},{4,6},{6,4},{8,10},{10,8},{12,14},{14,12},{16,18},{18,... | collective-permute-start | bytes 2211848 | tf_op jit(solution)/shard_map/ppermute | solution.py:978
  6.6 19.1 %copy-start.46 = (bf16[768]{0:T(1024)(128)(2,1)S(1)}, bf16[768]{0:T(1024)(128)(2,1)}, u32[]{:S(2)}) copy-start(bf16[768]{0:T(1024)(128)(2,1)} %param.34) | copy-start | bytes 4612
  6.6 19.1 %copy-start.41 = (bf16[768]{0:T(1024)(128)(2,1)S(1)}, bf16[768]{0:T(1024)(128)(2,1)}, u32[]{:S(2)}) copy-start(bf16[768]{0:T(1024)(128)(2,1)} %param.37) | copy-start | bytes 4612
  6.6 19.1 %copy-start.38 = (bf16[768]{0:T(1024)(128)(2,1)S(1)}, bf16[768]{0:T(1024)(128)(2,1)}, u32[]{:S(2)}) copy-start(bf16[768]{0:T(1024)(128)(2,1)} %param.36) | copy-start | bytes 4612
  6.6 19.1 %copy-start.37 = (bf16[768,49]{0,1:T(8,128)(2,1)S(1)}, bf16[768,49]{0,1:T(8,128)(2,1)}, u32[]{:S(2)}) copy-start(bf16[768,49]{0,1:T(8,128)(2,1)} %param.35) | copy-start | bytes 225796
  6.6 19.5 %copy-start.36 = (bf16[49,48,32]{0,2,1:T(8,128)(2,1)S(1)}, bf16[49,48,32]{0,2,1:T(8,128)(2,1)}, u32[]{:S(2)}) copy-start(bf16[49,48,32]{0,2,1:T(8,128)(2,1)} %param.31) | copy-start | bytes 451588
  10.0 17.7 %slice-start.4 = ((bf16[31,900,49]{1,0,2:T(8,128)(2,1)}), bf16[31,100,49]{1,0,2:T(8,128)(2,1)S(1)}, s32[]{:S(2)}) async-start(bf16[31,900,49]{1,0,2:T(8,128)(2,1)} %param.32), calls=%async_computation.4 | async-start | bytes 802816 | tf_op jit(solution)/shard_map/slice | solution.py:1086
  10.0 17.9 %copy-start.48 = (bf16[384]{0:T(512)(128)(2,1)S(1)}, bf16[384]{0:T(512)(128)(2,1)}, u32[]{:S(2)}) copy-start(bf16[384]{0:T(512)(128)(2,1)} %param.42) | copy-start | bytes 2308
  10.0 17.9 %copy-start.49 = (bf16[384]{0:T(512)(128)(2,1)S(1)}, bf16[384]{0:T(512)(128)(2,1)}, u32[]{:S(2)}) copy-start(bf16[384]{0:T(512)(128)(2,1)} %param.39) | copy-start | bytes 2308
  12.7 72.2 %collective-permute-start.4 = (f32[512,768]{1,0:T(8,128)}, f32[512,768]{1,0:T(8,128)}, u32[]{:S(2)}, u32[]{:S(2)}) collective-permute-start(f32[512,768]{1,0:T(8,128)} %constant_dynamic-slice_fusion.1), channel_id=1, source_target_pairs={{0,2},{2,0},{4,6},{6,4},{8,10},{10,8},{12,14},{14,12},{16,18},{18,... | collective-permute-start | bytes 4718600 | tf_op jit(solution)/shard_map/ppermute | solution.py:978
  24.2 8.5 %collective-permute-start.1 = (f32[3,240,256]{2,1,0:T(8,128)}, f32[3,240,256]{2,1,0:T(8,128)}, u32[]{:S(2)}, u32[]{:S(2)}) collective-permute-start(f32[3,240,256]{2,1,0:T(8,128)} %collective-permute-done), channel_id=1, source_target_pairs={{0,1},{1,0},{2,3},{3,2},{4,5},{5,4},{6,7},{7,6},{8,9},{9,8},{10,11... | collective-permute-start | bytes 2211848 | tf_op jit(solution)/shard_map/ppermute | solution.py:979
  26.2 16.9 %copy-start.5 = (bf16[1,900,49]{2,1,0:T(8,128)(2,1)}, bf16[1,900,49]{2,1,0:T(8,128)(2,1)S(1)}, u32[]{:S(2)}) copy-start(bf16[1,900,49]{2,1,0:T(8,128)(2,1)S(1)} %copy.56) | copy-start | bytes 264604
  43.1 25.0 %copy-start.7 = (bf16[3,100,49]{2,1,0:T(8,128)(2,1)}, bf16[3,100,49]{2,1,0:T(8,128)(2,1)S(1)}, u32[]{:S(2)}) copy-start(bf16[3,100,49]{2,1,0:T(8,128)(2,1)S(1)} %broadcast_select_fusion.1.pos.refs_14_) | copy-start | bytes 88204
  84.9 16.6 %copy-start.1 = (bf16[1232,1152]{1,0:T(8,128)(2,1)}, bf16[1232,1152]{1,0:T(8,128)(2,1)S(1)}, u32[]{:S(2)}) copy-start(bf16[1232,1152]{1,0:T(8,128)(2,1)S(1)} %fusion.7.query.key.value.refs_0_) | copy-start | bytes 8515588
  84.9 23.1 %collective-permute-start.5 = (f32[512,768]{1,0:T(8,128)}, f32[512,768]{1,0:T(8,128)}, u32[]{:S(2)}, u32[]{:S(2)}) collective-permute-start(f32[512,768]{1,0:T(8,128)} %collective-permute-done.4), channel_id=1, source_target_pairs={{0,1},{1,0},{2,3},{3,2},{4,5},{5,4},{6,7},{7,6},{8,9},{9,8},{10,11... | collective-permute-start | bytes 4718600 | tf_op jit(solution)/shard_map/ppermute | solution.py:979
  88.3 13.2 %copy-start.3 = (s32[1232,1]{1,0:T(8,128)}, s32[1232,1]{1,0:T(8,128)S(1)}, u32[]{:S(2)}) copy-start(s32[1232,1]{1,0:T(8,128)S(1)} %and_select_fusion.segment.refs_2_) | copy-start | bytes 14788
  104.6 16.9 %collective-permute-start.2 = (f32[1232,768]{1,0:T(8,128)}, f32[1232,768]{1,0:T(8,128)}, u32[]{:S(2)}, u32[]{:S(2)}) collective-permute-start(f32[1232,768]{1,0:T(8,128)} %fusion.52), channel_id=1, source_target_pairs={{0,1},{1,0},{2,3},{3,2},{4,5},{5,4},{6,7},{7,6},{8,9},{9,8},{10,11... | collective-permute-start | bytes 11354120 | tf_op jit(solution)/shard_map/ppermute | solution.py:973
  144.8 20.9 %collective-permute-start.6 = (f32[1232,768]{1,0:T(8,128)}, f32[1232,768]{1,0:T(8,128)}, u32[]{:S(2)}, u32[]{:S(2)}) collective-permute-start(f32[1232,768]{1,0:T(8,128)} %fusion.55), channel_id=1, source_target_pairs={{0,1},{1,0},{2,3},{3,2},{4,5},{5,4},{6,7},{7,6},{8,9},{9,8},{10,11... | collective-permute-start | bytes 11354120 | tf_op jit(solution)/shard_map/ppermute | solution.py:973
  150.3 19.9 %collective-permute-start.3 = (f32[1232,768]{1,0:T(8,128)}, f32[1232,768]{1,0:T(8,128)}, u32[]{:S(2)}, u32[]{:S(2)}) collective-permute-start(f32[1232,768]{1,0:T(8,128)} %fusion.53), channel_id=1, source_target_pairs={{0,1},{1,0},{2,3},{3,2},{4,5},{5,4},{6,7},{7,6},{8,9},{9,8},{10,11... | collective-permute-start | bytes 11354120 | tf_op jit(solution)/shard_map/ppermute | solution.py:973
  182.1 263.8 %copy-start.10 = (bf16[3,64,768]{2,1,0:T(8,128)(2,1)S(1)}, bf16[3,64,768]{2,1,0:T(8,128)(2,1)}, u32[]{:S(2)}) copy-start(bf16[3,64,768]{2,1,0:T(8,128)(2,1)} %copy-done.9) | copy-start | bytes 884740
  450.3 12.8 %copy-start.34 = (bf16[104,768]{1,0:T(8,128)(2,1)S(1)}, bf16[104,768]{1,0:T(8,128)(2,1)}, u32[]{:S(2)}) copy-start(bf16[104,768]{1,0:T(8,128)(2,1)} %get-tuple-element.83) | copy-start | bytes 479236
  450.3 12.8 %copy-start.35 = (bf16[104,768]{1,0:T(8,128)(2,1)S(1)}, bf16[104,768]{1,0:T(8,128)(2,1)}, u32[]{:S(2)}) copy-start(bf16[104,768]{1,0:T(8,128)(2,1)} %get-tuple-element.84) | copy-start | bytes 479236
  450.3 17.1 %copy-start.20 = (f32[768,3072]{1,0:T(8,128)S(1)}, f32[768,3072]{1,0:T(8,128)}, u32[]{:S(2)}) copy-start(f32[768,3072]{1,0:T(8,128)} %get-tuple-element.117) | copy-start | bytes 28311556
  (46 other events, 215.8 us)

commit v5 on v4

--- a/solution.py
+++ b/solution.py
@@ -323,7 +323,7 @@
 MESH_ID = pl.DeviceIdType.MESH
 PIECE_ROWS = 192
 PIECE_COLS = 384
-CROSS_EVERY = 4
+CROSS_EVERY = 3
 SEMS = 48
 
 
@@ -678,41 +678,60 @@
 
 
 QUERY_BLOCK = 384
-LN_ROWS = 112
+CHUNK = 112
 POINT_ROWS = 64
 
 
-def back_kernel(pieces, sizes, fine, start, points, counts, *refs):
-    replicas, given = counts
+def gelu_slope(value):
+    root = math.sqrt(2.0 / math.pi)
+    square = value * value
+    bend = jnp.tanh(root * value * (1.0 + 0.044715 * square))
+    return 0.5 * (1.0 + bend) + (0.5 * root) * value * (1.0 - bend * bend) * (
+        1.0 + (3 * 0.044715) * square
+    )
+
+
+def back_kernel(pieces, sizes, fine, start, points, replicas, *refs):
     (
         qkv,
-        grad_mixed,
         segment,
         segment_row,
         normed_part,
+        normed_two_part,
+        mixed_part,
         w_qkv,
-        standard,
+        w_out,
+        w_up,
+        w_down,
+        bias_up,
         inverse,
-        grad_middle,
-        gain,
+        gain_one,
+        gain_two,
         tokens,
         patches,
         fine_pairs,
         pos_fine,
         pos,
         rest,
-    ) = refs[:16]
-    early = refs[16 : 16 + given]
-    refs = refs[16 + given :]
-    outs, grad_embedded, refs = refs[:sizes], refs[sizes], refs[sizes + 1 :]
+        standard_one,
+        standard_two,
+        normed_two,
+        grad_branch,
+        grad_w_down,
+    ) = refs[:25]
+    refs = refs[25:]
+    outs, grad_embedded, middle, refs = refs[:sizes], refs[sizes], refs[sizes + 1], refs[sizes + 2 :]
     (
-        grad_qkv,
+        shared,
+        grad_mixed,
         grad_key,
         grad_value,
         partial,
         arrived,
         grad_w_qkv,
         grad_w_base,
+        grad_w_up,
+        grad_w_out,
         bundle,
         acc,
         land,
@@ -720,17 +739,137 @@
         land_left,
         sems,
         swap_sems,
-        chunk_standard,
-        chunk_middle,
+        free_sem,
+        chunk_one,
+        chunk_two,
+        chunk_branch,
+        chunk_low,
         chunk_sems,
+        out_sem,
     ) = refs
-    rows, width = standard.shape
+    rows, width = standard_one.shape
     third = qkv.shape[1] // 3
+    hidden_width = w_up.shape[1]
     scale = 1.0 / math.sqrt(HD)
     low = lambda value: value.astype(jnp.bfloat16)
-    blocks = range(0, rows, LN_ROWS)
+    column_sum = lambda value: jnp.sum(value, axis=0, keepdims=True)
+    count = rows // CHUNK
 
     def prepare(core, place_x, sibling, remote):
+        def rows_of(ref, number):
+            return ref.at[pl.ds(pl.multiple_of(number * CHUNK, 16), CHUNK)]
+
+        def stream(ref, slots, kind, number):
+            at = lax.rem(number, 2)
+            return pltpu.make_async_copy(rows_of(ref, number), slots.at[at], chunk_sems.at[kind, at])
+
+        def over_chunks(begin, end, streams, body):
+            for ref, slots, kind in streams:
+                stream(ref, slots, kind, begin).start()
+
+            @pl.loop(begin, end)
+            def _(number):
+                @pl.when(number + 1 < end)
+                def _():
+                    for ref, slots, kind in streams:
+                        stream(ref, slots, kind, number + 1).start()
+
+                for ref, slots, kind in streams:
+                    stream(ref, slots, kind, number).wait()
+                body(number, lax.rem(number, 2))
+
+        def swap(turn):
+            return remote(
+                partial, arrived, swap_sems.at[2 * turn], swap_sems.at[2 * turn + 1], sibling
+            )
+
+        def ffn_job(begin, end):
+            def body(number, at):
+                here = pl.ds(pl.multiple_of(number * CHUNK, 16), CHUNK)
+                hidden = nn(chunk_low[at], w_up[...]) + bias_up[...]
+                grad_hidden = low(nt(chunk_branch[at], w_down[...]) * gelu_slope(hidden))
+                shared[here, :] = grad_hidden
+                partial[here, :] = nt(grad_hidden, w_up[...])
+                total = column_sum(grad_hidden.astype(jnp.float32))
+                for k in range(hidden_width // width):
+                    bundle[points + 8 + k : points + 9 + k, :] += total[
+                        :, k * width : (k + 1) * width
+                    ]
+
+            def job():
+                if begin == 0:
+                    bundle[...] = rest[...]
+                over_chunks(
+                    begin, end, [(normed_two, chunk_low, 0), (grad_branch, chunk_branch, 1)], body
+                )
+                if end == count:
+                    swap(0).start()
+
+            return job
+
+        def up_job():
+            grad_w_up[...] = tn(normed_two_part[...], shared[...])
+
+        def norm_rows(number, at, slots, gain, scale_column, row, before, after):
+            @pl.loop(0, CHUNK // 16)
+            def _(i):
+                inner = pl.ds(pl.multiple_of(i * 16, 16), 16)
+                here = pl.ds(pl.multiple_of(number * CHUNK + i * 16, 16), 16)
+                grad = partial[here, :] + arrived[here, :]
+                z = slots[at, inner, :]
+                up = grad * gain[...]
+                mean = jnp.mean(up, axis=1, keepdims=True)
+                along = jnp.mean(up * z, axis=1, keepdims=True)
+                back = (up - mean - z * along) * inverse[here, scale_column : scale_column + 1]
+                value = before(inner) + back
+                bundle[row : row + 1, :] += column_sum(grad * z)
+                bundle[row + 1 : row + 2, :] += column_sum(grad)
+                after(here, inner, value)
+
+        def two_job(begin, end):
+            def body(number, at):
+                @pl.when(number >= 2)
+                def _():
+                    store_middle(number - 2).wait()
+
+                def before(inner):
+                    return chunk_branch[at, inner, :].astype(jnp.float32)
+
+                def after(here, inner, value):
+                    chunk_two[at, inner, :] = value
+                    chunk_low[0, inner, :] = low(value)
+                    bundle[points + 3 : points + 4, :] += column_sum(
+                        low(value).astype(jnp.float32)
+                    )
+
+                norm_rows(number, at, chunk_one, gain_two, 1, points + 4, before, after)
+                store_middle(number).start()
+                here = pl.ds(pl.multiple_of(number * CHUNK, 16), CHUNK)
+                grad_mixed[here, :] = low(nt(chunk_low[0], w_out[...]))
+                grad_w_out[...] += tn(mixed_part[here, :], chunk_low[0])
+
+            def job():
+                if begin == 0:
+                    swap(0).wait()
+                    grad_w_out[...] = jnp.zeros_like(grad_w_out)
+                over_chunks(
+                    begin, end, [(standard_two, chunk_one, 0), (grad_branch, chunk_branch, 1)], body
+                )
+                if end == count:
+                    store_middle(count - 2).wait()
+                    store_middle(count - 1).wait()
+                    pl.semaphore_signal(
+                        free_sem, inc=1, device_id=sibling, device_id_type=MESH_ID
+                    )
+
+            return job
+
+        def store_middle(number):
+            at = lax.rem(number, 2)
+            return pltpu.make_async_copy(
+                chunk_two.at[at], rows_of(middle, number), chunk_sems.at[2, at]
+            )
+
         def back_rows(pair, here, keys, mask):
             column = lambda k: slice(k * third + pair * PAIR, k * third + (pair + 1) * PAIR)
             return attend_back_block(
@@ -743,7 +882,7 @@
             )
 
         def store_qkv(pair, k, here, value):
-            grad_qkv[here, k * third + pair * PAIR : k * third + (pair + 1) * PAIR] = low(value)
+            shared[here, k * third + pair * PAIR : k * third + (pair + 1) * PAIR] = low(value)
 
         def fine_job(pair, begin):
             def job():
@@ -774,60 +913,27 @@
             return job
 
         def weight_job():
-            grad_w_qkv[...] = tn(normed_part[...], grad_qkv[...])
+            grad_w_qkv[...] = tn(normed_part[...], shared[:, : 3 * third])
 
         def partial_job():
-            partial[...] = nt(grad_qkv[...], w_qkv[...])
-            swap().start()
-
-        def swap():
-            return remote(partial, arrived, swap_sems.at[0], swap_sems.at[1], sibling)
-
-        def chunk_copies(number):
-            here = pl.ds(pl.multiple_of(number * LN_ROWS, 8), LN_ROWS)
-            at = lax.rem(number, 2)
-            return [
-                pltpu.make_async_copy(standard.at[here], chunk_standard.at[at], chunk_sems.at[0, at]),
-                pltpu.make_async_copy(
-                    grad_middle.at[here], chunk_middle.at[at], chunk_sems.at[1, at]
-                ),
-            ]
-
-        def norm_job():
-            swap().wait()
-            for copy in chunk_copies(0):
-                copy.start()
-            for k in range(3):
-                bundle[points + k : points + k + 1, :] = jnp.zeros((1, width), jnp.float32)
-
-            @pl.loop(0, len(blocks))
-            def _(number):
-                @pl.when(number + 1 < len(blocks))
-                def _():
-                    for copy in chunk_copies(number + 1):
-                        copy.start()
-
-                for copy in chunk_copies(number):
-                    copy.wait()
-                at = lax.rem(number, 2)
-
-                @pl.loop(0, LN_ROWS // 16)
-                def _(i):
-                    inner = pl.ds(pl.multiple_of(i * 16, 8), 16)
-                    here = pl.ds(pl.multiple_of(number * LN_ROWS + i * 16, 8), 16)
-                    grad = partial[here, :] + arrived[here, :]
-                    z = chunk_standard[at, inner, :]
-                    up = grad * gain[...]
-                    mean = jnp.mean(up, axis=1, keepdims=True)
-                    along = jnp.mean(up * z, axis=1, keepdims=True)
-                    value = (
-                        chunk_middle[at, inner, :] + (up - mean - z * along) * inverse[here, :]
-                    )
-                    grad_embedded[here, :] = value
-                    column = lambda v: jnp.sum(v, axis=0, keepdims=True)
-                    bundle[points : points + 1, :] += column(low(value).astype(jnp.float32))
-                    bundle[points + 1 : points + 2, :] += column(grad * z)
-                    bundle[points + 2 : points + 3, :] += column(grad)
+            partial[...] = nt(shared[:, : 3 * third], w_qkv[...])
+            pl.semaphore_wait(free_sem, 1)
+            swap(1).start()
+
+        def one_job():
+            def body(number, at):
+                def before(inner):
+                    return chunk_two[at, inner, :]
+
+                def after(here, inner, value):
+                    partial[here, :] = value
+                    bundle[points : points + 1, :] += column_sum(low(value).astype(jnp.float32))
+
+                norm_rows(number, at, chunk_one, gain_one, 0, points + 1, before, after)
+
+            swap(1).wait()
+            over_chunks(0, count, [(standard_one, chunk_one, 0), (middle, chunk_two, 2)], body)
+            pltpu.make_async_copy(partial, grad_embedded, out_sem).start()
 
         def base_job():
             half = grad_w_base.shape[0]
@@ -836,7 +942,7 @@
             area = 2 * part
             columns = pl.ds(pl.multiple_of(core * half, 128), half)
             stride = tokens.shape[1]
-            some = low(grad_embedded[:fine, columns])
+            some = low(partial[:fine, columns])
             wanted = fine_pairs[:, pl.ds(pl.multiple_of(place_x * part, 128), part)]
             for c in range(channels):
                 gathered = low(tn(patches[c, :fine, :], some))
@@ -844,31 +950,32 @@
                 for k in range(3):
                     begin = start + k * stride
                     here = pl.ds(pl.multiple_of(c * area + place_x * part, 128), part)
-                    total += tn(low(grad_embedded[begin : begin + stride, columns]), tokens[k, :, here])
+                    total += tn(low(partial[begin : begin + stride, columns]), tokens[k, :, here])
                 grad_w_base[:, c * part : (c + 1) * part] = total
 
         def bundle_job():
-            gathered = tn(pos_fine[...], low(grad_embedded[:fine, :]))
-            count = pos.shape[1]
+            gathered = tn(pos_fine[...], low(partial[:fine, :]))
             for k in range(3):
                 begin = start + k * tokens.shape[1]
-                gathered += tn(pos[k], low(grad_embedded[begin : begin + count, :]))
+                gathered += tn(pos[k], low(partial[begin : begin + pos.shape[1], :]))
             bundle[:points, :] = gathered
-            bundle[points + 3 : 2 * POINT_ROWS, :] = rest[points + 3 : 2 * POINT_ROWS, :]
-            sums = jnp.sum(grad_qkv[...].astype(jnp.float32), axis=0, keepdims=True)
+            sums = column_sum(shared[:, : 3 * third].astype(jnp.float32))
             bundle[points + 7 : points + 8, :third] = sums[:, :third]
             bundle[points + 7 : points + 8, third : 2 * third] = sums[:, 2 * third :]
-
-        jobs = []
+            pltpu.make_async_copy(partial, grad_embedded, out_sem).wait()
+
+        cuts = [count * k // 4 for k in range(5)]
+        jobs = [[ffn_job(a, b)] for a, b in zip(cuts[:-1], cuts[1:])]
+        jobs += [[up_job], [two_job(0, count)]]
         for pair in range(third // PAIR):
             jobs += [[fine_job(pair, begin)] for begin in range(0, start, QUERY_BLOCK)]
             jobs[-1].append(coarse_job(pair))
-        return jobs + [[partial_job], [weight_job], [norm_job], [base_job], [bundle_job]]
+        return jobs + [[weight_job], [partial_job], [one_job], [base_job], [bundle_job]]
 
     move_pieces(
         pieces,
         1.0 / replicas,
-        list(early) + [grad_w_qkv, grad_w_base, bundle],
+        [grad_w_down, grad_w_up, grad_w_out, grad_w_qkv, grad_w_base, bundle],
         outs,
         acc,
         land,
@@ -879,94 +986,59 @@
     )
 
 
-def back_and_sync(
-    qkv,
-    grad_mixed,
-    segment,
-    normed_part,
-    w_qkv,
-    standard,
-    inverse,
-    grad_middle,
-    gain,
-    tokens,
-    patches,
-    fine_pairs,
-    pos_fine,
-    pos,
-    rest,
-    early,
-    out_shapes,
-    grads,
-    outs,
-    fine,
-    start,
-    replicas,
-):
-    rows, width = standard.shape
+def back_and_sync(inside, anywhere, segment, out_shapes, grads, outs, fine, start, replicas):
+    qkv = inside[0]
+    rows, width = anywhere[0].shape
+    w_qkv, w_out, w_up = inside[4:7]
+    patches, fine_pairs, pos_fine, pos = inside[13:17]
     channels = patches.shape[0]
     pieces = sync_plan(grads, outs)
     count = len(pieces)
     high = max(p.rows for p in pieces)
     wide = max(p.cols for p in pieces)
-    points = pos.shape[2]
     kernel = functools.partial(
-        back_kernel, pieces, len(out_shapes), fine, start, points, (replicas, len(early))
+        back_kernel, pieces, len(out_shapes), fine, start, pos.shape[2], replicas
     )
     f32 = lambda *dims: pltpu.VMEM(dims, jnp.float32)
-    anywhere = pl.BlockSpec(memory_space=pl.ANY)
+    low = lambda *dims: pltpu.VMEM(dims, jnp.bfloat16)
     results = pl.pallas_call(
         kernel,
         out_shape=[jax.ShapeDtypeStruct(s, jnp.float32) for s in out_shapes]
-        + [jax.ShapeDtypeStruct((rows, width), jnp.float32)],
-        in_specs=[VMEM] * 6
-        + [anywhere, VMEM, anywhere]
-        + [VMEM] * 7
-        + [anywhere] * len(early),
-        out_specs=[anywhere] * len(out_shapes) + [VMEM],
+        + [jax.ShapeDtypeStruct((rows, width), jnp.float32)] * 2,
+        in_specs=[VMEM] * (len(inside) + 2) + [pl.BlockSpec(memory_space=pl.ANY)] * len(anywhere),
+        out_specs=[pl.BlockSpec(memory_space=pl.ANY)] * (len(out_shapes) + 2),
         scratch_shapes=[
-            pltpu.VMEM(qkv.shape, jnp.bfloat16),
+            low(rows, max(qkv.shape[1], w_up.shape[1])),
+            low(rows, qkv.shape[1] // 3),
             f32(start, PAIR),
             f32(start, PAIR),
             f32(rows, width),
             f32(rows, width),
             f32(width // 2, qkv.shape[1]),
             f32(width // 2, channels * fine_pairs.shape[1] // 2),
+            f32(width // 2, w_up.shape[1]),
+            f32(w_out.shape[0] // 2, width),
             f32(2 * POINT_ROWS, width),
             f32(count, high // 2, wide),
             f32(count, high // 2, wide),
             f32(count, LINE - 1, high // 8, wide),
             f32(count, LINE - 1, high // 8, wide),
             pltpu.SemaphoreType.DMA((count, SEMS + 2)),
-            pltpu.SemaphoreType.DMA((2,)),
-            f32(2, LN_ROWS, width),
-            f32(2, LN_ROWS, width),
-            pltpu.SemaphoreType.DMA((2, 2)),
+            pltpu.SemaphoreType.DMA((4,)),
+            pltpu.SemaphoreType.REGULAR,
+            f32(2, CHUNK, width),
+            f32(2, CHUNK, width),
+            low(2, CHUNK, width),
+            low(2, CHUNK, width),
+            pltpu.SemaphoreType.DMA((3, 2)),
+            pltpu.SemaphoreType.DMA,
         ],
         compiler_params=pltpu.CompilerParams(
             collective_id=0, has_side_effects=True, vmem_limit_bytes=63 << 20
         ),
         name="back_and_sync",
-    )(
-        qkv,
-        grad_mixed,
-        segment[:, None],
-        segment[None, start:],
-        normed_part,
-        w_qkv,
-        standard,
-        inverse,
-        grad_middle,
-        gain,
-        tokens,
-        patches,
-        fine_pairs,
-        pos_fine,
-        pos,
-        rest,
-        *early,
-    )
-    return results[:-1], results[-1]
+    )(inside[0], segment[:, None], segment[None, start:], *inside[1:], *anywhere)
+    return results[:-2], results[-2]
 
 
 def tensor_sum(partial):
@@ -1114,11 +1186,12 @@
         bias_out
     )
     middle = embedded + attended
-    standard_two, standard_back_two = jax.vjp(standardize, middle)
+    centered = middle - jnp.mean(middle, axis=-1, keepdims=True)
+    inverse_two = lax.rsqrt(jnp.mean(centered * centered, axis=-1, keepdims=True) + 1e-06)
+    standard_two = centered * inverse_two
     normed_two = (standard_two * wide(gain_two) + wide(shift_two)).astype(jnp.bfloat16)
     hidden = jnp.dot(normed_two, w_up, preferred_element_type=jnp.float32) + wide(bias_up)
-    activated_wide, gelu_back = jax.vjp(jax.nn.gelu, hidden)
-    activated = activated_wide.astype(jnp.bfloat16)
+    activated = jax.nn.gelu(hidden).astype(jnp.bfloat16)
     branch = tensor_sum(jnp.dot(activated, w_down, preferred_element_type=jnp.float32)) + wide(
         bias_down
     )
@@ -1153,42 +1226,17 @@
     grad_w_down = jnp.einsum(
         "tf,td->fd", own_part(activated), grad_branch, preferred_element_type=jnp.float32
     )
-    grad_activated = jnp.einsum(
-        "td,fd->tf", grad_branch, w_down, preferred_element_type=jnp.float32
-    )
-    grad_hidden = gelu_back(grad_activated)[0].astype(jnp.bfloat16)
-    grad_w_up = jnp.einsum(
-        "td,tf->df", own_part(normed_two), grad_hidden, preferred_element_type=jnp.float32
-    )
-    grad_bias_up = jnp.sum(grad_hidden, axis=0, dtype=jnp.float32)
-    grad_normed_two = tensor_sum(
-        jnp.einsum("tf,df->td", grad_hidden, w_up, preferred_element_type=jnp.float32)
-    )
-    grad_middle = grad_out + standard_back_two(grad_normed_two * wide(gain_two))[0]
-    grad_attended = grad_middle.astype(jnp.bfloat16)
-    grad_w_out = jnp.einsum(
-        "te,td->ed", own_part(mixed), grad_attended, preferred_element_type=jnp.float32
-    )
-    grad_mixed = jnp.einsum(
-        "td,ed->te", grad_attended, w_out, preferred_element_type=jnp.float32
-    ).astype(jnp.bfloat16)
     points = pos.shape[2]
-    width = grad_attended.shape[1]
+    width = grad_branch.shape[1]
+    used = points + 8 + w_up.shape[1] // width
     bundle = jnp.concatenate(
         [
-            jnp.zeros((points + 3, width), jnp.float32),
-            jnp.sum(grad_attended, axis=0, dtype=jnp.float32)[None],
-            jnp.sum(grad_normed_two * standard_two, axis=0)[None],
-            jnp.sum(grad_normed_two, axis=0)[None],
+            jnp.zeros((points + 6, width), jnp.float32),
             jnp.sum(grad_branch, axis=0, dtype=jnp.float32)[None],
-            jnp.zeros((1, width), jnp.float32),
-            grad_bias_up.reshape(-1, width),
+            jnp.zeros((2 * POINT_ROWS - points - 7, width), jnp.float32),
         ],
         axis=0,
     )
-    used = bundle.shape[0]
-    bundle = jnp.pad(bundle, ((0, 2 * POINT_ROWS - used), (0, 0)))
-    early = [grad_w_down, grad_w_up, grad_w_out]
     area = w_base.shape[1] // channels
     ff = w_down.shape[0]
     deep = w_up.shape[0]
@@ -1220,22 +1268,28 @@
         [(7, width, POINT_ROWS, 0, 0, 0)],
     ]
     synced, grad_embedded = back_and_sync(
-        qkv,
-        grad_mixed,
+        [
+            qkv,
+            own_part(normed_one),
+            own_part(normed_two),
+            own_part(mixed),
+            w_qkv,
+            w_out,
+            w_up,
+            w_down,
+            wide(bias_up)[None],
+            jnp.concatenate([inverse_one, inverse_two], axis=1),
+            wide(gain_one)[None],
+            wide(gain_two)[None],
+            tokens,
+            patches,
+            fine_pairs,
+            pos_fine,
+            pos,
+            bundle,
+        ],
+        [standard_one, standard_two, normed_two, grad_branch, grad_w_down],
         segment,
-        own_part(normed_one),
-        w_qkv,
-        standard_one,
-        inverse_one,
-        grad_middle,
-        wide(gain_one)[None],
-        tokens,
-        patches,
-        fine_pairs,
-        pos_fine,
-        pos,
-        bundle,
-        early,
         out_shapes,
         grads,
         outs,

time: 490 us -> 539 us (1.10)
  Pallas kernels: 309 us -> 353 us
  waiting for transfers between devices: 11.4 us -> 43.1 us
  matrix products: 45.1 us -> 20.9 us
    pallas_call x1, Pallas kernels: 258 us -> 303 us  [back_and_sync(): pl.pallas_call(kernel, out_shape=[jax.ShapeDtypeStruct(s, jnp.float32) fo...]
    ppermute x2, waiting for transfers between devices: 11.4 us -> 43.1 us  [from_partner(): direct = lax.ppermute(mine, 'dp', there)]
    dot_general x5 -> x0, matrix products: 17.6 us -> none  [the longest x1 5.67 us: local(): jnp.einsum('td,fd->tf', grad_branch, w_down, preferred_element_type=jnp.f...]
    reduce_sum x5 -> x1, other arithmetic: 14.4 us -> 4.91 us  [local(): centered = middle - jnp.mean(middle, axis=-1, keepdims=True)]
    dot_general x1, matrix products: 11.1 us -> 4.78 us  [local(): jnp.dot(normed_two, w_up, preferred_element_type=jnp.float32)]
    unnamed x138 -> x124, local copies, waits for them, and re-layouts: 30.5 us -> 31 us
  transfers between devices with their start and end apart: 7 -> 6, of which waited for: 1 -> 2; matrix products, arithmetic and copies ran while one was open for 16% -> 11% of each run, Pallas kernels for 8% -> 60%
where the time goes in v5:
time: 539 us; the launch traced here: 531 us
  Pallas kernels  353 us (65%)
  local copies, waits for them, and re-layouts  53.7 us (10%)
  other arithmetic  48.1 us (9%)
  waiting for transfers between devices  43.1 us (8%)
  matrix products  20.9 us (4%)
  between operations  6.91 us (1%)
  starting transfers between devices  5.5 us (1%)
    pallas_call x1, Pallas kernels, back_and_sync(): pl.pallas_call(kernel, out_shape=[jax.ShapeDtypeStruct(s, jnp.float32) fo...  303 us
    ppermute x2, waiting for transfers between devices, from_partner(): direct = lax.ppermute(mine, 'dp', there)  43.1 us
    unnamed x124, local copies, waits for them, and re-layouts  31 us
    pallas_call x1, Pallas kernels, embed(): pl.pallas_call(embed_kernel, out_shape=[jax.ShapeDtypeStruct((rows, width...  23.5 us
    pallas_call x1, Pallas kernels, pixel_back(): pl.pallas_call(pixel_kernel, out_shape=jax.ShapeDtypeStruct(shape, jnp.fl...  13.4 us
    pallas_call x1, Pallas kernels, attend(): pl.pallas_call(kernel, grid=(heads,), out_shape=jax.ShapeDtypeStruct((row...  13.2 us
  transfers between devices with their start and end apart: 6, of which 2 were waited for; matrix products, arithmetic and copies ran while one was open for 11% of the time, Pallas kernels for 60%

profile of v5, /device:TPU:0, one launch (start us, length us, event | category | flops | bytes accessed | tf_op | source)
XLA Modules:
  0.0 531.4 jit_solution(4074718976490783806)
XLA Ops:
  3.8 2.9 collective-permute-start
  6.8 16.6 %collective-permute-done = f32[3,240,256]{2,1,0:T(8,128)S(1)} collective-permute-done((f32[3,240,256]{2,1,0:T(8,128)}, f32[3,240,256]{2,1,0:T(8,128)S(1)}, u32[]{:S(2)}, u32[]{:S(2)}) %collective-permute-start) | collective-permute-done | bytes 737312 | tf_op jit(solution)/shard_map/ppermute | solution.py:1050
  25.5 2.7 copy.57
  36.8 2.6 compare_and_fusion
  39.4 2.8 and_select_fusion.segment.refs_1_
  45.8 3.3 pad_maximum_fusion.pix
  49.3 23.5 %embed.1 = (f32[1232,768]{1,0:T(8,128)}, bf16[3,104,3072]{2,1,0:T(8,128)(2,1)S(1)}, bf16[3,912,64]{2,1,0:T(8,128)(2,1)S(1)}, bf16[3,64,768]{2,1,0:T(8,128)(2,1)S(1)}, bf16[64,1024]{1,0:T(8,128)(2,1)S(1)}) custom-call(s32[4]{0:T(128)S(1)} %get-tuple-element.70.sizes, s32[4]{0:T(128)S(1)} %get-tuple-element.71.order, f32[4,3,240,256]{3,2,1,0:T(8,128)} %pad_maximum_fusion.pix, ...), custom_call_target="tpu_custom_call" | custom-call | tf_op jit(solution)/shard_map/embed/pallas_call | solution.py:161
  78.7 2.8 multiply_reduce_fusion.1
  84.5 2.8 fusion.8.query.key.value.refs_0_
  87.3 13.2 %attend.1 = bf16[1232,384]{1,0:T(8,128)(2,1)S(1)} custom-call(bf16[1232,1152]{1,0:T(8,128)(2,1)S(1)} %fusion.8.query.key.value.refs_0_, bf16[1232,1152]{1,0:T(8,128)(2,1)S(1)} %fusion.8.query.key.value.refs_0_, bf16[1232,1152]{1,0:T(8,128)(2,1)S(1)} %fusion.8.query.key.value.refs_0_, s32[1232,1]{1,0:T(8,128)S(1)} %and_select_fusion.segment.refs_1_, ...), custom_call_target="tpu_custom_call" | custom-call | tf_op jit(solution)/shard_map/attend/pallas_call | solution.py:286
  100.6 3.0 fusion.42
  105.9 2.7 constant_dynamic-slice_fusion
  118.9 26.5 %collective-permute-done.4 = f32[512,768]{1,0:T(8,128)} collective-permute-done((f32[512,768]{1,0:T(8,128)}, f32[512,768]{1,0:T(8,128)}, u32[]{:S(2)}, u32[]{:S(2)}) %collective-permute-start.4) | collective-permute-done | bytes 1572896 | tf_op jit(solution)/shard_map/ppermute | solution.py:1050
  145.3 4.9 fusion.39
  150.9 2.6 add_convert_fusion.1
  154.3 4.8 fusion.7
  159.1 5.0 fusion.43
  168.6 3.6 broadcast_select_fusion
  178.5 5.2 fusion.10.refs_24_
  183.7 303.1 %back_and_sync.1 = (f32[768,3072]{1,0:T(8,128)}, f32[1536,768]{1,0:T(8,128)}, f32[768,1536]{1,0:T(8,128)}, f32[768,384]{1,0:T(8,128)}, f32[768,384]{1,0:T(8,128)...) custom-call(bf16[1232,1152]{1,0:T(8,128)(2,1)} %copy-done, ...), custom_call_target="tpu_custom_call" | custom-call | tf_op jit(solution)/shard_map/back_and_sync/pallas_call | solution.py:1004
  492.7 13.4 %pixel_back.1 = f32[2,3,240,240]{3,2,1,0:T(8,128)} custom-call(s32[4]{0:T(128)S(1)} %get-tuple-element.70.sizes, s32[1]{0:T(128)S(6)} %broadcast_in_dim.192.is_fine, f32[1232,768]{1,0:T(8,128)S(1)} %copy-done.3, bf16[4,48,32]{2,1,0:T(8,128)(2,1)S(1)} %copy-done.9, bf16[768,3072]{1,0:T(8,128)(2,1)S(1)} %copy-done.1, bf16[3,64,768]{2,1,0:T(8,128)(2,1)S(1)} %copy-done.11), custom_call_target="tpu_custom_call" | custom-call | tf_op jit(solution)/shard_map/pixel_back/pallas_call | solution.py:233
  508.0 4.6 add_convert_fusion
  512.7 3.0 fusion.14
  515.8 4.8 copy.79
  (221 shorter events, 64.0 us)
Async XLA Ops:
  0.7 24.3 %copy-start.40 = (bf16[768]{0:T(1024)(128)(2,1)S(1)}, bf16[768]{0:T(1024)(128)(2,1)}, u32[]{:S(2)}) copy-start(bf16[768]{0:T(1024)(128)(2,1)} %param.34) | copy-start | bytes 4612
  0.7 24.3 %copy-start.36 = (bf16[768]{0:T(1024)(128)(2,1)S(1)}, bf16[768]{0:T(1024)(128)(2,1)}, u32[]{:S(2)}) copy-start(bf16[768]{0:T(1024)(128)(2,1)} %param.37) | copy-start | bytes 4612
  0.7 24.4 %copy-start.34 = (bf16[768]{0:T(1024)(128)(2,1)S(1)}, bf16[768]{0:T(1024)(128)(2,1)}, u32[]{:S(2)}) copy-start(bf16[768]{0:T(1024)(128)(2,1)} %param.36) | copy-start | bytes 4612
  0.7 24.4 %copy-start.32 = (bf16[768,49]{0,1:T(8,128)(2,1)S(1)}, bf16[768,49]{0,1:T(8,128)(2,1)}, u32[]{:S(2)}) copy-start(bf16[768,49]{0,1:T(8,128)(2,1)} %param.35) | copy-start | bytes 225796
  1.5 26.8 %slice-start.7 = ((bf16[31,900,49]{1,0,2:T(8,128)(2,1)}), bf16[31,100,49]{1,0,2:T(8,128)(2,1)S(1)}, s32[]{:S(2)}) async-start(bf16[31,900,49]{1,0,2:T(8,128)(2,1)} %param.32), calls=%async_computation.7 | async-start | bytes 802816 | tf_op jit(solution)/shard_map/slice | solution.py:1158
  1.5 27.7 %copy-start.42 = (bf16[384]{0:T(512)(128)(2,1)S(1)}, bf16[384]{0:T(512)(128)(2,1)}, u32[]{:S(2)}) copy-start(bf16[384]{0:T(512)(128)(2,1)} %param.42) | copy-start | bytes 2308
  1.5 27.7 %copy-start.43 = (bf16[384]{0:T(512)(128)(2,1)S(1)}, bf16[384]{0:T(512)(128)(2,1)}, u32[]{:S(2)}) copy-start(bf16[384]{0:T(512)(128)(2,1)} %param.39) | copy-start | bytes 2308
  3.8 19.6 %collective-permute-start = (f32[3,240,256]{2,1,0:T(8,128)}, f32[3,240,256]{2,1,0:T(8,128)S(1)}, u32[]{:S(2)}, u32[]{:S(2)}) collective-permute-start(f32[3,240,256]{2,1,0:T(8,128)} %dynamic-slice_bitcast_fusion), channel_id=1, source_target_pairs={{0,2},{2,0},{4,6},{6,4},{8,10},{10,8},{12,14},{14,12},{16,18},{18,... | collective-permute-start | bytes 2211848 | tf_op jit(solution)/shard_map/ppermute | solution.py:1050
  23.4 8.9 %collective-permute-start.1 = (f32[3,240,256]{2,1,0:T(8,128)S(1)}, f32[3,240,256]{2,1,0:T(8,128)}, u32[]{:S(2)}, u32[]{:S(2)}) collective-permute-start(f32[3,240,256]{2,1,0:T(8,128)S(1)} %collective-permute-done), channel_id=1, source_target_pairs={{0,1},{1,0},{2,3},{3,2},{4,5},{5,4},{6,7},{7,6},{8,9},{9,8},{10,11... | collective-permute-start | bytes 2211848 | tf_op jit(solution)/shard_map/ppermute | solution.py:1051
  25.5 23.8 %copy-start.4 = (bf16[1,900,49]{2,1,0:T(8,128)(2,1)}, bf16[1,900,49]{2,1,0:T(8,128)(2,1)S(1)}, u32[]{:S(2)}) copy-start(bf16[1,900,49]{2,1,0:T(8,128)(2,1)S(1)} %copy.64) | copy-start | bytes 264604
  42.2 45.1 %copy-start.2 = (s32[1232,1]{1,0:T(8,128)}, s32[1232,1]{1,0:T(8,128)S(1)}, u32[]{:S(2)}) copy-start(s32[1232,1]{1,0:T(8,128)S(1)} %and_select_fusion.segment.refs_1_) | copy-start | bytes 14788
  42.3 45.0 %copy-start.13 = (s32[1,320]{1,0:T(1,128)}, s32[1,320]{1,0:T(1,128)S(1)}, u32[]{:S(2)}) copy-start(s32[1,320]{1,0:T(1,128)S(1)} %broadcast_in_dim.188.segment_row.refs_2_) | copy-start | bytes 3844
  49.2 23.6 %copy-start.8 = (bf16[4,48,32]{2,1,0:T(8,128)(2,1)}, bf16[4,48,32]{2,1,0:T(8,128)(2,1)S(1)}, u32[]{:S(2)}) copy-start(bf16[4,48,32]{2,1,0:T(8,128)(2,1)S(1)} %broadcast_select_fusion.2.table) | copy-start | bytes 36868
  49.3 23.6 %copy-start.6 = (bf16[3,100,49]{2,1,0:T(8,128)(2,1)}, bf16[3,100,49]{2,1,0:T(8,128)(2,1)S(1)}, u32[]{:S(2)}) copy-start(bf16[3,100,49]{2,1,0:T(8,128)(2,1)S(1)} %broadcast_select_fusion.1.pos.refs_18_) | copy-start | bytes 88204
  103.6 41.7 %collective-permute-start.2 = (f32[1232,768]{1,0:T(8,128)}, f32[1232,768]{1,0:T(8,128)}, u32[]{:S(2)}, u32[]{:S(2)}) collective-permute-start(f32[1232,768]{1,0:T(8,128)} %fusion.42), channel_id=1, source_target_pairs={{0,1},{1,0},{2,3},{3,2},{4,5},{5,4},{6,7},{7,6},{8,9},{9,8},{10,11... | collective-permute-start | bytes 11354120 | tf_op jit(solution)/shard_map/ppermute | solution.py:1045
  108.5 36.8 %collective-permute-start.4 = (f32[512,768]{1,0:T(8,128)}, f32[512,768]{1,0:T(8,128)}, u32[]{:S(2)}, u32[]{:S(2)}) collective-permute-start(f32[512,768]{1,0:T(8,128)} %constant_dynamic-slice_fusion), channel_id=1, source_target_pairs={{0,2},{2,0},{4,6},{6,4},{8,10},{10,8},{12,14},{14,12},{16,18},{18,... | collective-permute-start | bytes 4718600 | tf_op jit(solution)/shard_map/ppermute | solution.py:1050
  145.3 23.3 %collective-permute-start.5 = (f32[512,768]{1,0:T(8,128)}, f32[512,768]{1,0:T(8,128)}, u32[]{:S(2)}, u32[]{:S(2)}) collective-permute-start(f32[512,768]{1,0:T(8,128)} %collective-permute-done.4), channel_id=1, source_target_pairs={{0,1},{1,0},{2,3},{3,2},{4,5},{5,4},{6,7},{7,6},{8,9},{9,8},{10,11... | collective-permute-start | bytes 4718600 | tf_op jit(solution)/shard_map/ppermute | solution.py:1051
  153.6 23.9 %copy-start.17 = (bf16[1232,768]{1,0:T(8,128)(2,1)}, bf16[1232,768]{1,0:T(8,128)(2,1)S(1)}, u32[]{:S(2)}) copy-start(bf16[1232,768]{1,0:T(8,128)(2,1)S(1)} %get-tuple-element.61.refs_22_) | copy-start | bytes 5677060
  164.2 343.8 %collective-permute-start.3 = (f32[1232,768]{1,0:T(8,128)}, f32[1232,768]{1,0:T(8,128)}, u32[]{:S(2)}, u32[]{:S(2)}) collective-permute-start(f32[1232,768]{1,0:T(8,128)} %fusion.43), channel_id=1, source_target_pairs={{0,1},{1,0},{2,3},{3,2},{4,5},{5,4},{6,7},{7,6},{8,9},{9,8},{10,11... | collective-permute-start | bytes 11354120 | tf_op jit(solution)/shard_map/ppermute | solution.py:1045
  183.7 304.5 %copy-start.9 = (bf16[4,48,32]{2,1,0:T(8,128)(2,1)S(1)}, bf16[4,48,32]{2,1,0:T(8,128)(2,1)}, u32[]{:S(2)}) copy-start(bf16[4,48,32]{2,1,0:T(8,128)(2,1)} %copy-done.8) | copy-start | bytes 36868
  183.7 304.5 %copy-start.11 = (bf16[3,64,768]{2,1,0:T(8,128)(2,1)S(1)}, bf16[3,64,768]{2,1,0:T(8,128)(2,1)}, u32[]{:S(2)}) copy-start(bf16[3,64,768]{2,1,0:T(8,128)(2,1)} %copy-done.10) | copy-start | bytes 884740
  492.7 13.4 %copy-start.31 = (f32[128,768]{1,0:T(8,128)S(1)}, f32[128,768]{1,0:T(8,128)}, u32[]{:S(2)}) copy-start(f32[128,768]{1,0:T(8,128)} %get-tuple-element.41) | copy-start | bytes 1179652
  492.7 15.3 %copy-start.15 = (f32[1232,768]{1,0:T(8,128)S(1)}, f32[1232,768]{1,0:T(8,128)}, u32[]{:S(2)}) copy-start(f32[1232,768]{1,0:T(8,128)} %copy-done.14) | copy-start | bytes 11354116
  492.7 23.1 %slice-start = ((s8[9437184]{0:T(1024)(128)(4,1)}), s8[1048576]{0:T(1024)(128)(4,1)S(1)}, s32[]{:S(2)}) async-start(s8[9437184]{0:T(1024)(128)(4,1)} %bitcast.36), calls=%async_computation | async-start | bytes 2097152
  (38 other events, 198.1 us)

commit v6 on v4

--- a/solution.py
+++ b/solution.py
@@ -90,22 +90,34 @@
 
 def embed_kernel(
     sizes,
-    order,
-    pix,
+    slots,
     table,
     pos_fine,
-    pos,
+    pos_all,
     weight,
     bias,
     pos_base,
+    gain,
+    shift,
+    own,
+    direct,
+    across,
     emb,
+    standard,
+    inverse,
+    normed,
     tokens,
     patches,
     mixed_weight,
     fine_pairs,
+    pos,
+    segment,
+    segment_row,
+    pix,
     line,
     pair,
     long,
+    sems,
 ):
     area = table.shape[2] ** 2
     channels, res = pix.shape[1:3]
@@ -114,17 +126,31 @@
     start = up_to(count, 16)
     stride = tokens.shape[1]
     low = jnp.bfloat16
+    copies = [
+        pltpu.make_async_copy(source, pix.at[slots[k]], sems.at[k])
+        for k, source in enumerate((own.at[0], own.at[1], direct, across))
+    ]
+    for copy in copies:
+        copy.start()
     emb[...] = jnp.broadcast_to(bias[...], emb.shape)
     tokens[...] = jnp.zeros_like(tokens)
-
-    fill_pairs(pair, long, table[0], FINE)
+    fill_pairs(pair, long, table[FINE], FINE)
     fine_pairs[...] = pair[: FINE * FINE, :].astype(low)
     emb[:count, :] += nt(pos_fine[...], pos_base[...])
-
-    @functools.partial(loop, channels, unroll=True)
-    def _(c):
-        columns = pl.ds(c * area, area)
-        patch = cut_patches(line, pix, order[0], c, FINE, grid, res)
+    for target, axis in ((segment, 0), (segment_row, 1)):
+        row = lax.broadcasted_iota(jnp.int32, target.shape, axis)
+        found = jnp.full(target.shape, 4, jnp.int32)
+        for k in range(1, 4):
+            side = res // sizes[k]
+            within = row - (k - 1) * stride
+            found = jnp.where((within >= 0) & (within < side * side), k, found)
+        target[...] = found
+    for copy in copies:
+        copy.wait()
+
+    for c in range(channels):
+        columns = slice(c * area, (c + 1) * area)
+        patch = cut_patches(line, pix, 0, c, FINE, grid, res)
         mixed = nt(fine_pairs[...], weight[:, columns]).astype(low)
         mixed_weight[c] = mixed
         patches[c, :count, :] = patch
@@ -139,54 +165,65 @@
 
             @pl.when(sizes[slot] == side)
             def _():
-                fill_pairs(pair, long, table[slot], side)
+                fill_pairs(pair, long, table[side], side)
                 here = pl.ds(row, count)
-                emb[here, :] += nt(pos[slot - 1, :count, :], pos_base[...])
-
-                @functools.partial(loop, channels, unroll=True)
-                def _(c):
-                    columns = pl.ds(c * area, area)
-                    patch = cut_patches(line, pix, order[slot], c, side, grid, res)
+                pos[slot - 1] = pos_all[grid]
+                emb[here, :] += nt(pos_all[grid, :count, :], pos_base[...])
+                for c in range(channels):
+                    columns = slice(c * area, (c + 1) * area)
+                    patch = cut_patches(line, pix, slot, c, side, grid, res)
                     token = nn(patch, pair[: side * side, :].astype(low)).astype(low)
                     tokens[slot - 1, :count, columns] = token
                     emb[here, :] += nt(token, weight[:, columns])
 
-
-def embed(sizes, order, pix, table, pos_fine, pos, w_base, patch_bias, pos_base, rows):
-    _, channels, res, _ = pix.shape
+    @pl.loop(0, emb.shape[0] // 16)
+    def _(i):
+        here = pl.ds(pl.multiple_of(i * 16, 16), 16)
+        value = emb[here, :]
+        centered = value - jnp.mean(value, axis=1, keepdims=True)
+        scale = lax.rsqrt(jnp.mean(centered * centered, axis=1, keepdims=True) + 1e-06)
+        standard[here, :] = centered * scale
+        inverse[here, :] = scale
+        normed[here, :] = (centered * scale * gain[...] + shift[...]).astype(low)
+
+
+def embed(sizes, slots, table, pos_fine, pos_all, w_base, rows_of, pos_base, pixels, rows):
+    own = pixels[0]
+    _, channels, res, lanes = own.shape
     width, features = w_base.shape
     fine = (res // FINE) ** 2
     side = table.shape[1]
     area = features // channels
+    stride = pos_all.shape[1]
+    rest = rows - up_to(fine, 16)
+    shape = jax.ShapeDtypeStruct
     return pl.pallas_call(
         embed_kernel,
         out_shape=[
-            jax.ShapeDtypeStruct((rows, width), jnp.float32),
-            jax.ShapeDtypeStruct((3, up_to(pos.shape[1], 8), features), jnp.bfloat16),
-            jax.ShapeDtypeStruct((channels, up_to(fine, 16), FINE * FINE), jnp.bfloat16),
-            jax.ShapeDtypeStruct((channels, FINE * FINE, width), jnp.bfloat16),
-            jax.ShapeDtypeStruct((FINE * FINE, area), jnp.bfloat16),
+            shape((rows, width), jnp.float32),
+            shape((rows, width), jnp.float32),
+            shape((rows, 1), jnp.float32),
+            shape((rows, width), jnp.bfloat16),
+            shape((3, stride, features), jnp.bfloat16),
+            shape((channels, up_to(fine, 16), FINE * FINE), jnp.bfloat16),
+            shape((channels, FINE * FINE, width), jnp.bfloat16),
+            shape((FINE * FINE, area), jnp.bfloat16),
+            shape((3,) + pos_all.shape[1:], jnp.bfloat16),
+            shape((rest, 1), jnp.int32),
+            shape((1, rest), jnp.int32),
         ],
-        in_specs=[SMEM] * 2 + [VMEM] * 7,
-        out_specs=[VMEM] * 5,
+        in_specs=[SMEM] * 2 + [VMEM] * 8 + [pl.BlockSpec(memory_space=pl.ANY)] * 3,
+        out_specs=[VMEM] * 11,
         scratch_shapes=[
+            pltpu.VMEM((4, channels, res, lanes), jnp.float32),
             pltpu.VMEM((res * res // FINE, 128), jnp.float32),
             pltpu.VMEM((side * side, area), jnp.float32),
             pltpu.VMEM((side, area), jnp.float32),
+            pltpu.SemaphoreType.DMA((4,)),
         ],
-        compiler_params=pltpu.CompilerParams(vmem_limit_bytes=48 << 20),
+        compiler_params=pltpu.CompilerParams(vmem_limit_bytes=56 << 20),
         name="embed",
-    )(
-        sizes,
-        order,
-        pix,
-        table,
-        pos_fine,
-        pos,
-        w_base,
-        patch_bias.astype(jnp.float32)[None],
-        pos_base,
-    )
+    )(sizes, slots, table, pos_fine, pos_all, w_base, rows_of[0], pos_base, *rows_of[1:], *pixels)
 
 
 def pixel_kernel(sizes, is_fine, grad, table, weight, mixed_weight, pixel_grad, line, pair, long):
@@ -215,7 +252,7 @@
 
             @pl.when((sizes[slot] == side) & (wanted == 1))
             def _():
-                fill_pairs(pair, long, table[slot], side)
+                fill_pairs(pair, long, table[side], side)
                 rows = grad[pl.ds(row, count), :].astype(low)
 
                 @pl.loop(0, channels)
@@ -267,7 +304,7 @@
 
 def block_masks(fine, start, rows, segment, segment_row, axis):
     inside = lax.broadcasted_iota(jnp.int32, (start, start), axis) < fine
-    same = segment[start:rows, :] == segment_row[:, : rows - start]
+    same = segment[...] == segment_row[...]
     return inside, same
 
 
@@ -278,7 +315,7 @@
         mixed[here, :] = attend_block(scale, query[here, :], key[here, :], value[here, :], mask)
 
 
-def attend(qkv, segment, fine, start):
+def attend(qkv, segment, segment_row, fine, start):
     rows, width = qkv.shape
     heads = width // 3 // PAIR
     kernel = functools.partial(attend_kernel, 1.0 / math.sqrt(HD), fine, start)
@@ -291,13 +328,13 @@
             column(0),
             column(1),
             column(2),
-            pl.BlockSpec((rows, 1), lambda j: (0, 0)),
+            pl.BlockSpec((rows - start, 1), lambda j: (0, 0)),
             pl.BlockSpec((1, rows - start), lambda j: (0, 0)),
         ],
         out_specs=column(0),
         compiler_params=pltpu.CompilerParams(vmem_limit_bytes=48 << 20),
         name="attend",
-    )(qkv, qkv, qkv, segment[:, None], segment[None, start:])
+    )(qkv, qkv, qkv, segment, segment_row)
 
 
 def attend_back_block(scale, query, key, value, grad_mixed, mask):
@@ -323,7 +360,7 @@
 MESH_ID = pl.DeviceIdType.MESH
 PIECE_ROWS = 192
 PIECE_COLS = 384
-CROSS_EVERY = 4
+CROSS_EVERY = 3
 SEMS = 48
 
 
@@ -644,7 +681,7 @@
                 line[tick - j]()
 
 
-GROUP = 1
+GROUP = 2
 AHEAD = 1
 
 
@@ -678,6 +715,7 @@
 
 
 QUERY_BLOCK = 384
+FIRST_TICKS = 8
 LN_ROWS = 112
 POINT_ROWS = 64
 
@@ -767,7 +805,7 @@
         def coarse_job(pair):
             def job():
                 here = slice(start, rows)
-                same = segment[here, :] == segment_row[...]
+                same = segment[...] == segment_row[...]
                 for k, value in enumerate(back_rows(pair, here, here, same)):
                     store_qkv(pair, k, here, value)
 
@@ -859,11 +897,14 @@
             bundle[points + 7 : points + 8, :third] = sums[:, :third]
             bundle[points + 7 : points + 8, third : 2 * third] = sums[:, 2 * third :]
 
-        jobs = []
+        heads = []
         for pair in range(third // PAIR):
-            jobs += [[fine_job(pair, begin)] for begin in range(0, start, QUERY_BLOCK)]
-            jobs[-1].append(coarse_job(pair))
-        return jobs + [[partial_job], [weight_job], [norm_job], [base_job], [bundle_job]]
+            heads += [fine_job(pair, begin) for begin in range(0, start, QUERY_BLOCK)]
+            heads.append(coarse_job(pair))
+        ticks = FIRST_TICKS
+        parts = [heads[len(heads) * k // ticks : len(heads) * (k + 1) // ticks] for k in range(ticks)]
+        parts[-1] = parts[-1] + [weight_job]
+        return parts + [[partial_job], [norm_job], [base_job], [bundle_job]]
 
     move_pieces(
         pieces,
@@ -883,6 +924,7 @@
     qkv,
     grad_mixed,
     segment,
+    segment_row,
     normed_part,
     w_qkv,
     standard,
@@ -950,8 +992,8 @@
     )(
         qkv,
         grad_mixed,
-        segment[:, None],
-        segment[None, start:],
+        segment,
+        segment_row,
         normed_part,
         w_qkv,
         standard,
@@ -973,16 +1015,12 @@
     return partial + lax.ppermute(partial, "tensor", [(0, 1), (1, 0)])
 
 
-def from_partner(mine, core, replicas):
-    there = [(i, i ^ 1) for i in range(replicas)]
-    direct = lax.ppermute(mine, "dp", there)
-    across = lax.ppermute(direct, "tensor", [(0, 1), (1, 0)])
-    return direct, across
+def swap_cores(value):
+    return lax.ppermute(value, "tensor", [(0, 1), (1, 0)])
 
 
 def merged_rows(fine_rows, light_rows, second, counts, start, stride, rows):
     width = fine_rows.shape[1]
-    small = stride - stride % 4
     keep = jnp.arange(stride, dtype=jnp.int32)[:, None]
     fine = fine_rows.shape[0]
     padded = jnp.pad(light_rows, ((0, stride), (0, 0)))
@@ -1057,59 +1095,66 @@
     stride = up_to(small, 8)
     rows = up_to(start + 3 * stride, 16)
 
-    lane = jnp.arange(up_to(res, 128), dtype=jnp.int32)
+    there = [(i, i ^ 1) for i in range(replicas)]
+    other_sizes = lax.ppermute(patch_size, "dp", there)
     own_pix = jnp.pad(wide(pixels), ((0, 0), (0, 0), (0, 0), (0, -res % 128)))
-    own_pix = jnp.where(lane == res, wide(patch_size)[:, None, None, None], own_pix)
-    direct, across = from_partner(
-        lax.dynamic_index_in_dim(own_pix, core, 0, keepdims=False), core, replicas
-    )
-    pix = jnp.concatenate([own_pix, direct[None], across[None]], axis=0)
+    direct = lax.ppermute(
+        lax.dynamic_index_in_dim(own_pix, core, 0, keepdims=False), "dp", there
+    )
     half_rows = rows_total // 2
     own_cotangent = wide(cotangent)
-    cot_direct, cot_across = from_partner(
-        lax.dynamic_slice_in_dim(own_cotangent, core * half_rows, half_rows, axis=0),
-        core,
-        replicas,
-    )
-    is_fine = patch_size[0] == FINE
-    other = jnp.where(core == 0, jnp.array([2, 3], jnp.int32), jnp.array([3, 2], jnp.int32))
-    order = jnp.where(
-        is_fine,
-        jnp.concatenate([jnp.array([0, 1], jnp.int32), other]),
-        jnp.concatenate([other, jnp.array([0, 1], jnp.int32)]),
-    )
-    found = jnp.concatenate([patch_size, jnp.stack([direct[0, 0, res], across[0, 0, res]]).astype(jnp.int32)])
-    sizes = jnp.take(found, order)
-    counts4 = (res // sizes) ** 2
-    table = jnp.take(resize_table, sizes, axis=0)
-    pos_fine = pos_table[res // FINE, :fine]
-    pos = jnp.take(pos_table[:, :small], res // sizes[1:], axis=0)
-
-    row = jnp.arange(rows, dtype=jnp.int32)
-    slot = jnp.where(row < start, 0, (row - start) // stride + 1)
-    first = jnp.where(slot == 0, 0, start + (slot - 1) * stride)
-    limit = jnp.where(
-        slot == 0,
-        counts4[0],
-        jnp.where(slot == 1, counts4[1], jnp.where(slot == 2, counts4[2], counts4[3])),
-    )
-    valid = (slot < 4) & (row - first < limit)
-    segment = jnp.where(valid, slot, 4)
-    valid_rows = wide(valid)[:, None]
-
-    embedded, tokens, patches, mixed_weight, fine_pairs = embed(
-        sizes, order, pix, table, pos_fine, pos, w_base, patch_bias, pos_base, rows
-    )
+    cot_half = lax.dynamic_slice_in_dim(own_cotangent, core * half_rows, half_rows, axis=0)
     w_qkv = jnp.concatenate([w_query, w_key, w_value], axis=1)
     bias_qkv = jnp.concatenate([bias_query, jnp.zeros_like(bias_query), bias_value])
-    centered = embedded - jnp.mean(embedded, axis=-1, keepdims=True)
-    inverse_one = lax.rsqrt(jnp.mean(centered * centered, axis=-1, keepdims=True) + 1e-06)
-    standard_one = centered * inverse_one
-    normed_one = (standard_one * wide(gain_one) + wide(shift_one)).astype(jnp.bfloat16)
+    pos_fine = pos_table[res // FINE, :fine]
+    pos_coarse = pos_table[:, :stride]
+    direct, other_sizes, cot_half, w_qkv, bias_qkv, pos_fine, pos_coarse = (
+        lax.optimization_barrier(
+            (direct, other_sizes, cot_half, w_qkv, bias_qkv, pos_fine, pos_coarse)
+        )
+    )
+    across = swap_cores(direct)
+    cot_direct = lax.ppermute(cot_half, "dp", there)
+    cot_across = swap_cores(cot_direct)
+    is_fine = patch_size[0] == FINE
+    fine_first = is_fine.astype(jnp.int32)
+    sizes = jnp.where(
+        is_fine,
+        jnp.concatenate([patch_size, other_sizes]),
+        jnp.concatenate([other_sizes, patch_size]),
+    )
+    slots = jnp.stack([0 * core, 0 * core + 1, core, 1 - core]) + 2 * jnp.stack(
+        [1 - fine_first] * 2 + [fine_first] * 2
+    )
+    counts4 = (res // sizes) ** 2
+    (
+        embedded,
+        standard_one,
+        inverse_one,
+        normed_one,
+        tokens,
+        patches,
+        mixed_weight,
+        fine_pairs,
+        pos,
+        segment,
+        segment_row,
+    ) = embed(
+        sizes,
+        slots,
+        resize_table,
+        pos_fine,
+        pos_coarse,
+        w_base,
+        [wide(patch_bias)[None], wide(gain_one)[None], wide(shift_one)[None]],
+        pos_base,
+        [own_pix, direct, across],
+        rows,
+    )
     qkv = (
         jnp.dot(normed_one, w_qkv, preferred_element_type=jnp.float32) + wide(bias_qkv)
     ).astype(jnp.bfloat16)
-    mixed = attend(qkv, segment, fine, start)
+    mixed = attend(qkv, segment, segment_row, fine, start)
     attended = tensor_sum(jnp.dot(mixed, w_out, preferred_element_type=jnp.float32)) + wide(
         bias_out
     )
@@ -1144,7 +1189,6 @@
             stride,
             rows,
         )
-        * valid_rows
     )
     grad_branch = grad_out.astype(jnp.bfloat16)
     own_part = lambda value: lax.dynamic_slice_in_dim(
@@ -1223,6 +1267,7 @@
         qkv,
         grad_mixed,
         segment,
+        segment_row,
         own_part(normed_one),
         w_qkv,
         standard_one,
@@ -1253,7 +1298,7 @@
         sizes,
         is_fine.astype(jnp.int32)[None],
         grad_embedded,
-        table,
+        resize_table,
         w_base,
         mixed_weight,
         pixels.shape,

time: 490 us -> 498 us (1.016)
  Pallas kernels: 309 us -> 340 us
  other arithmetic: 50.9 us -> 33.2 us
  local copies, waits for them, and re-layouts: 54.5 us -> 47.2 us
    pallas_call x1, Pallas kernels: 25 us -> 51.3 us  [embed(): pl.pallas_call(embed_kernel, out_shape=[shape((rows, width), jnp.float32)...]
    dot_general x1, matrix products: 5.67 us -> 11.5 us  [local(): jnp.einsum('td,fd->tf', grad_branch, w_down, preferred_element_type=jnp.f...]
    reduce_sum x3 -> x0, other arithmetic: 5.48 us -> none  [the longest x1 2.77 us: local(): jnp.mean(centered * centered, axis=-1, keepdims=True) + 1e-06]
    pallas_call x1, Pallas kernels: 258 us -> 263 us  [back_and_sync(): pl.pallas_call(kernel, out_shape=[jax.ShapeDtypeStruct(s, jnp.float32) fo...]
    unnamed x138 -> x109, local copies, waits for them, and re-layouts: 30.5 us -> 27.2 us
    ppermute x4 -> x5, waiting for transfers between devices: 11.4 us -> 9.98 us  [the longest x1 5.24 us: local(): other_sizes = lax.ppermute(patch_size, 'dp', there)]
  transfers between devices with their start and end apart: 7 -> 8, of which waited for: 1 -> 2; matrix products, arithmetic and copies ran while one was open for 16% -> 11% of each run, Pallas kernels for 8% -> 13%
where the time goes in v6:
time: 498 us; the launch traced here: 490 us
  Pallas kernels  340 us (68%)
  matrix products  47.5 us (10%)
  local copies, waits for them, and re-layouts  47.2 us (9%)
  other arithmetic  33.2 us (7%)
  waiting for transfers between devices  9.99 us (2%)
  between operations  6.93 us (1%)
  starting transfers between devices  5.8 us (1%)
    pallas_call x1, Pallas kernels, back_and_sync(): pl.pallas_call(kernel, out_shape=[jax.ShapeDtypeStruct(s, jnp.float32) fo...  263 us
    pallas_call x1, Pallas kernels, embed(): pl.pallas_call(embed_kernel, out_shape=[shape((rows, width), jnp.float32)...  51.3 us
    unnamed x109, local copies, waits for them, and re-layouts  27.2 us
    pallas_call x1, Pallas kernels, attend(): pl.pallas_call(kernel, grid=(heads,), out_shape=jax.ShapeDtypeStruct((row...  13.2 us
    pallas_call x1, Pallas kernels, pixel_back(): pl.pallas_call(pixel_kernel, out_shape=jax.ShapeDtypeStruct(shape, jnp.fl...  12.4 us
    dot_general x1, matrix products, local(): jnp.einsum('td,fd->tf', grad_branch, w_down, preferred_element_type=jnp.f...  11.5 us
  transfers between devices with their start and end apart: 8, of which 2 were waited for; matrix products, arithmetic and copies ran while one was open for 11% of the time, Pallas kernels for 13%

profile of v6, /device:TPU:0, one launch (start us, length us, event | category | flops | bytes accessed | tf_op | source)
XLA Modules:
  0.0 490.5 jit_solution(42779521460050363)
XLA Ops:
  3.0 2.9 collective-permute-start
  9.7 3.4 convert_element_type.78
  13.2 2.7 constant_dynamic-slice_fusion.1
  17.5 5.2 %collective-permute-done.1 = s32[2]{0:T(128)S(1)} collective-permute-done((s32[2]{0:T(128)}, s32[2]{0:T(128)S(1)}, u32[]{:S(2)}, u32[]{:S(2)}) %collective-permute-start.1) | collective-permute-done | bytes 40 | tf_op jit(solution)/shard_map/ppermute | solution.py:1099
  30.8 51.3 %embed.1 = (f32[1232,768]{1,0:T(8,128)}, f32[1232,768]{1,0:T(8,128)}, f32[1232,1]{1,0:T(8,128)}, bf16[1232,768]{1,0:T(8,128)(2,1)}, bf16[3,104,3072]{2,1,0:T(8,1...) custom-call(s32[4]{0:T(128)} %get-tuple-element.96.sizes, ...), custom_call_target="tpu_custom_call" | custom-call | tf_op jit(solution)/shard_map/embed/pallas_call | solution.py:200
  82.2 4.2 fusion.7.query.key.value.refs_0_
  86.4 13.2 %attend.1 = bf16[1232,384]{1,0:T(8,128)(2,1)S(1)} custom-call(bf16[1232,1152]{1,0:T(8,128)(2,1)S(1)} %fusion.7.query.key.value.refs_0_, bf16[1232,1152]{1,0:T(8,128)(2,1)S(1)} %fusion.7.query.key.value.refs_0_, bf16[1232,1152]{1,0:T(8,128)(2,1)S(1)} %fusion.7.query.key.value.refs_0_, s32[320,1]{1,0:T(8,128)S(1)} %copy-done.5, s32[1,320]{1,0:T(1,128)S(1)} %copy-done.7), custom_call_target="tpu_custom_call" | custom-call | tf_op jit(solution)/shard_map/attend/pallas_call | solution.py:323
  99.6 3.0 fusion.37
  107.1 4.7 collective-permute-done.6
  111.8 3.6 broadcast_select_fusion
  117.7 4.8 fusion.34
  125.5 6.5 %multiply_convert_fusion = (bf16[1232,1536]{1,0:T(8,128)(2,1)S(1)}, f32[1232,1536]{1,0:T(8,128)}) fusion(f32[1536]{0:T(1024)S(1)} %convert_element_type.86, bf16[1232,768]{1,0:T(8,128)(2,1)S(1)} %add_convert_fusion.1, bf16[768,1536]{1,0:T(8,128)(2,1)S(1)} %copy-done.40), kind=kOutput, calls=%fused_computation.12 | convolution fusion | flops 2925576192 | bytes 15611904 | tf_op jit(solution)/shard_map/dot_general | solution.py:1164
  132.0 11.5 %convert_reduce_fusion = (f32[1536]{0:T(1024)S(1)}, bf16[1232,1536]{1,0:T(8,128)(2,1)S(1)}) fusion(f32[1232,1536]{1,0:T(8,128)} %get-tuple-element.106, bf16[1536,768]{1,0:T(8,128)(2,1)S(1)} %copy-done.41, f32[1232,768]{1,0:T(8,128)S(1)} %broadcast_dynamic-update-slice_fusion), kind=kOutput, calls=%fused_computation.11 | convolution fusion | flops 2949229056 | bytes 17504256 | tf_op jit(solution)/shard_map/td,fd->tf/dot_general | solution.py:1200
  143.5 5.0 %fusion.39 = f32[1232,768]{1,0:T(8,128)} fusion(bf16[1232,1536]{1,0:T(8,128)(2,1)S(1)} %get-tuple-element.108, bf16[768,1536]{1,0:T(8,128)(2,1)S(1)} %copy-done.40), kind=kOutput, calls=%fused_computation.91 | convolution fusion | flops 2906652672 | bytes 9928704 | tf_op jit(solution)/shard_map/tf,df->td/dot_general | solution.py:1209
  148.7 4.9 %fusion.38 = f32[1232,768]{1,0:T(8,128)} fusion(bf16[1232,1536]{1,0:T(8,128)(2,1)S(1)} %get-tuple-element.105, bf16[1536,768]{1,0:T(8,128)(2,1)S(1)} %copy-done.41), kind=kOutput, calls=%fused_computation.90 | convolution fusion | flops 2906652672 | bytes 9928704 | tf_op jit(solution)/shard_map/dot_general | solution.py:1167
  160.2 5.4 %fusion.14.refs_17_ = f32[384,1536]{1,0:T(8,128)} fusion(bf16[1232,1536]{1,0:T(8,128)(2,1)} %copy-done.44, bf16[1232,768]{1,0:T(8,128)(2,1)S(1)} %add_convert_fusion.1, s32[]{:T(128)S(6)} %select_n.101), kind=kOutput, calls=%fused_computation.37 | convolution fusion | flops 1453326336 | bytes 7090180 | tf_op jit(solution)/shard_map/td,tf->df/dot_general | solution.py:1204
  165.6 3.2 fusion.9.refs_16_
  168.8 4.3 multiply_reduce_fusion
  173.1 4.5 fusion.33
  185.0 263.0 %back_and_sync.1 = (f32[768,3072]{1,0:T(8,128)}, f32[1536,768]{1,0:T(8,128)}, f32[768,1536]{1,0:T(8,128)}, f32[768,384]{1,0:T(8,128)}, f32[768,384]{1,0:T(8,128)...) custom-call(bf16[1232,1152]{1,0:T(8,128)(2,1)} %copy-done.1, ...), custom_call_target="tpu_custom_call" | custom-call | tf_op jit(solution)/shard_map/back_and_sync/pallas_call | solution.py:960
  459.5 12.4 %pixel_back.1 = f32[2,3,240,240]{3,2,1,0:T(8,128)} custom-call(s32[4]{0:T(128)S(1)} %copy-done.8, s32[1]{0:T(128)} %bitcast.9.is_fine, f32[1232,768]{1,0:T(8,128)S(1)} %copy-done.4, bf16[49,48,32]{2,1,0:T(8,128)(2,1)S(1)} %copy-done.3, bf16[768,3072]{1,0:T(8,128)(2,1)S(1)} %copy-done.2, bf16[3,64,768]{2,1,0:T(8,128)(2,1)S(1)} %copy-done.6), custom_call_target="tpu_custom_call" | custom-call | tf_op jit(solution)/shard_map/pixel_back/pallas_call | solution.py:270
  471.9 2.8 fusion.13
  474.8 4.8 copy.61
  484.3 2.4 copy.66
  (180 shorter events, 53.7 us)
Async XLA Ops:
  0.7 98.9 %copy-start = (bf16[384,768]{1,0:T(8,128)(2,1)S(1)}, bf16[384,768]{1,0:T(8,128)(2,1)}, u32[]{:S(2)}) copy-start(bf16[384,768]{1,0:T(8,128)(2,1)} %param.39) | copy-start | bytes 1769476
  3.0 19.7 %collective-permute-start = (f32[3,240,256]{2,1,0:T(8,128)}, f32[3,240,256]{2,1,0:T(8,128)S(1)}, u32[]{:S(2)}, u32[]{:S(2)}) collective-permute-start(f32[3,240,256]{2,1,0:T(8,128)} %dynamic-slice_bitcast_fusion), channel_id=1, source_target_pairs={{0,2},{2,0},{4,6},{6,4},{8,10},{10,8},{12,14},{14,12},{16,18},{18,... | collective-permute-start | bytes 2211848 | tf_op jit(solution)/shard_map/ppermute | solution.py:1101
  6.0 16.8 %collective-permute-start.1 = (s32[2]{0:T(128)}, s32[2]{0:T(128)S(1)}, u32[]{:S(2)}, u32[]{:S(2)}) collective-permute-start(s32[2]{0:T(128)} %param.26), channel_id=1, source_target_pairs={{0,2},{2,0},{4,6},{6,4},{8,10},{10,8},{12,14},{14,12},{16,18},{18,... | collective-permute-start | bytes 32 | tf_op jit(solution)/shard_map/ppermute | solution.py:1099
  13.1 12.6 %copy-start.34 = (bf16[768]{0:T(1024)(128)(2,1)S(1)}, bf16[768]{0:T(1024)(128)(2,1)}, u32[]{:S(2)}) copy-start(bf16[768]{0:T(1024)(128)(2,1)} %param.30) | copy-start | bytes 4612
  13.1 13.2 %copy-start.35 = (bf16[768]{0:T(1024)(128)(2,1)S(1)}, bf16[768]{0:T(1024)(128)(2,1)}, u32[]{:S(2)}) copy-start(bf16[768]{0:T(1024)(128)(2,1)} %param.33) | copy-start | bytes 4612
  13.2 13.8 %copy-start.27 = (bf16[768,49]{0,1:T(8,128)(2,1)S(1)}, bf16[768,49]{0,1:T(8,128)(2,1)}, u32[]{:S(2)}) copy-start(bf16[768,49]{0,1:T(8,128)(2,1)} %param.31) | copy-start | bytes 225796
  17.5 64.6 %copy-start.16 = (bf16[768,1152]{1,0:T(8,128)(2,1)}, bf16[768,1152]{1,0:T(8,128)(2,1)S(1)}, u32[]{:S(2)}) copy-start(bf16[768,1152]{1,0:T(8,128)(2,1)S(1)} %pad_maximum_fusion.refs_5_) | copy-start | bytes 5308420
  22.7 8.1 %collective-permute-start.2 = (f32[3,240,256]{2,1,0:T(8,128)S(1)}, f32[3,240,256]{2,1,0:T(8,128)}, u32[]{:S(2)}, u32[]{:S(2)}) collective-permute-start(f32[3,240,256]{2,1,0:T(8,128)S(1)} %collective-permute-done.direct), channel_id=1, source_target_pairs={{0,1},{1,0},{2,3},{3,2},{4,5},{5,4},{6,7},{7,6},{8,9},{9,8},{10,11... | collective-permute-start | bytes 2211848 | tf_op jit(solution)/shard_map/ppermute | solution.py:1019
  22.8 80.1 %collective-permute-start.5 = (f32[512,768]{1,0:T(8,128)}, f32[512,768]{1,0:T(8,128)}, u32[]{:S(2)}, u32[]{:S(2)}) collective-permute-start(f32[512,768]{1,0:T(8,128)} %constant_dynamic-slice_fusion.1), channel_id=1, source_target_pairs={{0,2},{2,0},{4,6},{6,4},{8,10},{10,8},{12,14},{14,12},{16,18},{18,... | collective-permute-start | bytes 4718600 | tf_op jit(solution)/shard_map/ppermute | solution.py:1117
  86.3 13.2 %copy-start.1 = (bf16[1232,1152]{1,0:T(8,128)(2,1)}, bf16[1232,1152]{1,0:T(8,128)(2,1)S(1)}, u32[]{:S(2)}) copy-start(bf16[1232,1152]{1,0:T(8,128)(2,1)S(1)} %fusion.7.query.key.value.refs_0_) | copy-start | bytes 8515588
  99.6 12.2 %copy-start.17 = (bf16[1024,768]{1,0:T(8,128)(2,1)S(1)}, bf16[1024,768]{1,0:T(8,128)(2,1)}, u32[]{:S(2)}) copy-start(bf16[1024,768]{1,0:T(8,128)(2,1)} %param.47) | copy-start | bytes 4718596
  102.7 14.7 %collective-permute-start.3 = (f32[1232,768]{1,0:T(8,128)}, f32[1232,768]{1,0:T(8,128)}, u32[]{:S(2)}, u32[]{:S(2)}) collective-permute-start(f32[1232,768]{1,0:T(8,128)} %fusion.37), channel_id=1, source_target_pairs={{0,1},{1,0},{2,3},{3,2},{4,5},{5,4},{6,7},{7,6},{8,9},{9,8},{10,11... | collective-permute-start | bytes 11354120 | tf_op jit(solution)/shard_map/ppermute | solution.py:1015
  102.9 8.9 %collective-permute-start.6 = (f32[512,768]{1,0:T(8,128)}, f32[512,768]{1,0:T(8,128)}, u32[]{:S(2)}, u32[]{:S(2)}) collective-permute-start(f32[512,768]{1,0:T(8,128)} %collective-permute-done.5), channel_id=1, source_target_pairs={{0,1},{1,0},{2,3},{3,2},{4,5},{5,4},{6,7},{7,6},{8,9},{9,8},{10,11... | collective-permute-start | bytes 4718600 | tf_op jit(solution)/shard_map/ppermute | solution.py:1019
  117.3 14.7 %copy-start.12 = (f32[1232,768]{1,0:T(8,128)}, f32[1232,768]{1,0:T(8,128)S(1)}, u32[]{:S(2)}) copy-start(f32[1232,768]{1,0:T(8,128)S(1)} %broadcast_dynamic-update-slice_fusion) | copy-start | bytes 11354116
  132.0 16.8 %copy-start.42 = (bf16[1232,1536]{1,0:T(8,128)(2,1)}, bf16[1232,1536]{1,0:T(8,128)(2,1)S(1)}, u32[]{:S(2)}) copy-start(bf16[1232,1536]{1,0:T(8,128)(2,1)S(1)} %get-tuple-element.105) | copy-start | bytes 11354116
  148.5 20.3 %collective-permute-start.7 = (f32[1232,768]{1,0:T(8,128)}, f32[1232,768]{1,0:T(8,128)}, u32[]{:S(2)}, u32[]{:S(2)}) collective-permute-start(f32[1232,768]{1,0:T(8,128)} %fusion.39), channel_id=1, source_target_pairs={{0,1},{1,0},{2,3},{3,2},{4,5},{5,4},{6,7},{7,6},{8,9},{9,8},{10,11... | collective-permute-start | bytes 11354120 | tf_op jit(solution)/shard_map/ppermute | solution.py:1015
  153.7 19.4 %collective-permute-start.4 = (f32[1232,768]{1,0:T(8,128)}, f32[1232,768]{1,0:T(8,128)}, u32[]{:S(2)}, u32[]{:S(2)}) collective-permute-start(f32[1232,768]{1,0:T(8,128)} %fusion.38), channel_id=1, source_target_pairs={{0,1},{1,0},{2,3},{3,2},{4,5},{5,4},{6,7},{7,6},{8,9},{9,8},{10,11... | collective-permute-start | bytes 11354120 | tf_op jit(solution)/shard_map/ppermute | solution.py:1015
  185.0 269.0 %copy-start.6 = (bf16[3,64,768]{2,1,0:T(8,128)(2,1)S(1)}, bf16[3,64,768]{2,1,0:T(8,128)(2,1)}, u32[]{:S(2)}) copy-start(bf16[3,64,768]{2,1,0:T(8,128)(2,1)} %get-tuple-element.65.mixed_weight) | copy-start | bytes 884740
  185.0 269.0 %copy-start.8 = (s32[4]{0:T(128)S(1)}, s32[4]{0:T(128)}, u32[]{:S(2)}) copy-start(s32[4]{0:T(128)} %get-tuple-element.96.sizes) | copy-start | bytes 52
  451.7 20.1 %copy-start.25 = (bf16[104,768]{1,0:T(8,128)(2,1)S(1)}, bf16[104,768]{1,0:T(8,128)(2,1)}, u32[]{:S(2)}) copy-start(bf16[104,768]{1,0:T(8,128)(2,1)} %get-tuple-element.99) | copy-start | bytes 479236
  451.7 20.1 %copy-start.26 = (bf16[104,768]{1,0:T(8,128)(2,1)S(1)}, bf16[104,768]{1,0:T(8,128)(2,1)}, u32[]{:S(2)}) copy-start(bf16[104,768]{1,0:T(8,128)(2,1)} %get-tuple-element.100) | copy-start | bytes 479236
  459.5 12.4 %copy-start.18 = (bf16[900,768]{1,0:T(8,128)(2,1)S(1)}, bf16[900,768]{1,0:T(8,128)(2,1)}, u32[]{:S(2)}) copy-start(bf16[900,768]{1,0:T(8,128)(2,1)} %slice.123) | copy-start | bytes 4147204
  459.5 15.3 %copy-start.14 = (f32[768,3072]{1,0:T(8,128)S(1)}, f32[768,3072]{1,0:T(8,128)}, u32[]{:S(2)}) copy-start(f32[768,3072]{1,0:T(8,128)} %get-tuple-element.133) | copy-start | bytes 28311556
  471.9 12.4 %slice-start.2 = ((s8[4718592]{0:T(1024)(128)(4,1)}), s8[524288]{0:T(1024)(128)(4,1)S(1)}, s32[]{:S(2)}) async-start(s8[4718592]{0:T(1024)(128)(4,1)} %bitcast.29), calls=%async_computation.2 | async-start | bytes 1048576
  (34 other events, 180.9 us)

commit v7 on v6

--- a/solution.py
+++ b/solution.py
@@ -21,6 +21,7 @@
 
 FINE = 8
 COARSE = (24, 30, 40, 48)
+NORM_ROWS = 112
 
 
 def nt(left, right):
@@ -176,9 +177,9 @@
                     tokens[slot - 1, :count, columns] = token
                     emb[here, :] += nt(token, weight[:, columns])
 
-    @pl.loop(0, emb.shape[0] // 16)
+    @pl.loop(0, emb.shape[0] // NORM_ROWS)
     def _(i):
-        here = pl.ds(pl.multiple_of(i * 16, 16), 16)
+        here = pl.ds(pl.multiple_of(i * NORM_ROWS, 16), NORM_ROWS)
         value = emb[here, :]
         centered = value - jnp.mean(value, axis=1, keepdims=True)
         scale = lax.rsqrt(jnp.mean(centered * centered, axis=1, keepdims=True) + 1e-06)
@@ -848,24 +849,18 @@
                 for copy in chunk_copies(number):
                     copy.wait()
                 at = lax.rem(number, 2)
-
-                @pl.loop(0, LN_ROWS // 16)
-                def _(i):
-                    inner = pl.ds(pl.multiple_of(i * 16, 8), 16)
-                    here = pl.ds(pl.multiple_of(number * LN_ROWS + i * 16, 8), 16)
-                    grad = partial[here, :] + arrived[here, :]
-                    z = chunk_standard[at, inner, :]
-                    up = grad * gain[...]
-                    mean = jnp.mean(up, axis=1, keepdims=True)
-                    along = jnp.mean(up * z, axis=1, keepdims=True)
-                    value = (
-                        chunk_middle[at, inner, :] + (up - mean - z * along) * inverse[here, :]
-                    )
-                    grad_embedded[here, :] = value
-                    column = lambda v: jnp.sum(v, axis=0, keepdims=True)
-                    bundle[points : points + 1, :] += column(low(value).astype(jnp.float32))
-                    bundle[points + 1 : points + 2, :] += column(grad * z)
-                    bundle[points + 2 : points + 3, :] += column(grad)
+                here = pl.ds(pl.multiple_of(number * LN_ROWS, 16), LN_ROWS)
+                grad = partial[here, :] + arrived[here, :]
+                z = chunk_standard[at]
+                up = grad * gain[...]
+                mean = jnp.mean(up, axis=1, keepdims=True)
+                along = jnp.mean(up * z, axis=1, keepdims=True)
+                value = chunk_middle[at] + (up - mean - z * along) * inverse[here, :]
+                grad_embedded[here, :] = value
+                column = lambda v: jnp.sum(v, axis=0, keepdims=True)
+                bundle[points : points + 1, :] += column(low(value).astype(jnp.float32))
+                bundle[points + 1 : points + 2, :] += column(grad * z)
+                bundle[points + 2 : points + 3, :] += column(grad)
 
         def base_job():
             half = grad_w_base.shape[0]
@@ -1115,7 +1110,6 @@
     )
     across = swap_cores(direct)
     cot_direct = lax.ppermute(cot_half, "dp", there)
-    cot_across = swap_cores(cot_direct)
     is_fine = patch_size[0] == FINE
     fine_first = is_fine.astype(jnp.int32)
     sizes = jnp.where(
@@ -1154,6 +1148,8 @@
     qkv = (
         jnp.dot(normed_one, w_qkv, preferred_element_type=jnp.float32) + wide(bias_qkv)
     ).astype(jnp.bfloat16)
+    qkv, cot_direct = lax.optimization_barrier((qkv, cot_direct))
+    cot_across = swap_cores(cot_direct)
     mixed = attend(qkv, segment, segment_row, fine, start)
     attended = tensor_sum(jnp.dot(mixed, w_out, preferred_element_type=jnp.float32)) + wide(
         bias_out

time: 498 us -> 481 us (0.966)
  Pallas kernels: 340 us -> 322 us
    pallas_call x1, Pallas kernels: 51.3 us -> 40.4 us  [embed(): pl.pallas_call(embed_kernel, out_shape=[shape((rows, width), jnp.float32)...]
    pallas_call x1, Pallas kernels: 263 us -> 255 us  [back_and_sync(): pl.pallas_call(kernel, out_shape=[jax.ShapeDtypeStruct(s, jnp.float32) fo...]
  transfers between devices with their start and end apart: 8 -> 8, of which waited for: 2 -> 2; matrix products, arithmetic and copies ran while one was open for 11% -> 11% of each run, Pallas kernels for 13% -> 9%
where the time goes in v7:
time: 481 us; the launch traced here: 472 us
  Pallas kernels  322 us (67%)
  matrix products  47.5 us (10%)
  local copies, waits for them, and re-layouts  47.2 us (10%)
  other arithmetic  33.2 us (7%)
  waiting for transfers between devices  10.1 us (2%)
  between operations  6.95 us (1%)
  starting transfers between devices  5.74 us (1%)
    pallas_call x1, Pallas kernels, back_and_sync(): pl.pallas_call(kernel, out_shape=[jax.ShapeDtypeStruct(s, jnp.float32) fo...  255 us
    pallas_call x1, Pallas kernels, embed(): pl.pallas_call(embed_kernel, out_shape=[shape((rows, width), jnp.float32)...  40.4 us
    unnamed x109, local copies, waits for them, and re-layouts  27.2 us
    pallas_call x1, Pallas kernels, attend(): pl.pallas_call(kernel, grid=(heads,), out_shape=jax.ShapeDtypeStruct((row...  13.2 us
    pallas_call x1, Pallas kernels, pixel_back(): pl.pallas_call(pixel_kernel, out_shape=jax.ShapeDtypeStruct(shape, jnp.fl...  13 us
    dot_general x1, matrix products, local(): jnp.einsum('td,fd->tf', grad_branch, w_down, preferred_element_type=jnp.f...  11.5 us
  transfers between devices with their start and end apart: 8, of which 2 were waited for; matrix products, arithmetic and copies ran while one was open for 11% of the time, Pallas kernels for 9%

profile of v7, /device:TPU:0, one launch (start us, length us, event | category | flops | bytes accessed | tf_op | source)
XLA Modules:
  0.0 472.5 jit_solution(7351992878524213511)
XLA Ops:
  3.0 2.9 collective-permute-start
  9.7 3.4 convert_element_type.78
  13.2 2.7 constant_dynamic-slice_fusion.1
  17.5 5.2 %collective-permute-done.1 = s32[2]{0:T(128)S(1)} collective-permute-done((s32[2]{0:T(128)}, s32[2]{0:T(128)S(1)}, u32[]{:S(2)}, u32[]{:S(2)}) %collective-permute-start.1) | collective-permute-done | bytes 40 | tf_op jit(solution)/shard_map/ppermute | solution.py:1094
  30.8 40.4 %embed.1 = (f32[1232,768]{1,0:T(8,128)}, f32[1232,768]{1,0:T(8,128)}, f32[1232,1]{1,0:T(8,128)}, bf16[1232,768]{1,0:T(8,128)(2,1)}, bf16[3,104,3072]{2,1,0:T(8,1...) custom-call(s32[4]{0:T(128)} %get-tuple-element.100.sizes, ...), custom_call_target="tpu_custom_call" | custom-call | tf_op jit(solution)/shard_map/embed/pallas_call | solution.py:201
  71.2 4.2 fusion.7.query.key.value.refs_0_
  75.4 13.2 %attend.1 = bf16[1232,384]{1,0:T(8,128)(2,1)S(1)} custom-call(bf16[1232,1152]{1,0:T(8,128)(2,1)S(1)} %fusion.7.query.key.value.refs_0_, bf16[1232,1152]{1,0:T(8,128)(2,1)S(1)} %fusion.7.query.key.value.refs_0_, bf16[1232,1152]{1,0:T(8,128)(2,1)S(1)} %fusion.7.query.key.value.refs_0_, s32[320,1]{1,0:T(8,128)S(1)} %copy-done.5, s32[1,320]{1,0:T(1,128)S(1)} %copy-done.7), custom_call_target="tpu_custom_call" | custom-call | tf_op jit(solution)/shard_map/attend/pallas_call | solution.py:324
  88.7 3.0 fusion.37
  96.2 4.9 %collective-permute-done.6 = f32[512,768]{1,0:T(8,128)} collective-permute-done((f32[512,768]{1,0:T(8,128)}, f32[512,768]{1,0:T(8,128)}, u32[]{:S(2)}, u32[]{:S(2)}) %collective-permute-start.6) | collective-permute-done | bytes 1572896 | tf_op jit(solution)/shard_map/ppermute | solution.py:1014
  101.0 3.6 broadcast_select_fusion
  106.9 4.8 %fusion.34 = (f32[1232]{0:T(1024)S(1)}, f32[1232,768]{1,0:T(8,128)S(1)}) fusion(f32[1232,768]{1,0:T(8,128)S(1)} %copy-done.19, f32[768]{0:T(1024)S(1)} %convert_element_type.82, f32[1232,768]{1,0:T(8,128)} %fusion.37, f32[1232,768]{1,0:T(8,128)} %collective-permute-done.4), kind=kLoop, calls=%fused_computation.86 | loop fusion | flops 3783472 | bytes 15146816 | tf_op jit(solution)/shard_map/jvp()/reduce_sum | solution.py:17
  114.7 6.5 %multiply_convert_fusion = (bf16[1232,1536]{1,0:T(8,128)(2,1)S(1)}, f32[1232,1536]{1,0:T(8,128)}) fusion(f32[1536]{0:T(1024)S(1)} %convert_element_type.86, bf16[1232,768]{1,0:T(8,128)(2,1)S(1)} %add_convert_fusion.1, bf16[768,1536]{1,0:T(8,128)(2,1)S(1)} %copy-done.40), kind=kOutput, calls=%fused_computation.12 | convolution fusion | flops 2925576192 | bytes 15611904 | tf_op jit(solution)/shard_map/dot_general | solution.py:1160
  121.2 11.5 %convert_reduce_fusion = (f32[1536]{0:T(1024)S(1)}, bf16[1232,1536]{1,0:T(8,128)(2,1)S(1)}) fusion(f32[1232,1536]{1,0:T(8,128)} %get-tuple-element.110, bf16[1536,768]{1,0:T(8,128)(2,1)S(1)} %copy-done.41, f32[1232,768]{1,0:T(8,128)S(1)} %broadcast_dynamic-update-slice_fusion), kind=kOutput, calls=%fused_computation.11 | convolution fusion | flops 2949229056 | bytes 17504256 | tf_op jit(solution)/shard_map/td,fd->tf/dot_general | solution.py:1196
  132.7 5.0 %fusion.39 = f32[1232,768]{1,0:T(8,128)} fusion(bf16[1232,1536]{1,0:T(8,128)(2,1)S(1)} %get-tuple-element.112, bf16[768,1536]{1,0:T(8,128)(2,1)S(1)} %copy-done.40), kind=kOutput, calls=%fused_computation.91 | convolution fusion | flops 2906652672 | bytes 9928704 | tf_op jit(solution)/shard_map/tf,df->td/dot_general | solution.py:1205
  138.1 4.9 %fusion.38 = f32[1232,768]{1,0:T(8,128)} fusion(bf16[1232,1536]{1,0:T(8,128)(2,1)S(1)} %get-tuple-element.109, bf16[1536,768]{1,0:T(8,128)(2,1)S(1)} %copy-done.41), kind=kOutput, calls=%fused_computation.90 | convolution fusion | flops 2906652672 | bytes 9928704 | tf_op jit(solution)/shard_map/dot_general | solution.py:1163
  149.4 5.4 %fusion.14.refs_17_ = f32[384,1536]{1,0:T(8,128)} fusion(bf16[1232,1536]{1,0:T(8,128)(2,1)} %copy-done.44, bf16[1232,768]{1,0:T(8,128)(2,1)S(1)} %add_convert_fusion.1, s32[]{:T(128)S(6)} %select_n.101), kind=kOutput, calls=%fused_computation.37 | convolution fusion | flops 1453326336 | bytes 7090180 | tf_op jit(solution)/shard_map/td,tf->df/dot_general | solution.py:1200
  154.8 3.2 fusion.9.refs_16_
  158.0 4.3 multiply_reduce_fusion
  162.3 4.5 fusion.33
  174.2 255.2 %back_and_sync.1 = (f32[768,3072]{1,0:T(8,128)}, f32[1536,768]{1,0:T(8,128)}, f32[768,1536]{1,0:T(8,128)}, f32[768,384]{1,0:T(8,128)}, f32[768,384]{1,0:T(8,128)...) custom-call(bf16[1232,1152]{1,0:T(8,128)(2,1)} %copy-done.1, ...), custom_call_target="tpu_custom_call" | custom-call | tf_op jit(solution)/shard_map/back_and_sync/pallas_call | solution.py:955
  440.9 13.0 %pixel_back.1 = f32[2,3,240,240]{3,2,1,0:T(8,128)} custom-call(s32[4]{0:T(128)S(1)} %copy-done.8, s32[1]{0:T(128)} %bitcast.9.is_fine, f32[1232,768]{1,0:T(8,128)S(1)} %copy-done.4, bf16[49,48,32]{2,1,0:T(8,128)(2,1)S(1)} %copy-done.3, bf16[768,3072]{1,0:T(8,128)(2,1)S(1)} %copy-done.2, bf16[3,64,768]{2,1,0:T(8,128)(2,1)S(1)} %copy-done.6), custom_call_target="tpu_custom_call" | custom-call | tf_op jit(solution)/shard_map/pixel_back/pallas_call | solution.py:271
  453.9 2.8 fusion.13
  456.8 4.8 %copy.61 = f32[768,3072]{1,0:T(8,128)} copy(f32[768,3072]{1,0:T(8,128)S(1)} %copy-done.14) | data formatting | bytes 18874368
  466.3 2.4 copy.66
  (180 shorter events, 53.7 us)
Async XLA Ops:
  0.7 88.0 %copy-start = (bf16[384,768]{1,0:T(8,128)(2,1)S(1)}, bf16[384,768]{1,0:T(8,128)(2,1)}, u32[]{:S(2)}) copy-start(bf16[384,768]{1,0:T(8,128)(2,1)} %param.39) | copy-start | bytes 1769476
  3.0 19.7 %collective-permute-start = (f32[3,240,256]{2,1,0:T(8,128)}, f32[3,240,256]{2,1,0:T(8,128)S(1)}, u32[]{:S(2)}, u32[]{:S(2)}) collective-permute-start(f32[3,240,256]{2,1,0:T(8,128)} %dynamic-slice_bitcast_fusion), channel_id=1, source_target_pairs={{0,2},{2,0},{4,6},{6,4},{8,10},{10,8},{12,14},{14,12},{16,18},{18,... | collective-permute-start | bytes 2211848 | tf_op jit(solution)/shard_map/ppermute | solution.py:1096
  6.0 16.8 %collective-permute-start.1 = (s32[2]{0:T(128)}, s32[2]{0:T(128)S(1)}, u32[]{:S(2)}, u32[]{:S(2)}) collective-permute-start(s32[2]{0:T(128)} %param.26), channel_id=1, source_target_pairs={{0,2},{2,0},{4,6},{6,4},{8,10},{10,8},{12,14},{14,12},{16,18},{18,... | collective-permute-start | bytes 32 | tf_op jit(solution)/shard_map/ppermute | solution.py:1094
  13.1 12.0 %copy-start.34 = (bf16[768]{0:T(1024)(128)(2,1)S(1)}, bf16[768]{0:T(1024)(128)(2,1)}, u32[]{:S(2)}) copy-start(bf16[768]{0:T(1024)(128)(2,1)} %param.30) | copy-start | bytes 4612
  13.1 12.6 %copy-start.35 = (bf16[768]{0:T(1024)(128)(2,1)S(1)}, bf16[768]{0:T(1024)(128)(2,1)}, u32[]{:S(2)}) copy-start(bf16[768]{0:T(1024)(128)(2,1)} %param.33) | copy-start | bytes 4612
  13.2 13.1 %copy-start.27 = (bf16[768,49]{0,1:T(8,128)(2,1)S(1)}, bf16[768,49]{0,1:T(8,128)(2,1)}, u32[]{:S(2)}) copy-start(bf16[768,49]{0,1:T(8,128)(2,1)} %param.31) | copy-start | bytes 225796
  17.5 53.7 %copy-start.16 = (bf16[768,1152]{1,0:T(8,128)(2,1)}, bf16[768,1152]{1,0:T(8,128)(2,1)S(1)}, u32[]{:S(2)}) copy-start(bf16[768,1152]{1,0:T(8,128)(2,1)S(1)} %pad_maximum_fusion.refs_5_) | copy-start | bytes 5308420
  22.7 52.7 %collective-permute-start.3 = (f32[512,768]{1,0:T(8,128)}, f32[512,768]{1,0:T(8,128)}, u32[]{:S(2)}, u32[]{:S(2)}) collective-permute-start(f32[512,768]{1,0:T(8,128)} %constant_dynamic-slice_fusion.1), channel_id=1, source_target_pairs={{0,2},{2,0},{4,6},{6,4},{8,10},{10,8},{12,14},{14,12},{16,18},{18,... | collective-permute-start | bytes 4718600 | tf_op jit(solution)/shard_map/ppermute | solution.py:1112
  24.5 6.3 %collective-permute-start.2 = (f32[3,240,256]{2,1,0:T(8,128)S(1)}, f32[3,240,256]{2,1,0:T(8,128)}, u32[]{:S(2)}, u32[]{:S(2)}) collective-permute-start(f32[3,240,256]{2,1,0:T(8,128)S(1)} %collective-permute-done.direct), channel_id=1, source_target_pairs={{0,1},{1,0},{2,3},{3,2},{4,5},{5,4},{6,7},{7,6},{8,9},{9,8},{10,11... | collective-permute-start | bytes 2211848 | tf_op jit(solution)/shard_map/ppermute | solution.py:1014
  75.4 13.2 %copy-start.1 = (bf16[1232,1152]{1,0:T(8,128)(2,1)}, bf16[1232,1152]{1,0:T(8,128)(2,1)S(1)}, u32[]{:S(2)}) copy-start(bf16[1232,1152]{1,0:T(8,128)(2,1)S(1)} %fusion.7.query.key.value.refs_0_) | copy-start | bytes 8515588
  88.7 12.3 %copy-start.17 = (bf16[1024,768]{1,0:T(8,128)(2,1)S(1)}, bf16[1024,768]{1,0:T(8,128)(2,1)}, u32[]{:S(2)}) copy-start(bf16[1024,768]{1,0:T(8,128)(2,1)} %param.47) | copy-start | bytes 4718596
  91.7 14.8 %collective-permute-start.4 = (f32[1232,768]{1,0:T(8,128)}, f32[1232,768]{1,0:T(8,128)}, u32[]{:S(2)}, u32[]{:S(2)}) collective-permute-start(f32[1232,768]{1,0:T(8,128)} %fusion.37), channel_id=1, source_target_pairs={{0,1},{1,0},{2,3},{3,2},{4,5},{5,4},{6,7},{7,6},{8,9},{9,8},{10,11... | collective-permute-start | bytes 11354120 | tf_op jit(solution)/shard_map/ppermute | solution.py:1010
  92.2 8.8 %collective-permute-start.6 = (f32[512,768]{1,0:T(8,128)}, f32[512,768]{1,0:T(8,128)}, u32[]{:S(2)}, u32[]{:S(2)}) collective-permute-start(f32[512,768]{1,0:T(8,128)} %collective-permute-done.3), channel_id=1, source_target_pairs={{0,1},{1,0},{2,3},{3,2},{4,5},{5,4},{6,7},{7,6},{8,9},{9,8},{10,11... | collective-permute-start | bytes 4718600 | tf_op jit(solution)/shard_map/ppermute | solution.py:1014
  106.5 14.7 %copy-start.12 = (f32[1232,768]{1,0:T(8,128)}, f32[1232,768]{1,0:T(8,128)S(1)}, u32[]{:S(2)}) copy-start(f32[1232,768]{1,0:T(8,128)S(1)} %broadcast_dynamic-update-slice_fusion) | copy-start | bytes 11354116
  121.2 16.9 %copy-start.42 = (bf16[1232,1536]{1,0:T(8,128)(2,1)}, bf16[1232,1536]{1,0:T(8,128)(2,1)S(1)}, u32[]{:S(2)}) copy-start(bf16[1232,1536]{1,0:T(8,128)(2,1)S(1)} %get-tuple-element.109) | copy-start | bytes 11354116
  137.7 20.3 %collective-permute-start.7 = (f32[1232,768]{1,0:T(8,128)}, f32[1232,768]{1,0:T(8,128)}, u32[]{:S(2)}, u32[]{:S(2)}) collective-permute-start(f32[1232,768]{1,0:T(8,128)} %fusion.39), channel_id=1, source_target_pairs={{0,1},{1,0},{2,3},{3,2},{4,5},{5,4},{6,7},{7,6},{8,9},{9,8},{10,11... | collective-permute-start | bytes 11354120 | tf_op jit(solution)/shard_map/ppermute | solution.py:1010
  143.0 19.3 %collective-permute-start.5 = (f32[1232,768]{1,0:T(8,128)}, f32[1232,768]{1,0:T(8,128)}, u32[]{:S(2)}, u32[]{:S(2)}) collective-permute-start(f32[1232,768]{1,0:T(8,128)} %fusion.38), channel_id=1, source_target_pairs={{0,1},{1,0},{2,3},{3,2},{4,5},{5,4},{6,7},{7,6},{8,9},{9,8},{10,11... | collective-permute-start | bytes 11354120 | tf_op jit(solution)/shard_map/ppermute | solution.py:1010
  174.2 261.2 %copy-start.6 = (bf16[3,64,768]{2,1,0:T(8,128)(2,1)S(1)}, bf16[3,64,768]{2,1,0:T(8,128)(2,1)}, u32[]{:S(2)}) copy-start(bf16[3,64,768]{2,1,0:T(8,128)(2,1)} %get-tuple-element.69.mixed_weight) | copy-start | bytes 884740
  174.2 261.2 %copy-start.8 = (s32[4]{0:T(128)S(1)}, s32[4]{0:T(128)}, u32[]{:S(2)}) copy-start(s32[4]{0:T(128)} %get-tuple-element.100.sizes) | copy-start | bytes 52
  433.2 20.7 %copy-start.25 = (bf16[104,768]{1,0:T(8,128)(2,1)S(1)}, bf16[104,768]{1,0:T(8,128)(2,1)}, u32[]{:S(2)}) copy-start(bf16[104,768]{1,0:T(8,128)(2,1)} %get-tuple-element.103) | copy-start | bytes 479236
  433.2 20.7 %copy-start.26 = (bf16[104,768]{1,0:T(8,128)(2,1)S(1)}, bf16[104,768]{1,0:T(8,128)(2,1)}, u32[]{:S(2)}) copy-start(bf16[104,768]{1,0:T(8,128)(2,1)} %get-tuple-element.104) | copy-start | bytes 479236
  440.9 13.0 %copy-start.18 = (bf16[900,768]{1,0:T(8,128)(2,1)S(1)}, bf16[900,768]{1,0:T(8,128)(2,1)}, u32[]{:S(2)}) copy-start(bf16[900,768]{1,0:T(8,128)(2,1)} %slice.123) | copy-start | bytes 4147204
  440.9 15.8 %copy-start.14 = (f32[768,3072]{1,0:T(8,128)S(1)}, f32[768,3072]{1,0:T(8,128)}, u32[]{:S(2)}) copy-start(f32[768,3072]{1,0:T(8,128)} %get-tuple-element.137) | copy-start | bytes 28311556
  453.9 12.4 %slice-start.2 = ((s8[4718592]{0:T(1024)(128)(4,1)}), s8[524288]{0:T(1024)(128)(4,1)S(1)}, s32[]{:S(2)}) async-start(s8[4718592]{0:T(1024)(128)(4,1)} %bitcast.29), calls=%async_computation.2 | async-start | bytes 1048576
  (34 other events, 181.9 us)

commit v8 on v7

--- a/solution.py
+++ b/solution.py
@@ -64,7 +64,7 @@
     def one(s):
         pair[pl.ds(aligned(s * side, side), side), :] = wide * long[pl.ds(s, 1), :]
 
-    loop(side, one, True)
+    loop(side, one, side % 8 != 0)
 
 
 def cut_patches(line, pix, image, channel, side, grid, res):
@@ -1151,6 +1151,7 @@
     qkv, cot_direct = lax.optimization_barrier((qkv, cot_direct))
     cot_across = swap_cores(cot_direct)
     mixed = attend(qkv, segment, segment_row, fine, start)
+    mixed, cot_across = lax.optimization_barrier((mixed, cot_across))
     attended = tensor_sum(jnp.dot(mixed, w_out, preferred_element_type=jnp.float32)) + wide(
         bias_out
     )

time: 481 us -> 480 us (level)
  waiting for transfers between devices: 10.1 us -> 5.25 us
    ppermute x2, waiting for transfers between devices: 4.85 us -> 0.01 us  [swap_cores(): return lax.ppermute(value, 'tensor', [(0, 1), (1, 0)])]
    unnamed x109 -> x111, local copies, waits for them, and re-layouts: 27.2 us -> 27.2 us
  transfers between devices with their start and end apart: 8 -> 8, of which waited for: 2 -> 1; matrix products, arithmetic and copies ran while one was open for 11% -> 11% of each run, Pallas kernels for 9% -> 12%
where the time goes in v8:
time: 480 us; the launch traced here: 471 us
  Pallas kernels  325 us (68%)
  matrix products  47.5 us (10%)
  local copies, waits for them, and re-layouts  47.3 us (10%)
  other arithmetic  33.2 us (7%)
  between operations  6.95 us (1%)
  starting transfers between devices  5.85 us (1%)
  waiting for transfers between devices  5.25 us (1%)
    pallas_call x1, Pallas kernels, back_and_sync(): pl.pallas_call(kernel, out_shape=[jax.ShapeDtypeStruct(s, jnp.float32) fo...  256 us
    pallas_call x1, Pallas kernels, embed(): pl.pallas_call(embed_kernel, out_shape=[shape((rows, width), jnp.float32)...  41.3 us
    unnamed x111, local copies, waits for them, and re-layouts  27.2 us
    pallas_call x1, Pallas kernels, pixel_back(): pl.pallas_call(pixel_kernel, out_shape=jax.ShapeDtypeStruct(shape, jnp.fl...  14.9 us
    pallas_call x1, Pallas kernels, attend(): pl.pallas_call(kernel, grid=(heads,), out_shape=jax.ShapeDtypeStruct((row...  13.2 us
    dot_general x1, matrix products, local(): jnp.einsum('td,fd->tf', grad_branch, w_down, preferred_element_type=jnp.f...  11.5 us
  transfers between devices with their start and end apart: 8, of which 1 were waited for; matrix products, arithmetic and copies ran while one was open for 11% of the time, Pallas kernels for 12%

profile of v8, /device:TPU:0, one launch (start us, length us, event | category | flops | bytes accessed | tf_op | source)
XLA Modules:
  0.0 471.1 jit_solution(10268411054472268597)
XLA Ops:
  3.0 2.9 collective-permute-start
  9.7 3.4 convert_element_type.78
  13.2 2.7 constant_dynamic-slice_fusion.1
  17.5 5.2 %collective-permute-done.1 = s32[2]{0:T(128)S(1)} collective-permute-done((s32[2]{0:T(128)}, s32[2]{0:T(128)S(1)}, u32[]{:S(2)}, u32[]{:S(2)}) %collective-permute-start.1) | collective-permute-done | bytes 40 | tf_op jit(solution)/shard_map/ppermute | solution.py:1094
  27.1 2.4 copy.45.table
  30.7 41.3 %embed.1 = (f32[1232,768]{1,0:T(8,128)}, f32[1232,768]{1,0:T(8,128)}, f32[1232,1]{1,0:T(8,128)}, bf16[1232,768]{1,0:T(8,128)(2,1)}, bf16[3,104,3072]{2,1,0:T(8,1...) custom-call(s32[4]{0:T(128)} %get-tuple-element.104.sizes, ...), custom_call_target="tpu_custom_call" | custom-call | tf_op jit(solution)/shard_map/embed/pallas_call | solution.py:201
  72.0 4.2 fusion.7.query.key.value.refs_0_
  76.8 13.2 %attend.1 = bf16[1232,384]{1,0:T(8,128)(2,1)S(1)} custom-call(bf16[1232,1152]{1,0:T(8,128)(2,1)S(1)} %fusion.7.query.key.value.refs_0_, bf16[1232,1152]{1,0:T(8,128)(2,1)S(1)} %fusion.7.query.key.value.refs_0_, bf16[1232,1152]{1,0:T(8,128)(2,1)S(1)} %fusion.7.query.key.value.refs_0_, s32[320,1]{1,0:T(8,128)S(1)} %copy-done.5, s32[1,320]{1,0:T(1,128)S(1)} %copy-done.7), custom_call_target="tpu_custom_call" | custom-call | tf_op jit(solution)/shard_map/attend/pallas_call | solution.py:324
  90.0 3.0 fusion.37
  97.0 3.6 broadcast_select_fusion
  103.0 4.8 %fusion.34 = (f32[1232]{0:T(1024)S(1)}, f32[1232,768]{1,0:T(8,128)S(1)}) fusion(f32[1232,768]{1,0:T(8,128)S(1)} %copy-done.19, f32[768]{0:T(1024)S(1)} %convert_element_type.82, f32[1232,768]{1,0:T(8,128)} %fusion.37, f32[1232,768]{1,0:T(8,128)} %collective-permute-done.5), kind=kLoop, calls=%fused_computation.86 | loop fusion | flops 3783472 | bytes 15146816 | tf_op jit(solution)/shard_map/jvp()/reduce_sum | solution.py:17
  110.7 6.5 %multiply_convert_fusion = (bf16[1232,1536]{1,0:T(8,128)(2,1)S(1)}, f32[1232,1536]{1,0:T(8,128)}) fusion(f32[1536]{0:T(1024)S(1)} %convert_element_type.86, bf16[1232,768]{1,0:T(8,128)(2,1)S(1)} %add_convert_fusion.1, bf16[768,1536]{1,0:T(8,128)(2,1)S(1)} %copy-done.41), kind=kOutput, calls=%fused_computation.12 | convolution fusion | flops 2925576192 | bytes 15611904 | tf_op jit(solution)/shard_map/dot_general | solution.py:1161
  117.2 11.5 %convert_reduce_fusion = (f32[1536]{0:T(1024)S(1)}, bf16[1232,1536]{1,0:T(8,128)(2,1)S(1)}) fusion(f32[1232,1536]{1,0:T(8,128)} %get-tuple-element.114, bf16[1536,768]{1,0:T(8,128)(2,1)S(1)} %copy-done.42, f32[1232,768]{1,0:T(8,128)S(1)} %broadcast_dynamic-update-slice_fusion), kind=kOutput, calls=%fused_computation.11 | convolution fusion | flops 2949229056 | bytes 17504256 | tf_op jit(solution)/shard_map/td,fd->tf/dot_general | solution.py:1197
  128.7 5.0 %fusion.39 = f32[1232,768]{1,0:T(8,128)} fusion(bf16[1232,1536]{1,0:T(8,128)(2,1)S(1)} %get-tuple-element.116, bf16[768,1536]{1,0:T(8,128)(2,1)S(1)} %copy-done.41), kind=kOutput, calls=%fused_computation.91 | convolution fusion | flops 2906652672 | bytes 9928704 | tf_op jit(solution)/shard_map/tf,df->td/dot_general | solution.py:1206
  134.2 4.9 %fusion.38 = f32[1232,768]{1,0:T(8,128)} fusion(bf16[1232,1536]{1,0:T(8,128)(2,1)S(1)} %get-tuple-element.113, bf16[1536,768]{1,0:T(8,128)(2,1)S(1)} %copy-done.42), kind=kOutput, calls=%fused_computation.90 | convolution fusion | flops 2906652672 | bytes 9928704 | tf_op jit(solution)/shard_map/dot_general | solution.py:1164
  145.5 5.4 %fusion.14.refs_17_ = f32[384,1536]{1,0:T(8,128)} fusion(bf16[1232,1536]{1,0:T(8,128)(2,1)} %copy-done.45, bf16[1232,768]{1,0:T(8,128)(2,1)S(1)} %add_convert_fusion.1, s32[]{:T(128)S(6)} %select_n.101), kind=kOutput, calls=%fused_computation.37 | convolution fusion | flops 1453326336 | bytes 7090180 | tf_op jit(solution)/shard_map/td,tf->df/dot_general | solution.py:1201
  150.9 3.2 fusion.9.refs_16_
  154.1 4.3 multiply_reduce_fusion
  158.4 4.5 fusion.33
  170.3 255.8 %back_and_sync.1 = (f32[768,3072]{1,0:T(8,128)}, f32[1536,768]{1,0:T(8,128)}, f32[768,1536]{1,0:T(8,128)}, f32[768,384]{1,0:T(8,128)}, f32[768,384]{1,0:T(8,128)...) custom-call(bf16[1232,1152]{1,0:T(8,128)(2,1)} %copy-done.1, ...), custom_call_target="tpu_custom_call" | custom-call | tf_op jit(solution)/shard_map/back_and_sync/pallas_call | solution.py:955
  437.6 14.9 %pixel_back.1 = f32[2,3,240,240]{3,2,1,0:T(8,128)} custom-call(s32[4]{0:T(128)S(1)} %copy-done.8, s32[1]{0:T(128)} %bitcast.9.is_fine, f32[1232,768]{1,0:T(8,128)S(1)} %copy-done.4, bf16[49,48,32]{2,1,0:T(8,128)(2,1)S(1)} %copy-done.3, bf16[768,3072]{1,0:T(8,128)(2,1)S(1)} %copy-done.2, bf16[3,64,768]{2,1,0:T(8,128)(2,1)S(1)} %copy-done.6), custom_call_target="tpu_custom_call" | custom-call | tf_op jit(solution)/shard_map/pixel_back/pallas_call | solution.py:271
  452.5 2.8 fusion.13
  455.4 4.8 %copy.61 = f32[768,3072]{1,0:T(8,128)} copy(f32[768,3072]{1,0:T(8,128)S(1)} %copy-done.14) | data formatting | bytes 18874368
  464.9 2.4 copy.66
  (182 shorter events, 51.4 us)
Async XLA Ops:
  0.7 89.4 %copy-start = (bf16[384,768]{1,0:T(8,128)(2,1)S(1)}, bf16[384,768]{1,0:T(8,128)(2,1)}, u32[]{:S(2)}) copy-start(bf16[384,768]{1,0:T(8,128)(2,1)} %param.39) | copy-start | bytes 1769476
  3.0 19.7 %collective-permute-start = (f32[3,240,256]{2,1,0:T(8,128)}, f32[3,240,256]{2,1,0:T(8,128)S(1)}, u32[]{:S(2)}, u32[]{:S(2)}) collective-permute-start(f32[3,240,256]{2,1,0:T(8,128)} %dynamic-slice_bitcast_fusion), channel_id=1, source_target_pairs={{0,2},{2,0},{4,6},{6,4},{8,10},{10,8},{12,14},{14,12},{16,18},{18,... | collective-permute-start | bytes 2211848 | tf_op jit(solution)/shard_map/ppermute | solution.py:1096
  6.0 16.8 %collective-permute-start.1 = (s32[2]{0:T(128)}, s32[2]{0:T(128)S(1)}, u32[]{:S(2)}, u32[]{:S(2)}) collective-permute-start(s32[2]{0:T(128)} %param.26), channel_id=1, source_target_pairs={{0,2},{2,0},{4,6},{6,4},{8,10},{10,8},{12,14},{14,12},{16,18},{18,... | collective-permute-start | bytes 32 | tf_op jit(solution)/shard_map/ppermute | solution.py:1094
  13.1 11.4 %copy-start.34 = (bf16[768]{0:T(1024)(128)(2,1)S(1)}, bf16[768]{0:T(1024)(128)(2,1)}, u32[]{:S(2)}) copy-start(bf16[768]{0:T(1024)(128)(2,1)} %param.32) | copy-start | bytes 4612
  13.1 12.0 %copy-start.35 = (bf16[768]{0:T(1024)(128)(2,1)S(1)}, bf16[768]{0:T(1024)(128)(2,1)}, u32[]{:S(2)}) copy-start(bf16[768]{0:T(1024)(128)(2,1)} %param.30) | copy-start | bytes 4612
  13.2 12.6 %copy-start.36 = (bf16[768]{0:T(1024)(128)(2,1)S(1)}, bf16[768]{0:T(1024)(128)(2,1)}, u32[]{:S(2)}) copy-start(bf16[768]{0:T(1024)(128)(2,1)} %param.33) | copy-start | bytes 4612
  13.2 13.1 %copy-start.28 = (bf16[768,49]{0,1:T(8,128)(2,1)S(1)}, bf16[768,49]{0,1:T(8,128)(2,1)}, u32[]{:S(2)}) copy-start(bf16[768,49]{0,1:T(8,128)(2,1)} %param.31) | copy-start | bytes 225796
  17.5 54.5 %copy-start.16 = (bf16[768,1152]{1,0:T(8,128)(2,1)}, bf16[768,1152]{1,0:T(8,128)(2,1)S(1)}, u32[]{:S(2)}) copy-start(bf16[768,1152]{1,0:T(8,128)(2,1)S(1)} %pad_maximum_fusion.refs_5_) | copy-start | bytes 5308420
  22.7 53.5 %collective-permute-start.3 = (f32[512,768]{1,0:T(8,128)}, f32[512,768]{1,0:T(8,128)}, u32[]{:S(2)}, u32[]{:S(2)}) collective-permute-start(f32[512,768]{1,0:T(8,128)} %constant_dynamic-slice_fusion.1), channel_id=1, source_target_pairs={{0,2},{2,0},{4,6},{6,4},{8,10},{10,8},{12,14},{14,12},{16,18},{18,... | collective-permute-start | bytes 4718600 | tf_op jit(solution)/shard_map/ppermute | solution.py:1112
  24.5 6.2 %collective-permute-start.2 = (f32[3,240,256]{2,1,0:T(8,128)S(1)}, f32[3,240,256]{2,1,0:T(8,128)}, u32[]{:S(2)}, u32[]{:S(2)}) collective-permute-start(f32[3,240,256]{2,1,0:T(8,128)S(1)} %collective-permute-done.direct), channel_id=1, source_target_pairs={{0,1},{1,0},{2,3},{3,2},{4,5},{5,4},{6,7},{7,6},{8,9},{9,8},{10,11... | collective-permute-start | bytes 2211848 | tf_op jit(solution)/shard_map/ppermute | solution.py:1014
  76.2 13.8 %copy-start.1 = (bf16[1232,1152]{1,0:T(8,128)(2,1)}, bf16[1232,1152]{1,0:T(8,128)(2,1)S(1)}, u32[]{:S(2)}) copy-start(bf16[1232,1152]{1,0:T(8,128)(2,1)S(1)} %fusion.7.query.key.value.refs_0_) | copy-start | bytes 8515588
  76.2 13.8 %collective-permute-start.4 = (f32[512,768]{1,0:T(8,128)}, f32[512,768]{1,0:T(8,128)S(1)}, u32[]{:S(2)}, u32[]{:S(2)}) collective-permute-start(f32[512,768]{1,0:T(8,128)} %collective-permute-done.3), channel_id=1, source_target_pairs={{0,1},{1,0},{2,3},{3,2},{4,5},{5,4},{6,7},{7,6},{8,9},{9,8},{10,11... | collective-permute-start | bytes 4718600 | tf_op jit(solution)/shard_map/ppermute | solution.py:1014
  93.1 9.5 %collective-permute-start.5 = (f32[1232,768]{1,0:T(8,128)}, f32[1232,768]{1,0:T(8,128)}, u32[]{:S(2)}, u32[]{:S(2)}) collective-permute-start(f32[1232,768]{1,0:T(8,128)} %fusion.37), channel_id=1, source_target_pairs={{0,1},{1,0},{2,3},{3,2},{4,5},{5,4},{6,7},{7,6},{8,9},{9,8},{10,11... | collective-permute-start | bytes 11354120 | tf_op jit(solution)/shard_map/ppermute | solution.py:1010
  102.6 14.7 %copy-start.12 = (f32[1232,768]{1,0:T(8,128)}, f32[1232,768]{1,0:T(8,128)S(1)}, u32[]{:S(2)}) copy-start(f32[1232,768]{1,0:T(8,128)S(1)} %broadcast_dynamic-update-slice_fusion) | copy-start | bytes 11354116
  117.2 17.0 %copy-start.43 = (bf16[1232,1536]{1,0:T(8,128)(2,1)}, bf16[1232,1536]{1,0:T(8,128)(2,1)S(1)}, u32[]{:S(2)}) copy-start(bf16[1232,1536]{1,0:T(8,128)(2,1)S(1)} %get-tuple-element.113) | copy-start | bytes 11354116
  133.8 20.3 %collective-permute-start.7 = (f32[1232,768]{1,0:T(8,128)}, f32[1232,768]{1,0:T(8,128)}, u32[]{:S(2)}, u32[]{:S(2)}) collective-permute-start(f32[1232,768]{1,0:T(8,128)} %fusion.39), channel_id=1, source_target_pairs={{0,1},{1,0},{2,3},{3,2},{4,5},{5,4},{6,7},{7,6},{8,9},{9,8},{10,11... | collective-permute-start | bytes 11354120 | tf_op jit(solution)/shard_map/ppermute | solution.py:1010
  139.2 19.2 %collective-permute-start.6 = (f32[1232,768]{1,0:T(8,128)}, f32[1232,768]{1,0:T(8,128)}, u32[]{:S(2)}, u32[]{:S(2)}) collective-permute-start(f32[1232,768]{1,0:T(8,128)} %fusion.38), channel_id=1, source_target_pairs={{0,1},{1,0},{2,3},{3,2},{4,5},{5,4},{6,7},{7,6},{8,9},{9,8},{10,11... | collective-permute-start | bytes 11354120 | tf_op jit(solution)/shard_map/ppermute | solution.py:1010
  170.2 261.9 %copy-start.6 = (bf16[3,64,768]{2,1,0:T(8,128)(2,1)S(1)}, bf16[3,64,768]{2,1,0:T(8,128)(2,1)}, u32[]{:S(2)}) copy-start(bf16[3,64,768]{2,1,0:T(8,128)(2,1)} %get-tuple-element.73.mixed_weight) | copy-start | bytes 884740
  170.2 261.9 %copy-start.8 = (s32[4]{0:T(128)S(1)}, s32[4]{0:T(128)}, u32[]{:S(2)}) copy-start(s32[4]{0:T(128)} %get-tuple-element.104.sizes) | copy-start | bytes 52
  429.9 22.7 %copy-start.26 = (bf16[104,768]{1,0:T(8,128)(2,1)S(1)}, bf16[104,768]{1,0:T(8,128)(2,1)}, u32[]{:S(2)}) copy-start(bf16[104,768]{1,0:T(8,128)(2,1)} %get-tuple-element.107) | copy-start | bytes 479236
  429.9 22.7 %copy-start.27 = (bf16[104,768]{1,0:T(8,128)(2,1)S(1)}, bf16[104,768]{1,0:T(8,128)(2,1)}, u32[]{:S(2)}) copy-start(bf16[104,768]{1,0:T(8,128)(2,1)} %get-tuple-element.108) | copy-start | bytes 479236
  437.6 14.9 %copy-start.18 = (bf16[900,768]{1,0:T(8,128)(2,1)S(1)}, bf16[900,768]{1,0:T(8,128)(2,1)}, u32[]{:S(2)}) copy-start(bf16[900,768]{1,0:T(8,128)(2,1)} %slice.123) | copy-start | bytes 4147204
  437.6 17.8 %copy-start.14 = (f32[768,3072]{1,0:T(8,128)S(1)}, f32[768,3072]{1,0:T(8,128)}, u32[]{:S(2)}) copy-start(f32[768,3072]{1,0:T(8,128)} %get-tuple-element.141) | copy-start | bytes 28311556
  452.5 12.4 %slice-start.2 = ((s8[4718592]{0:T(1024)(128)(4,1)}), s8[524288]{0:T(1024)(128)(4,1)S(1)}, s32[]{:S(2)}) async-start(s8[4718592]{0:T(1024)(128)(4,1)} %bitcast.29), calls=%async_computation.2 | async-start | bytes 1048576
  (35 other events, 175.0 us)
